TPU v7x, 256 devices: a whole 4x4x8 slice. The times are simulated.
256 devices in a mesh: blk: 64 (over x, y_hi, z), con: 4 (over y_lo, core).
Axes of the slice: x: 4, y: 4 (y_hi: 2, y_lo: 2; y = y_hi * 2 + y_lo), z: 8, core: 2. Of those that a mesh axis runs over, the one named last changes fastest.
Arguments:
- patch_rows: bfloat16 [4, 12288, 16, 1024], P('con', 'blk'), may hold values from -6 to 6
- subject_ids: int32 [12288], replicated, may hold values from 0 to 3071
- logit_scale: float32 [2], replicated, may hold values from 5 to 20
- logit_bias: float32 [2], replicated, may hold values from -6 to -2
Outputs:
- grad_emb: float32 [4, 12288, 1024], P('con', 'blk')
All inputs are finite; a program needn't handle non-finite values.
Results may differ from a plain program's by a relative error of at most 0.0037.
Values may be sent and summed in bfloat16 or wider, within the bound.
No kernel may reach another device: no remote copies, remote signals or barrier semaphores. Data moves between devices by JAX's collectives and lax.ppermute only.
A program may use at most 128 MiB of HBM per device.

v0:
```python
import jax
import jax.numpy as jnp
from jax import lax
from jax.sharding import PartitionSpec as P


def from_partner(shard, axis, stride):
    return lax.ppermute(shard, axis, [(i, i ^ 1 << stride) for i in range(lax.axis_size(axis))])


def on_device(patch_rows, subject_ids, logit_scale, logit_bias):
    row_count = patch_rows.shape[1]
    patch_count = patch_rows.shape[2]
    width = patch_rows.shape[3]
    pooled = jnp.sum(patch_rows[0], axis=1, dtype=jnp.float32) / patch_count
    row_norms = jnp.sqrt(jnp.sum(pooled * pooled, axis=1, keepdims=True) + 1e-06)
    own_emb = (pooled / row_norms).astype(jnp.bfloat16)
    contrast = lax.axis_index("con")
    pair_index = contrast // 2
    scale_value = logit_scale[pair_index]
    bias_value = logit_bias[pair_index]
    position = lax.axis_index("blk")
    own_ids = lax.dynamic_slice_in_dim(subject_ids, position * row_count, row_count, 0)
    partner = from_partner(own_emb, "con", 0)
    shard_rows = lax.all_gather(partner, "blk", axis=0, tiled=True)
    logits = (
        scale_value
        * lax.dot_general(
            own_emb, shard_rows, (((1,), (1,)), ((), ())), preferred_element_type=jnp.float32
        )
        + bias_value
    )
    label_sign = jnp.where(own_ids[:, None] == subject_ids[None, :], 1.0, -1.0).astype(jnp.float32)
    coeff = (scale_value * (jax.nn.sigmoid(label_sign * logits) - 1.0) * label_sign).astype(
        jnp.bfloat16
    )
    gradient = jnp.dot(coeff, shard_rows, preferred_element_type=jnp.float32)
    return gradient.reshape(1, row_count, width)


def solution(mesh):
    in_specs = (P("con", "blk", None, None), P(), P(), P())
    out_specs = P("con", "blk", None)
    return jax.shard_map(
        on_device, mesh=mesh, in_specs=in_specs, out_specs=out_specs, check_vma=False
    )
```

profile of v0, /device:TPU:1, one launch (start us, length us, event | category | flops | bytes accessed | tf_op | source)
XLA Modules:
  0.0 312.9 jit_solution(6936567670982369488)
XLA Ops:
  6.5 0.0 copy-start.2
  6.5 0.0 copy-start.3
  6.5 0.0 copy-start.1
  6.5 0.0 all-gather.2.cloned.1.call-start
  6.5 6.1 %convert_reduce_fusion = f32[192,1024]{1,0:T(8,128)S(1)} fusion(bf16[1,192,16,1024]{3,2,1,0:T(8,128)(2,1)} %param.4), kind=kLoop, calls=%fused_computation.11 | loop fusion | flops 6094848 | bytes 7077888 | tf_op jit(solution)/shard_map/reduce_sum | solution.py:15
  12.6 0.2 multiply_reduce_fusion
  12.8 0.1 divide_convert_fusion
  12.9 3.3 %collective-permute-start = (bf16[192,1024]{1,0:T(8,128)(2,1)S(1)}, bf16[192,1024]{1,0:T(8,128)(2,1)S(1)}, u32[]{:S(2)}, u32[]{:S(2)}) collective-permute-start(bf16[192,1024]{1,0:T(8,128)(2,1)S(1)} %divide_convert_fusion), channel_id=1, source_target_pairs={{0,1},{1,0},{2,3},{3,2},{4,5},{5,4},{6,7},{7,6},{8,9},{9,8},{10,11... | collective-permute-start | bytes 1179656 | tf_op jit(solution)/shard_map/ppermute | solution.py:8
  16.2 1.3 collective-permute-done
  17.6 0.0 copy-start
  17.6 0.7 copy-done
  18.3 0.0 all-gather.2.cloned.1.call-update
  18.4 0.0 copy-done.2
  18.4 0.6 dynamic_slice.11
  19.0 0.0 copy-done.3
  19.0 0.6 dynamic_slice.9
  19.6 0.0 copy-done.1
  19.6 0.1 dynamic_slice.10
  19.7 258.4 %all-gather.2.cloned.1.call-done = bf16[12288,1024]{1,0:T(8,128)(2,1)} async-done(((bf16[192,1024]{1,0:T(8,128)(2,1)}), bf16[12288,1024]{1,0:T(8,128)(2,1)}) %all-gather.2.cloned.1.call-update) | async-done | bytes 25165840 | tf_op jit(solution)/shard_map/all_gather | solution.py:25
  278.2 27.9 %fusion.17 = f32[1,192,1024]{2,1,0:T(8,128)} fusion(bf16[12288,1024]{1,0:T(8,128)(2,1)} %all-gather.2.cloned.1.call-done, bf16[192,1024]{1,0:T(8,128)(2,1)S(1)} %divide_convert_fusion, f32[]{:T(128)} %bitcast.1, s32[12288]{0:T(1024)S(1)} %copy-done.1, f32[]{:T(128)} %bitcast, s32[192]{0:T(256)S(1)} %dynamic_slice.10), kind=kOutput, calls=%fused_computation.19 | convolution fusion | flops 9691987968 | bytes 26395400 | tf_op jit(solution)/shard_map/dot_general | solution.py:37
  (1 shorter events, 0.0 us)
Async XLA Ops:
  6.5 11.8 %copy-start.2 = (f32[2]{0:T(128)S(1)}, f32[2]{0:T(128)}, u32[]{:S(2)}) copy-start(f32[2]{0:T(128)} %param.7) | copy-start | bytes 28
  6.5 12.4 %copy-start.3 = (f32[2]{0:T(128)S(1)}, f32[2]{0:T(128)}, u32[]{:S(2)}) copy-start(f32[2]{0:T(128)} %param.6) | copy-start | bytes 28
  6.5 13.1 %copy-start.1 = (s32[12288]{0:T(1024)S(1)}, s32[12288]{0:T(1024)}, u32[]{:S(2)}) copy-start(s32[12288]{0:T(1024)} %param.5) | copy-start | bytes 147460
  6.5 271.6 %all-gather.2.cloned.1.call-start = ((), (), s32[]{:S(2)}) async-start(), calls=%async_computation | async-start | bytes 25559040 | tf_op jit(solution)/shard_map/all_gather | solution.py:25
  12.9 4.6 %collective-permute-start = (bf16[192,1024]{1,0:T(8,128)(2,1)S(1)}, bf16[192,1024]{1,0:T(8,128)(2,1)S(1)}, u32[]{:S(2)}, u32[]{:S(2)}) collective-permute-start(bf16[192,1024]{1,0:T(8,128)(2,1)S(1)} %divide_convert_fusion), channel_id=1, source_target_pairs={{0,1},{1,0},{2,3},{3,2},{4,5},{5,4},{6,7},{7,6},{8,9},{9,8},{10,11... | collective-permute-start | bytes 1179656 | tf_op jit(solution)/shard_map/ppermute | solution.py:8
  17.6 0.7 copy-start
Sparse Core Ops, SparseCore 0:
  18.5 259.6 all-gather.1
where the time goes:
time: 313 us
  waiting for transfers between devices  260 us (83%)
  matrix products  27.9 us (9%)
  between operations  13.4 us (4%)
  other arithmetic  6.38 us (2%)
  starting transfers between devices  3.29 us (1%)
    all_gather x1, waiting for transfers between devices, on_device(): shard_rows = lax.all_gather(partner, 'blk', axis=0, tiled=True)  258 us
    dot_general x1, matrix products, on_device(): gradient = jnp.dot(coeff, shard_rows, preferred_element_type=jnp.float32)  27.9 us
  transfers between devices with their start and end apart: 2, of which 2 were waited for; matrix products, arithmetic and copies ran while one was open for 0% of the time, Pallas kernels for 0%

commit v1 on v0

v1 whole, which is shorter than its diff:
```python
import functools
import jax
import jax.numpy as jnp
from jax import lax
from jax.experimental import pallas as pl
from jax.experimental.pallas import tpu as pltpu
from jax.sharding import PartitionSpec as P

AXES = ("blk", "con")
NX, NYH, NZ, NYL = 4, 2, 8, 2
VMEM_LIMIT = 14 * 1024 * 1024
NT = (((1,), (1,)), ((), ()))


def flat(x, yh, z, yl, c):
    return (((x % NX) * NYH + yh % NYH) * NZ + z % NZ) * 4 + yl * 2 + c


def send(v, ways):
    pairs = []
    for x in range(NX):
        for yh in range(NYH):
            for z in range(NZ):
                for yl in range(NYL):
                    for c, way in enumerate(ways):
                        dx, dy, dz = way(z) if callable(way) else way
                        pairs.append((flat(x, yh, z, yl, c), flat(x + dx, yh + dy, z + dz, yl, c)))
    return lax.ppermute(v, AXES, pairs)


def partner(v):
    return lax.ppermute(v, AXES, [(i, i ^ 1) for i in range(NX * NYH * NZ * 4)])


POOL_STEP = 32


def pool_kernel(x_ref, o_ref, buf, sems):
    n, patches, width = buf.shape
    copies = [
        pltpu.make_async_copy(x_ref.at[pl.ds(i, POOL_STEP)], buf.at[pl.ds(i, POOL_STEP)], sems.at[i // POOL_STEP])
        for i in range(0, n, POOL_STEP)
    ]
    for copy in copies:
        copy.start()
    row = lax.broadcasted_iota(jnp.int32, (POOL_STEP, POOL_STEP * patches), 0) * patches
    col = lax.broadcasted_iota(jnp.int32, (POOL_STEP, POOL_STEP * patches), 1)
    pick = jnp.where((col >= row) & (col < row + patches), 1.0, 0.0).astype(jnp.bfloat16)
    for i, copy in zip(range(0, n, POOL_STEP), copies):
        copy.wait()
        flat_rows = buf[i:i + POOL_STEP].reshape(POOL_STEP * patches, width)
        pooled = jnp.dot(pick, flat_rows, preferred_element_type=jnp.float32) * (1.0 / patches)
        square = jnp.sum(pooled * pooled, axis=1, keepdims=True)
        o_ref[i:i + POOL_STEP, :] = (pooled * (1.0 / jnp.sqrt(square + 1e-06))).astype(o_ref.dtype)


def pool(rows):
    n, _, width = rows.shape
    return pl.pallas_call(
        pool_kernel,
        in_specs=[pl.BlockSpec(memory_space=pltpu.HBM)],
        out_specs=pl.BlockSpec(memory_space=pltpu.VMEM),
        out_shape=jax.ShapeDtypeStruct((n, width), jnp.bfloat16),
        scratch_shapes=[pltpu.VMEM(rows.shape, rows.dtype), pltpu.SemaphoreType.DMA((n // POOL_STEP,))],
        compiler_params=pltpu.CompilerParams(vmem_limit_bytes=60 * 1024 * 1024),
        cost_estimate=pl.CostEstimate(flops=2 * rows.size, bytes_accessed=2 * rows.size, transcendentals=0),
        name="pool",
    )(rows)


def grad_kernel(slots, first_col, groups, has_sum, par_ref, row_ref, col_ref, *refs):
    count = len(slots)
    s_refs, t_refs = refs[:count], refs[count:count + 4 * groups]
    sum_refs, o_refs = (refs[-2 * count:-count], refs[-count:]) if has_sum else (None, refs[-count:])
    pair = lax.axis_index("con") // 2
    scale, bias = par_ref[pl.ds(pair, 1), :], par_ref[pl.ds(pair + 2, 1), :]
    n = s_refs[0].shape[0]
    rows = jnp.concatenate([s[...] for s in s_refs], axis=0)
    row_ids = jnp.concatenate([row_ref[n * k:n * (k + 1), :] for k in slots], axis=0)
    total = jnp.concatenate([v[...] for v in sum_refs], axis=0) if has_sum else None
    for g in range(groups):
        cols = jnp.concatenate([t[...] for t in t_refs[4 * g:4 * g + 4]], axis=0)
        k = cols.shape[0]
        start = first_col * n + g * k
        dots = lax.dot_general(rows, cols, NT, preferred_element_type=jnp.float32)
        same = jnp.concatenate([row_ids] * (k // 128), axis=1) == col_ref[:, start:start + k]
        coeff = scale * jnp.tanh(scale * dots + bias) - jnp.where(same, scale, -scale)
        part = jnp.dot(coeff.astype(jnp.bfloat16), cols, preferred_element_type=jnp.float32)
        total = part if total is None else total + part
    for i, o_ref in enumerate(o_refs):
        o_ref[...] = total[n * i:n * (i + 1)].astype(o_ref.dtype)


def grads(state, slots, first_col, groups, sums, dtype):
    par, row_ids, col_ids, rows, cols = state
    n, width = rows[0].shape
    count = len(slots)
    vmem = pl.BlockSpec(memory_space=pltpu.VMEM)
    operands = [rows[k] for k in slots] + cols[first_col:first_col + 4 * groups] + list(sums or [])
    return pl.pallas_call(
        functools.partial(grad_kernel, slots, first_col, groups, sums is not None),
        in_specs=[vmem] * (3 + len(operands)),
        out_specs=[vmem] * count,
        out_shape=[jax.ShapeDtypeStruct((n, width), dtype)] * count,
        compiler_params=pltpu.CompilerParams(vmem_limit_bytes=VMEM_LIMIT),
        cost_estimate=pl.CostEstimate(flops=16 * groups * count * n * n * width, bytes_accessed=4 * n * width * 2, transcendentals=4 * groups * count * n * n),
    )(par, row_ids, col_ids, *operands)


MOVES = {
    1: ((0, 0, 2), (0, 1, 0)), 2: ((0, 0, -2), (2, 0, 0)), 3: ((0, 0, 1), (1, 0, 0)), 4: ((0, 0, -1), (-1, 0, 0)),
    5: ((0, 0, 1), (1, 0, 0)), 6: ((0, 0, -1), (0, 1, 0)), 7: (lambda z: (0, 0, -2 if z % 2 else 2), (-1, 0, 0)),
}
BACK = {
    k: tuple(((lambda z, way=way: tuple(-d for d in way(z))) if callable(way) else tuple(-d for d in way)) for way in ways)
    for k, ways in MOVES.items()
}
Z_OFF = (0, -2, 2, -1, 1, -3, 3, -4)
X_OFF = (0, 0, 2, -1, 1, -1, 2, 1)
Y_OFF = (0, 1, 0, 0, 0, 1, 1, 1)


def on_device(patch_rows, subject_ids, logit_scale, logit_bias):
    n, _, width = patch_rows.shape[1:]
    f32, bf16 = jnp.float32, jnp.bfloat16
    own = pool(patch_rows[0])

    blk = lax.axis_index("blk")
    first = lax.axis_index("con") % 2 == 0
    x, yh, z = blk // 16, (blk // 8) % 2, blk % 8

    def ids(on_first):
        parts = []
        for zo, xo, yo in zip(Z_OFF, X_OFF, Y_OFF):
            on_z = (x * NYH + yh) * NZ + (z + zo) % NZ
            on_xy = (((x + xo) % NX) * NYH + (yh + yo) % NYH) * NZ + z
            parts.append(lax.dynamic_slice_in_dim(subject_ids, jnp.where(on_first, on_z, on_xy) * n, n, 0))
        return jnp.concatenate(parts)

    par = jnp.broadcast_to(jnp.concatenate([logit_scale, logit_bias])[:, None] * 0.5, (4, 4 * n))
    row_ids = jnp.broadcast_to(ids(first)[:, None], (8 * n, 128))
    col_ids = ids(jnp.logical_not(first))[None, :]

    rows = [own] + [None] * 7
    rows[1] = send(own, MOVES[1])
    rows[2] = send(own, MOVES[2])
    later, par, row_ids, col_ids = lax.optimization_barrier((own, par, row_ids, col_ids))
    rows[3] = send(later, MOVES[3])
    rows[4] = send(later, MOVES[4])
    rows[5] = send(rows[1], MOVES[5])
    turn = jnp.logical_and(first, z % 2 == 1)
    rows[7] = send(jnp.where(turn, rows[2], rows[1]), MOVES[7])
    rows[6] = send(rows[2], MOVES[6])
    cols = [partner(v) for v in rows[:5]]
    state = (par, row_ids, col_ids, rows, cols)
    h0, h3, h4 = grads(state, (0, 3, 4), 0, 1, None, f32)
    h1, h2 = grads(state, (1, 2), 0, 1, None, f32)
    rows[5], rows[6], rows[7], h0, h1, h2, h3, h4 = lax.optimization_barrier((rows[5], rows[6], rows[7], h0, h1, h2, h3, h4))
    cols += [partner(rows[k]) for k in (5, 6, 7)]
    h7, h5 = grads(state, (7, 5), 0, 1, None, f32)
    g7, g5 = grads(state, (7, 5), 4, 1, (h7, h5), bf16)
    rows[6], r7, r5 = lax.optimization_barrier((rows[6], g7, g5))
    r7, r5 = send(r7, BACK[7]), send(r5, BACK[5])
    (g6,) = grads(state, (6,), 0, 2, None, bf16)
    r6 = send(g6, BACK[6])
    g1, g2 = grads(state, (1, 2), 4, 1, (h1, h2), f32)
    g3, g4 = grads(state, (3, 4), 4, 1, (h3, h4), bf16)
    r3 = send(g3, BACK[3])
    r4 = send(g4, BACK[4])
    r7 = r7.astype(f32)
    r1 = send((g1 + jnp.where(turn, 0.0, r7) + r5.astype(f32)).astype(bf16), BACK[1])
    r2 = send((g2 + jnp.where(turn, r7, 0.0) + r6.astype(f32)).astype(bf16), BACK[2])
    (g0,) = grads(state, (0,), 4, 1, (h0,), f32)
    out = g0 + r3.astype(f32) + r4.astype(f32) + r1.astype(f32) + r2.astype(f32)
    return out.reshape(1, n, width)


def solution(mesh):
    in_specs = (P("con", "blk", None, None), P(), P(), P())

    return jax.shard_map(on_device, mesh=mesh, in_specs=in_specs, out_specs=P("con", "blk", None), check_vma=False)
```

time: 313 us -> 78.9 us (0.25)
  waiting for transfers between devices: 260 us -> 6.34 us
  starting transfers between devices: 3.29 us -> 42.3 us
  matrix products: 27.9 us -> 0 us
  Pallas kernels: 0 us -> 24 us
  between operations: 13.4 us -> 0.26 us
  other arithmetic: 6.38 us -> 1.64 us
    all_gather x1 -> x0, waiting for transfers between devices: 258 us -> none  [on_device(): shard_rows = lax.all_gather(partner, 'blk', axis=0, tiled=True)]
    ppermute x1 -> x22, starting transfers between devices: 3.29 us -> 42.3 us  [the longest x14 26.8 us: send(): return lax.ppermute(v, AXES, pairs)]
    dot_general x1 -> x0, matrix products: 27.9 us -> none  [on_device(): gradient = jnp.dot(coeff, shard_rows, preferred_element_type=jnp.float32)]
    pallas_call x0 -> x9, Pallas kernels: none -> 24 us  [the longest x8 19.6 us: grads(): pl.pallas_call(functools.partial(grad_kernel, slots, first_col, groups, s...]
    reduce_sum x2 -> x0, other arithmetic: 6.23 us -> none  [the longest x1 6.07 us: on_device(): pooled = jnp.sum(patch_rows[0], axis=1, dtype=jnp.float32) / patch_count]
    ppermute x1 -> x22, waiting for transfers between devices: 1.35 us -> 6.34 us  [the longest x14 6.31 us: send(): return lax.ppermute(v, AXES, pairs)]
  transfers between devices with their start and end apart: 2 -> 22, of which waited for: 2 -> 3; matrix products, arithmetic and copies ran while one was open for 0% -> 4% of each run, Pallas kernels for 0% -> 23%
where the time goes in v1:
time: 78.9 us; the launch traced here: 77.5 us
  starting transfers between devices  42.3 us (54%)
  Pallas kernels  24 us (30%)
  waiting for transfers between devices  6.34 us (8%)
  local copies, waits for them, and re-layouts  2.96 us (4%)
  other arithmetic  1.64 us (2%)
    ppermute x14, starting transfers between devices, send(): return lax.ppermute(v, AXES, pairs)  26.8 us
    pallas_call x8, Pallas kernels, grads(): pl.pallas_call(functools.partial(grad_kernel, slots, first_col, groups, s...  19.6 us
    ppermute x8, starting transfers between devices, partner(): return lax.ppermute(v, AXES, [(i, i ^ 1) for i in range(NX * NYH * NZ * 4)])  15.5 us
    ppermute x14, waiting for transfers between devices, send(): return lax.ppermute(v, AXES, pairs)  6.31 us
    pallas_call x1, Pallas kernels, pool(): pl.pallas_call(pool_kernel, in_specs=[pl.BlockSpec(memory_space=pltpu.HBM...  4.39 us
  transfers between devices with their start and end apart: 22, of which 3 were waited for; matrix products, arithmetic and copies ran while one was open for 4% of the time, Pallas kernels for 23%

profile of v1, /device:TPU:1, one launch (start us, length us, event | category | flops | bytes accessed | tf_op | source)
XLA Modules:
  0.0 77.5 jit_solution(15591131436321586458)
XLA Ops:
  0.0 4.4 %pool.1.refs_0_ = bf16[192,1024]{1,0:T(8,128)(2,1)} custom-call(bf16[192,16,1024]{2,1,0:T(8,128)(2,1)} %bitcast.3), custom_call_target="tpu_custom_call" | custom-call | flops 6291456 | bytes 6291456 | tf_op jit(solution)/shard_map/pool/pallas_call | solution.py:59
  4.4 3.6 %collective-permute-start.4 = (bf16[192,1024]{1,0:T(8,128)(2,1)}, bf16[192,1024]{1,0:T(8,128)(2,1)S(1)}, u32[]{:S(2)}, u32[]{:S(2)}) collective-permute-start(bf16[192,1024]{1,0:T(8,128)(2,1)} %pool.1.refs_0_), channel_id=1, source_target_pairs={{0,24},{1,129},{2,26},{3,131},{4,28},{5,133},{6,30},{7,135},{8,0},... | collective-permute-start | bytes 1179656 | tf_op jit(solution)/shard_map/ppermute | solution.py:28
  8.1 2.9 %collective-permute-start.2 = (bf16[192,1024]{1,0:T(8,128)(2,1)}, bf16[192,1024]{1,0:T(8,128)(2,1)S(1)}, u32[]{:S(2)}, u32[]{:S(2)}) collective-permute-start(bf16[192,1024]{1,0:T(8,128)(2,1)} %pool.1.refs_0_), channel_id=1, source_target_pairs={{0,8},{1,33},{2,10},{3,35},{4,12},{5,37},{6,14},{7,39},{8,16},{9,4... | collective-permute-start | bytes 1179656 | tf_op jit(solution)/shard_map/ppermute | solution.py:28
  11.0 1.2 %fusion.6 = (s32[192]{0:T(256)S(1)}, s32[192]{0:T(256)S(1)}, s32[192]{0:T(256)S(1)}, s32[192]{0:T(256)S(1)}, s32[192]{0:T(256)S(1)}, /*index=5*/s32[192]{0:T(256...) fusion(s32[12288]{0:T(1024)} %param.5, ...), kind=kLoop, calls=%fused_computation.11 | loop fusion | bytes 24640 | tf_op jit(solution)/shard_map/dynamic_slice | solution.py:137
  12.2 0.6 broadcast_in_dim.23.col_ref
  13.7 2.1 %collective-permute-start.8 = (bf16[192,1024]{1,0:T(8,128)(2,1)}, bf16[192,1024]{1,0:T(8,128)(2,1)S(1)}, u32[]{:S(2)}, u32[]{:S(2)}) collective-permute-start(bf16[192,1024]{1,0:T(8,128)(2,1)} %pool.1.refs_0_), channel_id=1, source_target_pairs={{0,1},{1,0},{2,3},{3,2},{4,5},{5,4},{6,7},{7,6},{8,9},{9,8},{10,11... | collective-permute-start | bytes 1179656 | tf_op jit(solution)/shard_map/ppermute | solution.py:32
  15.8 2.5 %collective-permute-start = (bf16[192,1024]{1,0:T(8,128)(2,1)}, bf16[192,1024]{1,0:T(8,128)(2,1)S(1)}, u32[]{:S(2)}, u32[]{:S(2)}) collective-permute-start(bf16[192,1024]{1,0:T(8,128)(2,1)} %pool.1.refs_0_), channel_id=1, source_target_pairs={{0,28},{1,193},{2,30},{3,195},{4,0},{5,197},{6,2},{7,199},{8,4},{9... | collective-permute-start | bytes 1179656 | tf_op jit(solution)/shard_map/ppermute | solution.py:28
  18.2 2.6 %collective-permute-start.10 = (bf16[192,1024]{1,0:T(8,128)(2,1)S(1)}, bf16[192,1024]{1,0:T(8,128)(2,1)S(1)}, u32[]{:S(2)}, u32[]{:S(2)}) collective-permute-start(bf16[192,1024]{1,0:T(8,128)(2,1)S(1)} %collective-permute-done.4.refs_1_), channel_id=1, source_target_pairs={{0,1},{1,0},{2,3},{3,2},{4,5},{5,4},{6,7},{7,6},{8,9},{9,8},{10,11... | collective-permute-start | bytes 1179656 | tf_op jit(solution)/shard_map/ppermute | solution.py:32
  20.8 5.4 %collective-permute-start.9 = (bf16[192,1024]{1,0:T(8,128)(2,1)S(1)}, bf16[192,1024]{1,0:T(8,128)(2,1)}, u32[]{:S(2)}, u32[]{:S(2)}) collective-permute-start(bf16[192,1024]{1,0:T(8,128)(2,1)S(1)} %collective-permute-done.2.refs_0_), channel_id=1, source_target_pairs={{0,1},{1,0},{2,3},{3,2},{4,5},{5,4},{6,7},{7,6},{8,9},{9,8},{10,11... | collective-permute-start | bytes 1179656 | tf_op jit(solution)/shard_map/ppermute | solution.py:32
  26.2 4.2 %collective-permute-start.11 = (bf16[192,1024]{1,0:T(8,128)(2,1)S(1)}, bf16[192,1024]{1,0:T(8,128)(2,1)}, u32[]{:S(2)}, u32[]{:S(2)}) collective-permute-start(bf16[192,1024]{1,0:T(8,128)(2,1)S(1)} %collective-permute-done.7.refs_1_.refs_0_), channel_id=1, source_target_pairs={{0,1},{1,0},{2,3},{3,2},{4,5},{5,4},{6,7},{7,6},{8,9},{9,8},{10,11... | collective-permute-start | bytes 1179656 | tf_op jit(solution)/shard_map/ppermute | solution.py:32
  30.4 2.6 %collective-permute-start.6 = (bf16[192,1024]{1,0:T(8,128)(2,1)S(1)}, bf16[192,1024]{1,0:T(8,128)(2,1)S(1)}, u32[]{:S(2)}, u32[]{:S(2)}) collective-permute-start(bf16[192,1024]{1,0:T(8,128)(2,1)S(1)} %broadcast_select_fusion), channel_id=1, source_target_pairs={{0,8},{1,193},{2,10},{3,195},{4,28},{5,197},{6,30},{7,199},{8,16},... | collective-permute-start | bytes 1179656 | tf_op jit(solution)/shard_map/ppermute | solution.py:28
  33.0 2.9 %collective-permute-start.5 = (bf16[192,1024]{1,0:T(8,128)(2,1)S(1)}, bf16[192,1024]{1,0:T(8,128)(2,1)S(1)}, u32[]{:S(2)}, u32[]{:S(2)}) collective-permute-start(bf16[192,1024]{1,0:T(8,128)(2,1)S(1)} %collective-permute-done.4.refs_1_), channel_id=1, source_target_pairs={{0,28},{1,33},{2,30},{3,35},{4,0},{5,37},{6,2},{7,39},{8,4},{9,41}... | collective-permute-start | bytes 1179656 | tf_op jit(solution)/shard_map/ppermute | solution.py:28
  36.2 0.7 copy-done.1
  36.9 3.0 %shard_map.47 = (f32[192,1024]{1,0:T(8,128)S(1)}, f32[192,1024]{1,0:T(8,128)S(1)}) custom-call(f32[4,768]{1,0:T(4,128)S(1)} %broadcast_in_dim.11.par_ref, s32[1536,128]{1,0:T(8,128)S(1)} %broadcast_in_dim.22.row_ref, s32[1,1536]{1,0:T(1,128)S(1)} %copy-done.1, bf16[192,1024]{1,0:T(8,128)(2,1)S(1)} %collective-permute-done.2.refs_0_, ...), custom_call_target="tpu_custom_call" | custom-call | flops 1207959552 | bytes 1572864 | tf_op jit(solution)/shard_map/pallas_call | solution.py:100
  39.9 3.8 %shard_map.46 = (f32[192,1024]{1,0:T(8,128)S(1)}, f32[192,1024]{1,0:T(8,128)S(1)}, f32[192,1024]{1,0:T(8,128)S(1)}) custom-call(f32[4,768]{1,0:T(4,128)S(1)} %broadcast_in_dim.11.par_ref, s32[1536,128]{1,0:T(8,128)S(1)} %broadcast_in_dim.22.row_ref, s32[1,1536]{1,0:T(1,128)S(1)} %copy-done.1, bf16[192,1024]{1,0:T(8,128)(2,1)S(1)} %copy-done, ...), custom_call_target="tpu_custom_call" | custom-call | flops 1811939328 | bytes 1572864 | tf_op jit(solution)/shard_map/pallas_call | solution.py:100
  44.0 0.6 collective-permute-start.13
  44.6 0.5 collective-permute-start.14
  45.1 3.0 %shard_map.51 = (f32[192,1024]{1,0:T(8,128)S(1)}, f32[192,1024]{1,0:T(8,128)S(1)}) custom-call(f32[4,768]{1,0:T(4,128)S(1)} %broadcast_in_dim.11.par_ref, s32[1536,128]{1,0:T(8,128)S(1)} %broadcast_in_dim.22.row_ref, s32[1,1536]{1,0:T(1,128)S(1)} %copy-done.1, bf16[192,1024]{1,0:T(8,128)(2,1)S(1)} %collective-permute-done.6.refs_0_, ...), custom_call_target="tpu_custom_call" | custom-call | flops 1207959552 | bytes 1572864 | tf_op jit(solution)/shard_map/pallas_call | solution.py:100
  48.2 1.9 %shard_map.52 = (bf16[192,1024]{1,0:T(8,128)(2,1)S(1)}, bf16[192,1024]{1,0:T(8,128)(2,1)S(1)}) custom-call(f32[4,768]{1,0:T(4,128)S(1)} %broadcast_in_dim.11.par_ref, s32[1536,128]{1,0:T(8,128)S(1)} %broadcast_in_dim.22.row_ref, s32[1,1536]{1,0:T(1,128)S(1)} %copy-done.2, bf16[192,1024]{1,0:T(8,128)(2,1)S(1)} %collective-permute-done.6.refs_0_, ...), custom_call_target="tpu_custom_call" | custom-call | flops 1207959552 | bytes 1572864 | tf_op jit(solution)/shard_map/pallas_call | solution.py:100
  50.0 1.3 %collective-permute-start.17 = (bf16[192,1024]{1,0:T(8,128)(2,1)S(1)}, bf16[192,1024]{1,0:T(8,128)(2,1)S(1)}, u32[]{:S(2)}, u32[]{:S(2)}) collective-permute-start(bf16[192,1024]{1,0:T(8,128)(2,1)S(1)} %get-tuple-element.57), channel_id=1, source_target_pairs={{0,24},{1,65},{2,26},{3,67},{4,12},{5,69},{6,14},{7,71},{8,0},{9,7... | collective-permute-start | bytes 1179656 | tf_op jit(solution)/shard_map/ppermute | solution.py:28
  51.3 1.5 %collective-permute-start.18 = (bf16[192,1024]{1,0:T(8,128)(2,1)S(1)}, bf16[192,1024]{1,0:T(8,128)(2,1)S(1)}, u32[]{:S(2)}, u32[]{:S(2)}) collective-permute-start(bf16[192,1024]{1,0:T(8,128)(2,1)S(1)} %get-tuple-element.58), channel_id=1, source_target_pairs={{0,28},{1,193},{2,30},{3,195},{4,0},{5,197},{6,2},{7,199},{8,4},{9... | collective-permute-start | bytes 1179656 | tf_op jit(solution)/shard_map/ppermute | solution.py:28
  52.8 3.0 %shard_map.53 = bf16[192,1024]{1,0:T(8,128)(2,1)S(1)} custom-call(f32[4,768]{1,0:T(4,128)S(1)} %broadcast_in_dim.11.par_ref, s32[1536,128]{1,0:T(8,128)S(1)} %broadcast_in_dim.22.row_ref, s32[1,1536]{1,0:T(1,128)S(1)} %copy-done.2, bf16[192,1024]{1,0:T(8,128)(2,1)S(1)} %collective-permute-done.5.refs_0_, ...), custom_call_target="tpu_custom_call" | custom-call | flops 1207959552 | bytes 1572864 | tf_op jit(solution)/shard_map/pallas_call | solution.py:100
  55.8 3.2 %collective-permute-start.20 = (bf16[192,1024]{1,0:T(8,128)(2,1)S(1)}, bf16[192,1024]{1,0:T(8,128)(2,1)S(1)}, u32[]{:S(2)}, u32[]{:S(2)}) collective-permute-start(bf16[192,1024]{1,0:T(8,128)(2,1)S(1)} %shard_map.53), channel_id=1, source_target_pairs={{0,4},{1,33},{2,6},{3,35},{4,8},{5,37},{6,10},{7,39},{8,12},{9,41}... | collective-permute-start | bytes 1179656 | tf_op jit(solution)/shard_map/ppermute | solution.py:28
  59.0 1.9 %shard_map.49 = (bf16[192,1024]{1,0:T(8,128)(2,1)S(1)}, bf16[192,1024]{1,0:T(8,128)(2,1)S(1)}) custom-call(f32[4,768]{1,0:T(4,128)S(1)} %broadcast_in_dim.11.par_ref, s32[1536,128]{1,0:T(8,128)S(1)} %broadcast_in_dim.22.row_ref, s32[1,1536]{1,0:T(1,128)S(1)} %copy-done.2, bf16[192,1024]{1,0:T(8,128)(2,1)S(1)} %collective-permute-done.7.refs_1_.refs_0_, ...), custom_call_target="tpu_custom_call" | custom-call | flops 1207959552 | bytes 1572864 | tf_op jit(solution)/shard_map/pallas_call | solution.py:100
  60.9 1.3 %collective-permute-start.15 = (bf16[192,1024]{1,0:T(8,128)(2,1)S(1)}, bf16[192,1024]{1,0:T(8,128)(2,1)S(1)}, u32[]{:S(2)}, u32[]{:S(2)}) collective-permute-start(bf16[192,1024]{1,0:T(8,128)(2,1)S(1)} %get-tuple-element.48), channel_id=1, source_target_pairs={{0,28},{1,193},{2,30},{3,195},{4,0},{5,197},{6,2},{7,199},{8,4},{9... | collective-permute-start | bytes 1179656 | tf_op jit(solution)/shard_map/ppermute | solution.py:28
  62.4 1.9 %shard_map.50 = (f32[192,1024]{1,0:T(8,128)S(1)}, f32[192,1024]{1,0:T(8,128)S(1)}) custom-call(f32[4,768]{1,0:T(4,128)S(1)} %broadcast_in_dim.11.par_ref, s32[1536,128]{1,0:T(8,128)S(1)} %broadcast_in_dim.22.row_ref, s32[1,1536]{1,0:T(1,128)S(1)} %copy-done.2, bf16[192,1024]{1,0:T(8,128)(2,1)S(1)} %collective-permute-done.2.refs_0_, ...), custom_call_target="tpu_custom_call" | custom-call | flops 1207959552 | bytes 1572864 | tf_op jit(solution)/shard_map/pallas_call | solution.py:100
  64.7 3.1 %collective-permute-start.19 = (bf16[192,1024]{1,0:T(8,128)(2,1)S(1)}, bf16[192,1024]{1,0:T(8,128)(2,1)S(1)}, u32[]{:S(2)}, u32[]{:S(2)}) collective-permute-start(bf16[192,1024]{1,0:T(8,128)(2,1)S(1)} %get-tuple-element.61), channel_id=1, source_target_pairs={{0,24},{1,33},{2,26},{3,35},{4,28},{5,37},{6,30},{7,39},{8,0},{9,4... | collective-permute-start | bytes 1179656 | tf_op jit(solution)/shard_map/ppermute | solution.py:28
  67.9 1.2 %collective-permute-start.21 = (bf16[192,1024]{1,0:T(8,128)(2,1)S(1)}, bf16[192,1024]{1,0:T(8,128)(2,1)S(1)}, u32[]{:S(2)}, u32[]{:S(2)}) collective-permute-start(bf16[192,1024]{1,0:T(8,128)(2,1)S(1)} %get-tuple-element.62), channel_id=1, source_target_pairs={{0,8},{1,129},{2,10},{3,131},{4,12},{5,133},{6,14},{7,135},{8,16},... | collective-permute-start | bytes 1179656 | tf_op jit(solution)/shard_map/ppermute | solution.py:28
  69.1 1.2 %shard_map.48 = f32[192,1024]{1,0:T(8,128)S(1)} custom-call(f32[4,768]{1,0:T(4,128)S(1)} %broadcast_in_dim.11.par_ref, s32[1536,128]{1,0:T(8,128)S(1)} %broadcast_in_dim.22.row_ref, s32[1,1536]{1,0:T(1,128)S(1)} %copy-done.2, bf16[192,1024]{1,0:T(8,128)(2,1)S(1)} %copy-done, bf16[192,1024]{1,0:T(8,128)(2,1)S(1)} %collective-permute-done.1.refs_1_.refs_2_.refs_5_, ...), custom_call_target="tpu_custom_call" | custom-call | flops 603979776 | bytes 1572864 | tf_op jit(solution)/shard_map/pallas_call | solution.py:100
  70.3 3.0 %collective-permute-done.19 = bf16[192,1024]{1,0:T(8,128)(2,1)S(1)} collective-permute-done((bf16[192,1024]{1,0:T(8,128)(2,1)S(1)}, bf16[192,1024]{1,0:T(8,128)(2,1)S(1)}, u32[]{:S(2)}, u32[]{:S(2)}) %collective-permute-start.19) | collective-permute-done | bytes 393248 | tf_op jit(solution)/shard_map/ppermute | solution.py:28
  73.3 3.0 %collective-permute-done.21 = bf16[192,1024]{1,0:T(8,128)(2,1)S(1)} collective-permute-done((bf16[192,1024]{1,0:T(8,128)(2,1)S(1)}, bf16[192,1024]{1,0:T(8,128)(2,1)S(1)}, u32[]{:S(2)}, u32[]{:S(2)}) %collective-permute-start.21) | collective-permute-done | bytes 393248 | tf_op jit(solution)/shard_map/ppermute | solution.py:28
  76.3 1.2 %add_bitcast_fusion = f32[1,192,1024]{2,1,0:T(8,128)} fusion(bf16[192,1024]{1,0:T(8,128)(2,1)S(1)} %collective-permute-done.21, bf16[192,1024]{1,0:T(8,128)(2,1)S(1)} %collective-permute-done.19, bf16[192,1024]{1,0:T(8,128)(2,1)S(1)} %collective-permute-done.16, f32[192,1024]{1,0:T(8,128)S(1)} %shard_map.48, bf16[192,1024]{1,0:T(8,128)(2,1)S(1)} %collective-permute-done.15), kind=kLoop, calls=%fused_computation.8 | loop fusion | flops 1572864 | bytes 3145728 | tf_op jit(solution)/shard_map/reshape | solution.py:175
  (41 shorter events, 2.2 us)
Async XLA Ops:
  0.0 12.9 %copy-start.3 = (f32[2]{0:T(128)S(1)}, f32[2]{0:T(128)}, u32[]{:S(2)}) copy-start(f32[2]{0:T(128)} %param.7) | copy-start | bytes 28
  0.0 12.9 %copy-start.4 = (f32[2]{0:T(128)S(1)}, f32[2]{0:T(128)}, u32[]{:S(2)}) copy-start(f32[2]{0:T(128)} %param.6) | copy-start | bytes 28
  4.4 35.5 %copy-start = (bf16[192,1024]{1,0:T(8,128)(2,1)S(1)}, bf16[192,1024]{1,0:T(8,128)(2,1)}, u32[]{:S(2)}) copy-start(bf16[192,1024]{1,0:T(8,128)(2,1)} %pool.1.refs_0_) | copy-start | bytes 1179652
  4.4 13.8 %collective-permute-start.4 = (bf16[192,1024]{1,0:T(8,128)(2,1)}, bf16[192,1024]{1,0:T(8,128)(2,1)S(1)}, u32[]{:S(2)}, u32[]{:S(2)}) collective-permute-start(bf16[192,1024]{1,0:T(8,128)(2,1)} %pool.1.refs_0_), channel_id=1, source_target_pairs={{0,24},{1,129},{2,26},{3,131},{4,28},{5,133},{6,30},{7,135},{8,0},... | collective-permute-start | bytes 1179656 | tf_op jit(solution)/shard_map/ppermute | solution.py:28
  8.1 12.8 %collective-permute-start.2 = (bf16[192,1024]{1,0:T(8,128)(2,1)}, bf16[192,1024]{1,0:T(8,128)(2,1)S(1)}, u32[]{:S(2)}, u32[]{:S(2)}) collective-permute-start(bf16[192,1024]{1,0:T(8,128)(2,1)} %pool.1.refs_0_), channel_id=1, source_target_pairs={{0,8},{1,33},{2,10},{3,35},{4,12},{5,37},{6,14},{7,39},{8,16},{9,4... | collective-permute-start | bytes 1179656 | tf_op jit(solution)/shard_map/ppermute | solution.py:28
  13.3 12.9 %collective-permute-start.7 = (bf16[192,1024]{1,0:T(8,128)(2,1)}, bf16[192,1024]{1,0:T(8,128)(2,1)S(1)}, u32[]{:S(2)}, u32[]{:S(2)}) collective-permute-start(bf16[192,1024]{1,0:T(8,128)(2,1)} %pool.1.refs_0_), channel_id=1, source_target_pairs={{0,4},{1,65},{2,6},{3,67},{4,8},{5,69},{6,10},{7,71},{8,12},{9,73}... | collective-permute-start | bytes 1179656 | tf_op jit(solution)/shard_map/ppermute | solution.py:28
  13.7 16.7 %collective-permute-start.8 = (bf16[192,1024]{1,0:T(8,128)(2,1)}, bf16[192,1024]{1,0:T(8,128)(2,1)S(1)}, u32[]{:S(2)}, u32[]{:S(2)}) collective-permute-start(bf16[192,1024]{1,0:T(8,128)(2,1)} %pool.1.refs_0_), channel_id=1, source_target_pairs={{0,1},{1,0},{2,3},{3,2},{4,5},{5,4},{6,7},{7,6},{8,9},{9,8},{10,11... | collective-permute-start | bytes 1179656 | tf_op jit(solution)/shard_map/ppermute | solution.py:32
  15.8 17.2 %collective-permute-start = (bf16[192,1024]{1,0:T(8,128)(2,1)}, bf16[192,1024]{1,0:T(8,128)(2,1)S(1)}, u32[]{:S(2)}, u32[]{:S(2)}) collective-permute-start(bf16[192,1024]{1,0:T(8,128)(2,1)} %pool.1.refs_0_), channel_id=1, source_target_pairs={{0,28},{1,193},{2,30},{3,195},{4,0},{5,197},{6,2},{7,199},{8,4},{9... | collective-permute-start | bytes 1179656 | tf_op jit(solution)/shard_map/ppermute | solution.py:28
  18.2 17.7 %collective-permute-start.10 = (bf16[192,1024]{1,0:T(8,128)(2,1)S(1)}, bf16[192,1024]{1,0:T(8,128)(2,1)S(1)}, u32[]{:S(2)}, u32[]{:S(2)}) collective-permute-start(bf16[192,1024]{1,0:T(8,128)(2,1)S(1)} %collective-permute-done.4.refs_1_), channel_id=1, source_target_pairs={{0,1},{1,0},{2,3},{3,2},{4,5},{5,4},{6,7},{7,6},{8,9},{9,8},{10,11... | collective-permute-start | bytes 1179656 | tf_op jit(solution)/shard_map/ppermute | solution.py:32
  20.8 15.1 %collective-permute-start.9 = (bf16[192,1024]{1,0:T(8,128)(2,1)S(1)}, bf16[192,1024]{1,0:T(8,128)(2,1)}, u32[]{:S(2)}, u32[]{:S(2)}) collective-permute-start(bf16[192,1024]{1,0:T(8,128)(2,1)S(1)} %collective-permute-done.2.refs_0_), channel_id=1, source_target_pairs={{0,1},{1,0},{2,3},{3,2},{4,5},{5,4},{6,7},{7,6},{8,9},{9,8},{10,11... | collective-permute-start | bytes 1179656 | tf_op jit(solution)/shard_map/ppermute | solution.py:32
  26.2 10.0 %collective-permute-start.11 = (bf16[192,1024]{1,0:T(8,128)(2,1)S(1)}, bf16[192,1024]{1,0:T(8,128)(2,1)}, u32[]{:S(2)}, u32[]{:S(2)}) collective-permute-start(bf16[192,1024]{1,0:T(8,128)(2,1)S(1)} %collective-permute-done.7.refs_1_.refs_0_), channel_id=1, source_target_pairs={{0,1},{1,0},{2,3},{3,2},{4,5},{5,4},{6,7},{7,6},{8,9},{9,8},{10,11... | collective-permute-start | bytes 1179656 | tf_op jit(solution)/shard_map/ppermute | solution.py:32
  30.4 13.2 %collective-permute-start.6 = (bf16[192,1024]{1,0:T(8,128)(2,1)S(1)}, bf16[192,1024]{1,0:T(8,128)(2,1)S(1)}, u32[]{:S(2)}, u32[]{:S(2)}) collective-permute-start(bf16[192,1024]{1,0:T(8,128)(2,1)S(1)} %broadcast_select_fusion), channel_id=1, source_target_pairs={{0,8},{1,193},{2,10},{3,195},{4,28},{5,197},{6,30},{7,199},{8,16},... | collective-permute-start | bytes 1179656 | tf_op jit(solution)/shard_map/ppermute | solution.py:28
  33.0 10.7 %collective-permute-start.5 = (bf16[192,1024]{1,0:T(8,128)(2,1)S(1)}, bf16[192,1024]{1,0:T(8,128)(2,1)S(1)}, u32[]{:S(2)}, u32[]{:S(2)}) collective-permute-start(bf16[192,1024]{1,0:T(8,128)(2,1)S(1)} %collective-permute-done.4.refs_1_), channel_id=1, source_target_pairs={{0,28},{1,33},{2,30},{3,35},{4,0},{5,37},{6,2},{7,39},{8,4},{9,41}... | collective-permute-start | bytes 1179656 | tf_op jit(solution)/shard_map/ppermute | solution.py:28
  35.9 8.1 %collective-permute-start.3 = (bf16[192,1024]{1,0:T(8,128)(2,1)S(1)}, bf16[192,1024]{1,0:T(8,128)(2,1)S(1)}, u32[]{:S(2)}, u32[]{:S(2)}) collective-permute-start(bf16[192,1024]{1,0:T(8,128)(2,1)S(1)} %collective-permute-done.2.refs_0_), channel_id=1, source_target_pairs={{0,4},{1,65},{2,6},{3,67},{4,8},{5,69},{6,10},{7,71},{8,12},{9,73}... | collective-permute-start | bytes 1179656 | tf_op jit(solution)/shard_map/ppermute | solution.py:28
  35.9 12.2 %collective-permute-start.1 = (bf16[192,1024]{1,0:T(8,128)(2,1)S(1)}, bf16[192,1024]{1,0:T(8,128)(2,1)S(1)}, u32[]{:S(2)}, u32[]{:S(2)}) collective-permute-start(bf16[192,1024]{1,0:T(8,128)(2,1)S(1)} %collective-permute-done.refs_2_.refs_1_), channel_id=1, source_target_pairs={{0,1},{1,0},{2,3},{3,2},{4,5},{5,4},{6,7},{7,6},{8,9},{9,8},{10,11... | collective-permute-start | bytes 1179656 | tf_op jit(solution)/shard_map/ppermute | solution.py:32
  36.2 0.7 copy-start.1
  39.9 8.3 %copy-start.2 = (s32[1,1536]{1,0:T(1,128)S(1)}, s32[1,1536]{1,0:T(1,128)}, u32[]{:S(2)}) copy-start(s32[1,1536]{1,0:T(1,128)} %broadcast_in_dim.23.col_ref) | copy-start | bytes 18436
  44.0 4.1 %collective-permute-start.13 = (bf16[192,1024]{1,0:T(8,128)(2,1)S(1)}, bf16[192,1024]{1,0:T(8,128)(2,1)S(1)}, u32[]{:S(2)}, u32[]{:S(2)}) collective-permute-start(bf16[192,1024]{1,0:T(8,128)(2,1)S(1)} %collective-permute-done.5.refs_0_), channel_id=1, source_target_pairs={{0,1},{1,0},{2,3},{3,2},{4,5},{5,4},{6,7},{7,6},{8,9},{9,8},{10,11... | collective-permute-start | bytes 1179656 | tf_op jit(solution)/shard_map/ppermute | solution.py:32
  44.6 3.5 %collective-permute-start.12 = (bf16[192,1024]{1,0:T(8,128)(2,1)S(1)}, bf16[192,1024]{1,0:T(8,128)(2,1)S(1)}, u32[]{:S(2)}, u32[]{:S(2)}) collective-permute-start(bf16[192,1024]{1,0:T(8,128)(2,1)S(1)} %collective-permute-done.3.refs_1_), channel_id=1, source_target_pairs={{0,1},{1,0},{2,3},{3,2},{4,5},{5,4},{6,7},{7,6},{8,9},{9,8},{10,11... | collective-permute-start | bytes 1179656 | tf_op jit(solution)/shard_map/ppermute | solution.py:32
  44.6 3.5 %collective-permute-start.14 = (bf16[192,1024]{1,0:T(8,128)(2,1)S(1)}, bf16[192,1024]{1,0:T(8,128)(2,1)S(1)}, u32[]{:S(2)}, u32[]{:S(2)}) collective-permute-start(bf16[192,1024]{1,0:T(8,128)(2,1)S(1)} %collective-permute-done.6.refs_0_), channel_id=1, source_target_pairs={{0,1},{1,0},{2,3},{3,2},{4,5},{5,4},{6,7},{7,6},{8,9},{9,8},{10,11... | collective-permute-start | bytes 1179656 | tf_op jit(solution)/shard_map/ppermute | solution.py:32
  50.0 14.3 %collective-permute-start.17 = (bf16[192,1024]{1,0:T(8,128)(2,1)S(1)}, bf16[192,1024]{1,0:T(8,128)(2,1)S(1)}, u32[]{:S(2)}, u32[]{:S(2)}) collective-permute-start(bf16[192,1024]{1,0:T(8,128)(2,1)S(1)} %get-tuple-element.57), channel_id=1, source_target_pairs={{0,24},{1,65},{2,26},{3,67},{4,12},{5,69},{6,14},{7,71},{8,0},{9,7... | collective-permute-start | bytes 1179656 | tf_op jit(solution)/shard_map/ppermute | solution.py:28
  51.3 13.0 %collective-permute-start.18 = (bf16[192,1024]{1,0:T(8,128)(2,1)S(1)}, bf16[192,1024]{1,0:T(8,128)(2,1)S(1)}, u32[]{:S(2)}, u32[]{:S(2)}) collective-permute-start(bf16[192,1024]{1,0:T(8,128)(2,1)S(1)} %get-tuple-element.58), channel_id=1, source_target_pairs={{0,28},{1,193},{2,30},{3,195},{4,0},{5,197},{6,2},{7,199},{8,4},{9... | collective-permute-start | bytes 1179656 | tf_op jit(solution)/shard_map/ppermute | solution.py:28
  55.8 8.6 %collective-permute-start.20 = (bf16[192,1024]{1,0:T(8,128)(2,1)S(1)}, bf16[192,1024]{1,0:T(8,128)(2,1)S(1)}, u32[]{:S(2)}, u32[]{:S(2)}) collective-permute-start(bf16[192,1024]{1,0:T(8,128)(2,1)S(1)} %shard_map.53), channel_id=1, source_target_pairs={{0,4},{1,33},{2,6},{3,35},{4,8},{5,37},{6,10},{7,39},{8,12},{9,41}... | collective-permute-start | bytes 1179656 | tf_op jit(solution)/shard_map/ppermute | solution.py:28
  60.9 9.4 %collective-permute-start.15 = (bf16[192,1024]{1,0:T(8,128)(2,1)S(1)}, bf16[192,1024]{1,0:T(8,128)(2,1)S(1)}, u32[]{:S(2)}, u32[]{:S(2)}) collective-permute-start(bf16[192,1024]{1,0:T(8,128)(2,1)S(1)} %get-tuple-element.48), channel_id=1, source_target_pairs={{0,28},{1,193},{2,30},{3,195},{4,0},{5,197},{6,2},{7,199},{8,4},{9... | collective-permute-start | bytes 1179656 | tf_op jit(solution)/shard_map/ppermute | solution.py:28
  62.2 8.1 %collective-permute-start.16 = (bf16[192,1024]{1,0:T(8,128)(2,1)S(1)}, bf16[192,1024]{1,0:T(8,128)(2,1)S(1)}, u32[]{:S(2)}, u32[]{:S(2)}) collective-permute-start(bf16[192,1024]{1,0:T(8,128)(2,1)S(1)} %get-tuple-element.49), channel_id=1, source_target_pairs={{0,4},{1,65},{2,6},{3,67},{4,8},{5,69},{6,10},{7,71},{8,12},{9,73}... | collective-permute-start | bytes 1179656 | tf_op jit(solution)/shard_map/ppermute | solution.py:28
  64.7 8.6 %collective-permute-start.19 = (bf16[192,1024]{1,0:T(8,128)(2,1)S(1)}, bf16[192,1024]{1,0:T(8,128)(2,1)S(1)}, u32[]{:S(2)}, u32[]{:S(2)}) collective-permute-start(bf16[192,1024]{1,0:T(8,128)(2,1)S(1)} %get-tuple-element.61), channel_id=1, source_target_pairs={{0,24},{1,33},{2,26},{3,35},{4,28},{5,37},{6,30},{7,39},{8,0},{9,4... | collective-permute-start | bytes 1179656 | tf_op jit(solution)/shard_map/ppermute | solution.py:28
  67.9 8.4 %collective-permute-start.21 = (bf16[192,1024]{1,0:T(8,128)(2,1)S(1)}, bf16[192,1024]{1,0:T(8,128)(2,1)S(1)}, u32[]{:S(2)}, u32[]{:S(2)}) collective-permute-start(bf16[192,1024]{1,0:T(8,128)(2,1)S(1)} %get-tuple-element.62), channel_id=1, source_target_pairs={{0,8},{1,129},{2,10},{3,131},{4,12},{5,133},{6,14},{7,135},{8,16},... | collective-permute-start | bytes 1179656 | tf_op jit(solution)/shard_map/ppermute | solution.py:28

commit v2 on v1

--- a/solution.py
+++ b/solution.py
@@ -32,7 +32,8 @@
     return lax.ppermute(v, AXES, [(i, i ^ 1) for i in range(NX * NYH * NZ * 4)])
 
 
-POOL_STEP = 32
+POOL_STEP = 48
+PICK = 16
 
 
 def pool_kernel(x_ref, o_ref, buf, sems):
@@ -43,15 +44,16 @@
     ]
     for copy in copies:
         copy.start()
-    row = lax.broadcasted_iota(jnp.int32, (POOL_STEP, POOL_STEP * patches), 0) * patches
-    col = lax.broadcasted_iota(jnp.int32, (POOL_STEP, POOL_STEP * patches), 1)
+    row = lax.broadcasted_iota(jnp.int32, (PICK, PICK * patches), 0) * patches
+    col = lax.broadcasted_iota(jnp.int32, (PICK, PICK * patches), 1)
     pick = jnp.where((col >= row) & (col < row + patches), 1.0, 0.0).astype(jnp.bfloat16)
-    for i, copy in zip(range(0, n, POOL_STEP), copies):
-        copy.wait()
-        flat_rows = buf[i:i + POOL_STEP].reshape(POOL_STEP * patches, width)
-        pooled = jnp.dot(pick, flat_rows, preferred_element_type=jnp.float32) * (1.0 / patches)
+    for i in range(0, n, PICK):
+        if i % POOL_STEP == 0:
+            copies[i // POOL_STEP].wait()
+        pooled = jnp.dot(pick, buf[i:i + PICK].reshape(PICK * patches, width), preferred_element_type=jnp.float32)
+        pooled = pooled * (1.0 / patches)
         square = jnp.sum(pooled * pooled, axis=1, keepdims=True)
-        o_ref[i:i + POOL_STEP, :] = (pooled * (1.0 / jnp.sqrt(square + 1e-06))).astype(o_ref.dtype)
+        o_ref[i:i + PICK, :] = (pooled * (1.0 / jnp.sqrt(square + 1e-06))).astype(o_ref.dtype)
 
 
 def pool(rows):
@@ -91,7 +93,7 @@
         o_ref[...] = total[n * i:n * (i + 1)].astype(o_ref.dtype)
 
 
-def grads(state, slots, first_col, groups, sums, dtype):
+def grads(state, slots, first_col, groups, sums, dtypes):
     par, row_ids, col_ids, rows, cols = state
     n, width = rows[0].shape
     count = len(slots)
@@ -101,7 +103,7 @@
         functools.partial(grad_kernel, slots, first_col, groups, sums is not None),
         in_specs=[vmem] * (3 + len(operands)),
         out_specs=[vmem] * count,
-        out_shape=[jax.ShapeDtypeStruct((n, width), dtype)] * count,
+        out_shape=[jax.ShapeDtypeStruct((n, width), dtype) for dtype in dtypes],
         compiler_params=pltpu.CompilerParams(vmem_limit_bytes=VMEM_LIMIT),
         cost_estimate=pl.CostEstimate(flops=16 * groups * count * n * n * width, bytes_accessed=4 * n * width * 2, transcendentals=4 * groups * count * n * n),
     )(par, row_ids, col_ids, *operands)
@@ -153,25 +155,28 @@
     rows[6] = send(rows[2], MOVES[6])
     cols = [partner(v) for v in rows[:5]]
     state = (par, row_ids, col_ids, rows, cols)
-    h0, h3, h4 = grads(state, (0, 3, 4), 0, 1, None, f32)
-    h1, h2 = grads(state, (1, 2), 0, 1, None, f32)
+    h0, h3, h4 = grads(state, (0, 3, 4), 0, 1, None, (f32,) * 3)
+    h1, h2 = grads(state, (1, 2), 0, 1, None, (f32,) * 2)
     rows[5], rows[6], rows[7], h0, h1, h2, h3, h4 = lax.optimization_barrier((rows[5], rows[6], rows[7], h0, h1, h2, h3, h4))
     cols += [partner(rows[k]) for k in (5, 6, 7)]
-    h7, h5 = grads(state, (7, 5), 0, 1, None, f32)
-    g7, g5 = grads(state, (7, 5), 4, 1, (h7, h5), bf16)
-    rows[6], r7, r5 = lax.optimization_barrier((rows[6], g7, g5))
-    r7, r5 = send(r7, BACK[7]), send(r5, BACK[5])
-    (g6,) = grads(state, (6,), 0, 2, None, bf16)
+    h7, h5, h6 = grads(state, (7, 5, 6), 0, 1, None, (f32,) * 3)
+    g7, g5, g6 = grads(state, (7, 5, 6), 4, 1, (h7, h5, h6), (bf16,) * 3)
+    r7 = send(g7, BACK[7])
+    r5 = send(g5, BACK[5])
     r6 = send(g6, BACK[6])
-    g1, g2 = grads(state, (1, 2), 4, 1, (h1, h2), f32)
-    g3, g4 = grads(state, (3, 4), 4, 1, (h3, h4), bf16)
+    rows[1], g6 = lax.optimization_barrier((rows[1], g6))
+    g1, g2, g3, g4 = grads(state, (1, 2, 3, 4), 4, 1, (h1, h2, h3, h4), (f32, f32, bf16, bf16))
     r3 = send(g3, BACK[3])
     r4 = send(g4, BACK[4])
-    r7 = r7.astype(f32)
-    r1 = send((g1 + jnp.where(turn, 0.0, r7) + r5.astype(f32)).astype(bf16), BACK[1])
-    r2 = send((g2 + jnp.where(turn, r7, 0.0) + r6.astype(f32)).astype(bf16), BACK[2])
-    (g0,) = grads(state, (0,), 4, 1, (h0,), f32)
-    out = g0 + r3.astype(f32) + r4.astype(f32) + r1.astype(f32) + r2.astype(f32)
+    s1 = (g1 + jnp.where(turn, 0.0, r7.astype(f32)) + r5.astype(f32)).astype(bf16)
+    s1, r7 = lax.optimization_barrier((s1, r7))
+    r1 = send(s1, BACK[1])
+    s2 = (g2 + jnp.where(turn, r7.astype(f32), 0.0) + r6.astype(f32)).astype(bf16)
+    r2 = send(s2, BACK[2])
+    rows[0], s2 = lax.optimization_barrier((rows[0], s2))
+    (g0,) = grads(state, (0,), 4, 1, (h0,), (f32,))
+    near = lax.optimization_barrier(g0 + r3.astype(f32) + r4.astype(f32))
+    out = near + r1.astype(f32) + r2.astype(f32)
     return out.reshape(1, n, width)
 
 

time: 78.9 us -> 77.8 us (0.986)
  the two profiles are of different devices: /device:TPU:1 before, /device:TPU:28 now
where the time goes in v2:
time: 77.8 us; the launch traced here: 77.5 us
  starting transfers between devices  27.4 us (35%)
  waiting for transfers between devices  24.3 us (31%)
  Pallas kernels  22.2 us (29%)
  local copies, waits for them, and re-layouts  1.85 us (2%)
  other arithmetic  1.71 us (2%)
    ppermute x14, starting transfers between devices, send(): return lax.ppermute(v, AXES, pairs)  26.3 us
    ppermute x14, waiting for transfers between devices, send(): return lax.ppermute(v, AXES, pairs)  24.2 us
    pallas_call x6, Pallas kernels, grads(): pl.pallas_call(functools.partial(grad_kernel, slots, first_col, groups, s...  18.1 us
    pallas_call x1, Pallas kernels, pool(): pl.pallas_call(pool_kernel, in_specs=[pl.BlockSpec(memory_space=pltpu.HBM...  4.03 us
  transfers between devices with their start and end apart: 22, of which 8 were waited for; matrix products, arithmetic and copies ran while one was open for 1% of the time, Pallas kernels for 20%

profile of v2, /device:TPU:28, one launch (start us, length us, event | category | flops | bytes accessed | tf_op | source)
XLA Modules:
  0.0 77.5 jit_solution(14498700306232901144)
XLA Ops:
  0.0 1.3 %fusion = (s32[192]{0:T(256)S(1)}, s32[192]{0:T(256)S(1)}, s32[192]{0:T(256)S(1)}, s32[192]{0:T(256)S(1)}, s32[192]{0:T(256)S(1)}, /*index=5*/s32[192]{0:T(256)S...) fusion(s32[12288]{0:T(1024)} %param.5, ...), kind=kLoop, calls=%fused_computation.6 | loop fusion | bytes 24640 | tf_op jit(solution)/shard_map/dynamic_slice | solution.py:139
  1.4 4.0 %pool.1.refs_0_ = bf16[192,1024]{1,0:T(8,128)(2,1)} custom-call(bf16[192,16,1024]{2,1,0:T(8,128)(2,1)} %bitcast.3), custom_call_target="tpu_custom_call" | custom-call | flops 6291456 | bytes 6291456 | tf_op jit(solution)/shard_map/pool/pallas_call | solution.py:61
  6.0 1.9 %collective-permute-start.5 = (bf16[192,1024]{1,0:T(8,128)(2,1)}, bf16[192,1024]{1,0:T(8,128)(2,1)S(1)}, u32[]{:S(2)}, u32[]{:S(2)}) collective-permute-start(bf16[192,1024]{1,0:T(8,128)(2,1)} %pool.1.refs_0_), channel_id=1, source_target_pairs={{0,4},{1,65},{2,6},{3,67},{4,8},{5,69},{6,10},{7,71},{8,12},{9,73}... | collective-permute-start | bytes 1179656 | tf_op jit(solution)/shard_map/ppermute | solution.py:28
  7.9 3.2 %collective-permute-start = (bf16[192,1024]{1,0:T(8,128)(2,1)}, bf16[192,1024]{1,0:T(8,128)(2,1)S(1)}, u32[]{:S(2)}, u32[]{:S(2)}) collective-permute-start(bf16[192,1024]{1,0:T(8,128)(2,1)} %pool.1.refs_0_), channel_id=1, source_target_pairs={{0,8},{1,33},{2,10},{3,35},{4,12},{5,37},{6,14},{7,39},{8,16},{9,4... | collective-permute-start | bytes 1179656 | tf_op jit(solution)/shard_map/ppermute | solution.py:28
  11.2 2.2 %collective-permute-start.2 = (bf16[192,1024]{1,0:T(8,128)(2,1)}, bf16[192,1024]{1,0:T(8,128)(2,1)S(1)}, u32[]{:S(2)}, u32[]{:S(2)}) collective-permute-start(bf16[192,1024]{1,0:T(8,128)(2,1)} %pool.1.refs_0_), channel_id=1, source_target_pairs={{0,24},{1,129},{2,26},{3,131},{4,28},{5,133},{6,30},{7,135},{8,0},... | collective-permute-start | bytes 1179656 | tf_op jit(solution)/shard_map/ppermute | solution.py:28
  13.3 1.5 %collective-permute-start.6 = (bf16[192,1024]{1,0:T(8,128)(2,1)}, bf16[192,1024]{1,0:T(8,128)(2,1)S(1)}, u32[]{:S(2)}, u32[]{:S(2)}) collective-permute-start(bf16[192,1024]{1,0:T(8,128)(2,1)} %pool.1.refs_0_), channel_id=1, source_target_pairs={{0,28},{1,193},{2,30},{3,195},{4,0},{5,197},{6,2},{7,199},{8,4},{9... | collective-permute-start | bytes 1179656 | tf_op jit(solution)/shard_map/ppermute | solution.py:28
  14.9 2.9 %collective-permute-done.5.refs_1_.refs_2_ = bf16[192,1024]{1,0:T(8,128)(2,1)S(1)} collective-permute-done((bf16[192,1024]{1,0:T(8,128)(2,1)}, bf16[192,1024]{1,0:T(8,128)(2,1)S(1)}, u32[]{:S(2)}, u32[]{:S(2)}) %collective-permute-start.5) | collective-permute-done | bytes 393248 | tf_op jit(solution)/shard_map/ppermute | solution.py:28
  17.8 6.2 %collective-permute-done.refs_0_ = bf16[192,1024]{1,0:T(8,128)(2,1)S(1)} collective-permute-done((bf16[192,1024]{1,0:T(8,128)(2,1)}, bf16[192,1024]{1,0:T(8,128)(2,1)S(1)}, u32[]{:S(2)}, u32[]{:S(2)}) %collective-permute-start) | collective-permute-done | bytes 393248 | tf_op jit(solution)/shard_map/ppermute | solution.py:28
  24.0 0.5 collective-permute-start.9
  24.6 3.1 %collective-permute-start.4 = (bf16[192,1024]{1,0:T(8,128)(2,1)S(1)}, bf16[192,1024]{1,0:T(8,128)(2,1)S(1)}, u32[]{:S(2)}, u32[]{:S(2)}) collective-permute-start(bf16[192,1024]{1,0:T(8,128)(2,1)S(1)} %broadcast_select_fusion), channel_id=1, source_target_pairs={{0,8},{1,193},{2,10},{3,195},{4,28},{5,197},{6,30},{7,199},{8,16},... | collective-permute-start | bytes 1179656 | tf_op jit(solution)/shard_map/ppermute | solution.py:28
  27.7 1.1 %collective-permute-done.6.refs_2_.refs_3_ = bf16[192,1024]{1,0:T(8,128)(2,1)S(1)} collective-permute-done((bf16[192,1024]{1,0:T(8,128)(2,1)}, bf16[192,1024]{1,0:T(8,128)(2,1)S(1)}, u32[]{:S(2)}, u32[]{:S(2)}) %collective-permute-start.6) | collective-permute-done | bytes 393248 | tf_op jit(solution)/shard_map/ppermute | solution.py:28
  28.8 2.0 %collective-permute-start.1 = (bf16[192,1024]{1,0:T(8,128)(2,1)S(1)}, bf16[192,1024]{1,0:T(8,128)(2,1)S(1)}, u32[]{:S(2)}, u32[]{:S(2)}) collective-permute-start(bf16[192,1024]{1,0:T(8,128)(2,1)S(1)} %collective-permute-done.refs_0_), channel_id=1, source_target_pairs={{0,4},{1,65},{2,6},{3,67},{4,8},{5,69},{6,10},{7,71},{8,12},{9,73}... | collective-permute-start | bytes 1179656 | tf_op jit(solution)/shard_map/ppermute | solution.py:28
  30.8 1.2 %collective-permute-start.3 = (bf16[192,1024]{1,0:T(8,128)(2,1)S(1)}, bf16[192,1024]{1,0:T(8,128)(2,1)S(1)}, u32[]{:S(2)}, u32[]{:S(2)}) collective-permute-start(bf16[192,1024]{1,0:T(8,128)(2,1)S(1)} %collective-permute-done.2.refs_1_), channel_id=1, source_target_pairs={{0,28},{1,33},{2,30},{3,35},{4,0},{5,37},{6,2},{7,39},{8,4},{9,41}... | collective-permute-start | bytes 1179656 | tf_op jit(solution)/shard_map/ppermute | solution.py:28
  32.1 3.1 %shard_map.47 = (f32[192,1024]{1,0:T(8,128)S(1)}, f32[192,1024]{1,0:T(8,128)S(1)}) custom-call(f32[4,768]{1,0:T(4,128)S(1)} %broadcast_in_dim.11.par_ref, s32[1536,128]{1,0:T(8,128)S(1)} %broadcast_in_dim.22.row_ref, s32[1,1536]{1,0:T(1,128)S(1)} %broadcast_in_dim.23.col_ref, bf16[192,1024]{1,0:T(8,128)(2,1)S(1)} %collective-permute-done.refs_0_, ...), custom_call_target="tpu_custom_call" | custom-call | flops 1207959552 | bytes 1572864 | tf_op jit(solution)/shard_map/pallas_call | solution.py:102
  35.2 3.9 %shard_map.46 = (f32[192,1024]{1,0:T(8,128)S(1)}, f32[192,1024]{1,0:T(8,128)S(1)}, f32[192,1024]{1,0:T(8,128)S(1)}) custom-call(f32[4,768]{1,0:T(4,128)S(1)} %broadcast_in_dim.11.par_ref, s32[1536,128]{1,0:T(8,128)S(1)} %broadcast_in_dim.22.row_ref, s32[1,1536]{1,0:T(1,128)S(1)} %broadcast_in_dim.23.col_ref, bf16[192,1024]{1,0:T(8,128)(2,1)S(1)} %copy-done, ...), custom_call_target="tpu_custom_call" | custom-call | flops 1811939328 | bytes 1572864 | tf_op jit(solution)/shard_map/pallas_call | solution.py:102
  39.1 1.7 %collective-permute-done.3.refs_2_ = bf16[192,1024]{1,0:T(8,128)(2,1)S(1)} collective-permute-done((bf16[192,1024]{1,0:T(8,128)(2,1)S(1)}, bf16[192,1024]{1,0:T(8,128)(2,1)S(1)}, u32[]{:S(2)}, u32[]{:S(2)}) %collective-permute-start.3) | collective-permute-done | bytes 393248 | tf_op jit(solution)/shard_map/ppermute | solution.py:28
  40.9 0.5 collective-permute-start.13
  41.4 3.9 %shard_map.48 = (f32[192,1024]{1,0:T(8,128)S(1)}, f32[192,1024]{1,0:T(8,128)S(1)}, f32[192,1024]{1,0:T(8,128)S(1)}) custom-call(f32[4,768]{1,0:T(4,128)S(1)} %broadcast_in_dim.11.par_ref, s32[1536,128]{1,0:T(8,128)S(1)} %broadcast_in_dim.22.row_ref, s32[1,1536]{1,0:T(1,128)S(1)} %broadcast_in_dim.23.col_ref, ...), custom_call_target="tpu_custom_call" | custom-call | flops 1811939328 | bytes 1572864 | tf_op jit(solution)/shard_map/pallas_call | solution.py:102
  45.3 2.6 %shard_map.49 = (bf16[192,1024]{1,0:T(8,128)(2,1)S(1)}, bf16[192,1024]{1,0:T(8,128)(2,1)S(1)}, bf16[192,1024]{1,0:T(8,128)(2,1)S(1)}) custom-call(f32[4,768]{1,0:T(4,128)S(1)} %broadcast_in_dim.11.par_ref, s32[1536,128]{1,0:T(8,128)S(1)} %broadcast_in_dim.22.row_ref, s32[1,1536]{1,0:T(1,128)S(1)} %broadcast_in_dim.23.col_ref, ...), custom_call_target="tpu_custom_call" | custom-call | flops 1811939328 | bytes 1572864 | tf_op jit(solution)/shard_map/pallas_call | solution.py:102
  47.9 2.7 %collective-permute-start.15 = (bf16[192,1024]{1,0:T(8,128)(2,1)S(1)}, bf16[192,1024]{1,0:T(8,128)(2,1)S(1)}, u32[]{:S(2)}, u32[]{:S(2)}) collective-permute-start(bf16[192,1024]{1,0:T(8,128)(2,1)S(1)} %get-tuple-element.59), channel_id=1, source_target_pairs={{0,24},{1,65},{2,26},{3,67},{4,12},{5,69},{6,14},{7,71},{8,0},{9,7... | collective-permute-start | bytes 1179656 | tf_op jit(solution)/shard_map/ppermute | solution.py:28
  50.6 0.5 collective-permute-start.16
  51.1 1.6 %collective-permute-start.17 = (bf16[192,1024]{1,0:T(8,128)(2,1)S(1)}, bf16[192,1024]{1,0:T(8,128)(2,1)S(1)}, u32[]{:S(2)}, u32[]{:S(2)}) collective-permute-start(bf16[192,1024]{1,0:T(8,128)(2,1)S(1)} %get-tuple-element.51), channel_id=1, source_target_pairs={{0,4},{1,33},{2,6},{3,35},{4,8},{5,37},{6,10},{7,39},{8,12},{9,41}... | collective-permute-start | bytes 1179656 | tf_op jit(solution)/shard_map/ppermute | solution.py:28
  52.7 3.4 %shard_map.50 = (f32[192,1024]{1,0:T(8,128)S(1)}, f32[192,1024]{1,0:T(8,128)S(1)}, bf16[192,1024]{1,0:T(8,128)(2,1)S(1)}, bf16[192,1024]{1,0:T(8,128)(2,1)S(1)}) custom-call(f32[4,768]{1,0:T(4,128)S(1)} %broadcast_in_dim.11.par_ref, s32[1536,128]{1,0:T(8,128)S(1)} %broadcast_in_dim.22.row_ref, s32[1,1536]{1,0:T(1,128)S(1)} %broadcast_in_dim.23.col_ref, ...), custom_call_target="tpu_custom_call" | custom-call | flops 2415919104 | bytes 1572864 | tf_op jit(solution)/shard_map/pallas_call | solution.py:102
  56.1 1.7 %collective-permute-start.18 = (bf16[192,1024]{1,0:T(8,128)(2,1)S(1)}, bf16[192,1024]{1,0:T(8,128)(2,1)S(1)}, u32[]{:S(2)}, u32[]{:S(2)}) collective-permute-start(bf16[192,1024]{1,0:T(8,128)(2,1)S(1)} %get-tuple-element.64), channel_id=1, source_target_pairs={{0,28},{1,193},{2,30},{3,195},{4,0},{5,197},{6,2},{7,199},{8,4},{9... | collective-permute-start | bytes 1179656 | tf_op jit(solution)/shard_map/ppermute | solution.py:28
  57.8 0.4 collective-permute-start.19
  58.2 2.7 %collective-permute-done.16 = bf16[192,1024]{1,0:T(8,128)(2,1)S(1)} collective-permute-done((bf16[192,1024]{1,0:T(8,128)(2,1)S(1)}, bf16[192,1024]{1,0:T(8,128)(2,1)S(1)}, u32[]{:S(2)}, u32[]{:S(2)}) %collective-permute-start.16) | collective-permute-done | bytes 393248 | tf_op jit(solution)/shard_map/ppermute | solution.py:28
  61.3 2.2 %collective-permute-start.21 = (bf16[192,1024]{1,0:T(8,128)(2,1)S(1)}, bf16[192,1024]{1,0:T(8,128)(2,1)S(1)}, u32[]{:S(2)}, u32[]{:S(2)}) collective-permute-start(bf16[192,1024]{1,0:T(8,128)(2,1)S(1)} %add_convert_fusion), channel_id=1, source_target_pairs={{0,8},{1,129},{2,10},{3,131},{4,12},{5,133},{6,14},{7,135},{8,16},... | collective-permute-start | bytes 1179656 | tf_op jit(solution)/shard_map/ppermute | solution.py:28
  63.5 2.0 %collective-permute-start.20 = (bf16[192,1024]{1,0:T(8,128)(2,1)S(1)}, bf16[192,1024]{1,0:T(8,128)(2,1)S(1)}, u32[]{:S(2)}, u32[]{:S(2)}) collective-permute-start(bf16[192,1024]{1,0:T(8,128)(2,1)S(1)} %add_convert_fusion.1), channel_id=1, source_target_pairs={{0,24},{1,33},{2,26},{3,35},{4,28},{5,37},{6,30},{7,39},{8,0},{9,4... | collective-permute-start | bytes 1179656 | tf_op jit(solution)/shard_map/ppermute | solution.py:28
  65.5 1.2 %shard_map.51 = f32[192,1024]{1,0:T(8,128)S(1)} custom-call(f32[4,768]{1,0:T(4,128)S(1)} %broadcast_in_dim.11.par_ref, s32[1536,128]{1,0:T(8,128)S(1)} %broadcast_in_dim.22.row_ref, s32[1,1536]{1,0:T(1,128)S(1)} %broadcast_in_dim.23.col_ref, bf16[192,1024]{1,0:T(8,128)(2,1)S(1)} %copy-done, ...), custom_call_target="tpu_custom_call" | custom-call | flops 603979776 | bytes 1572864 | tf_op jit(solution)/shard_map/pallas_call | solution.py:102
  67.0 5.7 %collective-permute-done.21 = bf16[192,1024]{1,0:T(8,128)(2,1)S(1)} collective-permute-done((bf16[192,1024]{1,0:T(8,128)(2,1)S(1)}, bf16[192,1024]{1,0:T(8,128)(2,1)S(1)}, u32[]{:S(2)}, u32[]{:S(2)}) %collective-permute-start.21) | collective-permute-done | bytes 393248 | tf_op jit(solution)/shard_map/ppermute | solution.py:28
  72.7 3.8 %collective-permute-done.20 = bf16[192,1024]{1,0:T(8,128)(2,1)S(1)} collective-permute-done((bf16[192,1024]{1,0:T(8,128)(2,1)S(1)}, bf16[192,1024]{1,0:T(8,128)(2,1)S(1)}, u32[]{:S(2)}, u32[]{:S(2)}) %collective-permute-start.20) | collective-permute-done | bytes 393248 | tf_op jit(solution)/shard_map/ppermute | solution.py:28
  76.5 1.1 %add_bitcast_fusion = f32[1,192,1024]{2,1,0:T(8,128)} fusion(bf16[192,1024]{1,0:T(8,128)(2,1)S(1)} %collective-permute-done.21, f32[192,1024]{1,0:T(8,128)S(1)} %convert_add_fusion, bf16[192,1024]{1,0:T(8,128)(2,1)S(1)} %collective-permute-done.20), kind=kLoop, calls=%fused_computation | loop fusion | flops 786432 | bytes 2359296 | tf_op jit(solution)/shard_map/reshape | solution.py:180
  (37 shorter events, 1.3 us)
Async XLA Ops:
  0.0 5.5 %copy-start.2 = (f32[2]{0:T(128)S(1)}, f32[2]{0:T(128)}, u32[]{:S(2)}) copy-start(f32[2]{0:T(128)} %param.6) | copy-start | bytes 28
  0.0 5.5 %copy-start.1 = (f32[2]{0:T(128)S(1)}, f32[2]{0:T(128)}, u32[]{:S(2)}) copy-start(f32[2]{0:T(128)} %param.7) | copy-start | bytes 28
  5.5 29.7 %copy-start = (bf16[192,1024]{1,0:T(8,128)(2,1)S(1)}, bf16[192,1024]{1,0:T(8,128)(2,1)}, u32[]{:S(2)}) copy-start(bf16[192,1024]{1,0:T(8,128)(2,1)} %pool.1.refs_0_) | copy-start | bytes 1179652
  6.0 11.8 %collective-permute-start.5 = (bf16[192,1024]{1,0:T(8,128)(2,1)}, bf16[192,1024]{1,0:T(8,128)(2,1)S(1)}, u32[]{:S(2)}, u32[]{:S(2)}) collective-permute-start(bf16[192,1024]{1,0:T(8,128)(2,1)} %pool.1.refs_0_), channel_id=1, source_target_pairs={{0,4},{1,65},{2,6},{3,67},{4,8},{5,69},{6,10},{7,71},{8,12},{9,73}... | collective-permute-start | bytes 1179656 | tf_op jit(solution)/shard_map/ppermute | solution.py:28
  7.9 16.1 %collective-permute-start = (bf16[192,1024]{1,0:T(8,128)(2,1)}, bf16[192,1024]{1,0:T(8,128)(2,1)S(1)}, u32[]{:S(2)}, u32[]{:S(2)}) collective-permute-start(bf16[192,1024]{1,0:T(8,128)(2,1)} %pool.1.refs_0_), channel_id=1, source_target_pairs={{0,8},{1,33},{2,10},{3,35},{4,12},{5,37},{6,14},{7,39},{8,16},{9,4... | collective-permute-start | bytes 1179656 | tf_op jit(solution)/shard_map/ppermute | solution.py:28
  11.2 12.9 %collective-permute-start.2 = (bf16[192,1024]{1,0:T(8,128)(2,1)}, bf16[192,1024]{1,0:T(8,128)(2,1)S(1)}, u32[]{:S(2)}, u32[]{:S(2)}) collective-permute-start(bf16[192,1024]{1,0:T(8,128)(2,1)} %pool.1.refs_0_), channel_id=1, source_target_pairs={{0,24},{1,129},{2,26},{3,131},{4,28},{5,133},{6,30},{7,135},{8,0},... | collective-permute-start | bytes 1179656 | tf_op jit(solution)/shard_map/ppermute | solution.py:28
  13.3 11.2 %collective-permute-start.7 = (bf16[192,1024]{1,0:T(8,128)(2,1)}, bf16[192,1024]{1,0:T(8,128)(2,1)S(1)}, u32[]{:S(2)}, u32[]{:S(2)}) collective-permute-start(bf16[192,1024]{1,0:T(8,128)(2,1)} %pool.1.refs_0_), channel_id=1, source_target_pairs={{0,1},{1,0},{2,3},{3,2},{4,5},{5,4},{6,7},{7,6},{8,9},{9,8},{10,11... | collective-permute-start | bytes 1179656 | tf_op jit(solution)/shard_map/ppermute | solution.py:32
  13.3 15.5 %collective-permute-start.6 = (bf16[192,1024]{1,0:T(8,128)(2,1)}, bf16[192,1024]{1,0:T(8,128)(2,1)S(1)}, u32[]{:S(2)}, u32[]{:S(2)}) collective-permute-start(bf16[192,1024]{1,0:T(8,128)(2,1)} %pool.1.refs_0_), channel_id=1, source_target_pairs={{0,28},{1,193},{2,30},{3,195},{4,0},{5,197},{6,2},{7,199},{8,4},{9... | collective-permute-start | bytes 1179656 | tf_op jit(solution)/shard_map/ppermute | solution.py:28
  17.8 13.0 %collective-permute-start.10 = (bf16[192,1024]{1,0:T(8,128)(2,1)S(1)}, bf16[192,1024]{1,0:T(8,128)(2,1)}, u32[]{:S(2)}, u32[]{:S(2)}) collective-permute-start(bf16[192,1024]{1,0:T(8,128)(2,1)S(1)} %collective-permute-done.5.refs_1_.refs_2_), channel_id=1, source_target_pairs={{0,1},{1,0},{2,3},{3,2},{4,5},{5,4},{6,7},{7,6},{8,9},{9,8},{10,11... | collective-permute-start | bytes 1179656 | tf_op jit(solution)/shard_map/ppermute | solution.py:32
  24.0 8.1 %collective-permute-start.8 = (bf16[192,1024]{1,0:T(8,128)(2,1)S(1)}, bf16[192,1024]{1,0:T(8,128)(2,1)}, u32[]{:S(2)}, u32[]{:S(2)}) collective-permute-start(bf16[192,1024]{1,0:T(8,128)(2,1)S(1)} %collective-permute-done.refs_0_), channel_id=1, source_target_pairs={{0,1},{1,0},{2,3},{3,2},{4,5},{5,4},{6,7},{7,6},{8,9},{9,8},{10,11... | collective-permute-start | bytes 1179656 | tf_op jit(solution)/shard_map/ppermute | solution.py:32
  24.0 8.1 %collective-permute-start.9 = (bf16[192,1024]{1,0:T(8,128)(2,1)S(1)}, bf16[192,1024]{1,0:T(8,128)(2,1)}, u32[]{:S(2)}, u32[]{:S(2)}) collective-permute-start(bf16[192,1024]{1,0:T(8,128)(2,1)S(1)} %collective-permute-done.2.refs_1_), channel_id=1, source_target_pairs={{0,1},{1,0},{2,3},{3,2},{4,5},{5,4},{6,7},{7,6},{8,9},{9,8},{10,11... | collective-permute-start | bytes 1179656 | tf_op jit(solution)/shard_map/ppermute | solution.py:32
  24.6 14.5 %collective-permute-start.4 = (bf16[192,1024]{1,0:T(8,128)(2,1)S(1)}, bf16[192,1024]{1,0:T(8,128)(2,1)S(1)}, u32[]{:S(2)}, u32[]{:S(2)}) collective-permute-start(bf16[192,1024]{1,0:T(8,128)(2,1)S(1)} %broadcast_select_fusion), channel_id=1, source_target_pairs={{0,8},{1,193},{2,10},{3,195},{4,28},{5,197},{6,30},{7,199},{8,16},... | collective-permute-start | bytes 1179656 | tf_op jit(solution)/shard_map/ppermute | solution.py:28
  28.8 10.3 %collective-permute-start.1 = (bf16[192,1024]{1,0:T(8,128)(2,1)S(1)}, bf16[192,1024]{1,0:T(8,128)(2,1)S(1)}, u32[]{:S(2)}, u32[]{:S(2)}) collective-permute-start(bf16[192,1024]{1,0:T(8,128)(2,1)S(1)} %collective-permute-done.refs_0_), channel_id=1, source_target_pairs={{0,4},{1,65},{2,6},{3,67},{4,8},{5,69},{6,10},{7,71},{8,12},{9,73}... | collective-permute-start | bytes 1179656 | tf_op jit(solution)/shard_map/ppermute | solution.py:28
  30.8 10.0 %collective-permute-start.3 = (bf16[192,1024]{1,0:T(8,128)(2,1)S(1)}, bf16[192,1024]{1,0:T(8,128)(2,1)S(1)}, u32[]{:S(2)}, u32[]{:S(2)}) collective-permute-start(bf16[192,1024]{1,0:T(8,128)(2,1)S(1)} %collective-permute-done.2.refs_1_), channel_id=1, source_target_pairs={{0,28},{1,33},{2,30},{3,35},{4,0},{5,37},{6,2},{7,39},{8,4},{9,41}... | collective-permute-start | bytes 1179656 | tf_op jit(solution)/shard_map/ppermute | solution.py:28
  32.1 13.1 %collective-permute-start.11 = (bf16[192,1024]{1,0:T(8,128)(2,1)S(1)}, bf16[192,1024]{1,0:T(8,128)(2,1)S(1)}, u32[]{:S(2)}, u32[]{:S(2)}) collective-permute-start(bf16[192,1024]{1,0:T(8,128)(2,1)S(1)} %collective-permute-done.6.refs_2_.refs_3_), channel_id=1, source_target_pairs={{0,1},{1,0},{2,3},{3,2},{4,5},{5,4},{6,7},{7,6},{8,9},{9,8},{10,11... | collective-permute-start | bytes 1179656 | tf_op jit(solution)/shard_map/ppermute | solution.py:32
  40.8 4.4 %collective-permute-start.12 = (bf16[192,1024]{1,0:T(8,128)(2,1)S(1)}, bf16[192,1024]{1,0:T(8,128)(2,1)S(1)}, u32[]{:S(2)}, u32[]{:S(2)}) collective-permute-start(bf16[192,1024]{1,0:T(8,128)(2,1)S(1)} %collective-permute-done.1.refs_1_), channel_id=1, source_target_pairs={{0,1},{1,0},{2,3},{3,2},{4,5},{5,4},{6,7},{7,6},{8,9},{9,8},{10,11... | collective-permute-start | bytes 1179656 | tf_op jit(solution)/shard_map/ppermute | solution.py:32
  40.9 4.4 %collective-permute-start.13 = (bf16[192,1024]{1,0:T(8,128)(2,1)S(1)}, bf16[192,1024]{1,0:T(8,128)(2,1)S(1)}, u32[]{:S(2)}, u32[]{:S(2)}) collective-permute-start(bf16[192,1024]{1,0:T(8,128)(2,1)S(1)} %collective-permute-done.3.refs_2_), channel_id=1, source_target_pairs={{0,1},{1,0},{2,3},{3,2},{4,5},{5,4},{6,7},{7,6},{8,9},{9,8},{10,11... | collective-permute-start | bytes 1179656 | tf_op jit(solution)/shard_map/ppermute | solution.py:32
  41.4 3.9 %collective-permute-start.14 = (bf16[192,1024]{1,0:T(8,128)(2,1)S(1)}, bf16[192,1024]{1,0:T(8,128)(2,1)S(1)}, u32[]{:S(2)}, u32[]{:S(2)}) collective-permute-start(bf16[192,1024]{1,0:T(8,128)(2,1)S(1)} %collective-permute-done.4.refs_0_), channel_id=1, source_target_pairs={{0,1},{1,0},{2,3},{3,2},{4,5},{5,4},{6,7},{7,6},{8,9},{9,8},{10,11... | collective-permute-start | bytes 1179656 | tf_op jit(solution)/shard_map/ppermute | solution.py:32
  47.9 10.3 %collective-permute-start.15 = (bf16[192,1024]{1,0:T(8,128)(2,1)S(1)}, bf16[192,1024]{1,0:T(8,128)(2,1)S(1)}, u32[]{:S(2)}, u32[]{:S(2)}) collective-permute-start(bf16[192,1024]{1,0:T(8,128)(2,1)S(1)} %get-tuple-element.59), channel_id=1, source_target_pairs={{0,24},{1,65},{2,26},{3,67},{4,12},{5,69},{6,14},{7,71},{8,0},{9,7... | collective-permute-start | bytes 1179656 | tf_op jit(solution)/shard_map/ppermute | solution.py:28
  50.6 10.3 %collective-permute-start.16 = (bf16[192,1024]{1,0:T(8,128)(2,1)S(1)}, bf16[192,1024]{1,0:T(8,128)(2,1)S(1)}, u32[]{:S(2)}, u32[]{:S(2)}) collective-permute-start(bf16[192,1024]{1,0:T(8,128)(2,1)S(1)} %get-tuple-element.60), channel_id=1, source_target_pairs={{0,28},{1,193},{2,30},{3,195},{4,0},{5,197},{6,2},{7,199},{8,4},{9... | collective-permute-start | bytes 1179656 | tf_op jit(solution)/shard_map/ppermute | solution.py:28
  51.1 10.0 %collective-permute-start.17 = (bf16[192,1024]{1,0:T(8,128)(2,1)S(1)}, bf16[192,1024]{1,0:T(8,128)(2,1)S(1)}, u32[]{:S(2)}, u32[]{:S(2)}) collective-permute-start(bf16[192,1024]{1,0:T(8,128)(2,1)S(1)} %get-tuple-element.51), channel_id=1, source_target_pairs={{0,4},{1,33},{2,6},{3,35},{4,8},{5,37},{6,10},{7,39},{8,12},{9,41}... | collective-permute-start | bytes 1179656 | tf_op jit(solution)/shard_map/ppermute | solution.py:28
  56.1 10.6 %collective-permute-start.18 = (bf16[192,1024]{1,0:T(8,128)(2,1)S(1)}, bf16[192,1024]{1,0:T(8,128)(2,1)S(1)}, u32[]{:S(2)}, u32[]{:S(2)}) collective-permute-start(bf16[192,1024]{1,0:T(8,128)(2,1)S(1)} %get-tuple-element.64), channel_id=1, source_target_pairs={{0,28},{1,193},{2,30},{3,195},{4,0},{5,197},{6,2},{7,199},{8,4},{9... | collective-permute-start | bytes 1179656 | tf_op jit(solution)/shard_map/ppermute | solution.py:28
  57.8 9.0 %collective-permute-start.19 = (bf16[192,1024]{1,0:T(8,128)(2,1)S(1)}, bf16[192,1024]{1,0:T(8,128)(2,1)S(1)}, u32[]{:S(2)}, u32[]{:S(2)}) collective-permute-start(bf16[192,1024]{1,0:T(8,128)(2,1)S(1)} %get-tuple-element.65), channel_id=1, source_target_pairs={{0,4},{1,65},{2,6},{3,67},{4,8},{5,69},{6,10},{7,71},{8,12},{9,73}... | collective-permute-start | bytes 1179656 | tf_op jit(solution)/shard_map/ppermute | solution.py:28
  61.3 11.4 %collective-permute-start.21 = (bf16[192,1024]{1,0:T(8,128)(2,1)S(1)}, bf16[192,1024]{1,0:T(8,128)(2,1)S(1)}, u32[]{:S(2)}, u32[]{:S(2)}) collective-permute-start(bf16[192,1024]{1,0:T(8,128)(2,1)S(1)} %add_convert_fusion), channel_id=1, source_target_pairs={{0,8},{1,129},{2,10},{3,131},{4,12},{5,133},{6,14},{7,135},{8,16},... | collective-permute-start | bytes 1179656 | tf_op jit(solution)/shard_map/ppermute | solution.py:28
  63.5 13.0 %collective-permute-start.20 = (bf16[192,1024]{1,0:T(8,128)(2,1)S(1)}, bf16[192,1024]{1,0:T(8,128)(2,1)S(1)}, u32[]{:S(2)}, u32[]{:S(2)}) collective-permute-start(bf16[192,1024]{1,0:T(8,128)(2,1)S(1)} %add_convert_fusion.1), channel_id=1, source_target_pairs={{0,24},{1,33},{2,26},{3,35},{4,28},{5,37},{6,30},{7,39},{8,0},{9,4... | collective-permute-start | bytes 1179656 | tf_op jit(solution)/shard_map/ppermute | solution.py:28

commit v3 on v2

--- a/solution.py
+++ b/solution.py
@@ -155,17 +155,25 @@
     rows[6] = send(rows[2], MOVES[6])
     cols = [partner(v) for v in rows[:5]]
     state = (par, row_ids, col_ids, rows, cols)
-    h0, h3, h4 = grads(state, (0, 3, 4), 0, 1, None, (f32,) * 3)
-    h1, h2 = grads(state, (1, 2), 0, 1, None, (f32,) * 2)
-    rows[5], rows[6], rows[7], h0, h1, h2, h3, h4 = lax.optimization_barrier((rows[5], rows[6], rows[7], h0, h1, h2, h3, h4))
-    cols += [partner(rows[k]) for k in (5, 6, 7)]
-    h7, h5, h6 = grads(state, (7, 5, 6), 0, 1, None, (f32,) * 3)
-    g7, g5, g6 = grads(state, (7, 5, 6), 4, 1, (h7, h5, h6), (bf16,) * 3)
+    near_slots, far_slots = (1, 2, 3, 4), (5, 6)
+    h = grads(state, near_slots, 0, 1, None, (f32,) * 4)
+    rows[5], rows[6], h = lax.optimization_barrier((rows[5], rows[6], h))
+    cols += [partner(rows[k]) for k in far_slots]
+    h5, h6 = grads(state, far_slots, 0, 1, None, (f32,) * 2)
+    rows[7], h5, h6 = lax.optimization_barrier((rows[7], h5, h6))
+    cols += [partner(rows[7])]
+    (h7,) = grads(state, (7,), 0, 1, None, (f32,))
+    g7, g5 = grads(state, (7, 5), 4, 1, (h7, h5), (bf16,) * 2)
     r7 = send(g7, BACK[7])
+    rows[6], g5 = lax.optimization_barrier((rows[6], g5))
     r5 = send(g5, BACK[5])
+    (g6,) = grads(state, (6,), 4, 1, (h6,), (bf16,))
+    rows[1], g6 = lax.optimization_barrier((rows[1], g6))
     r6 = send(g6, BACK[6])
-    rows[1], g6 = lax.optimization_barrier((rows[1], g6))
-    g1, g2, g3, g4 = grads(state, (1, 2, 3, 4), 4, 1, (h1, h2, h3, h4), (f32, f32, bf16, bf16))
+    g1, g2, g3, g4 = grads(state, near_slots, 4, 1, h, (f32, f32, bf16, bf16))
+    rows[0], g1 = lax.optimization_barrier((rows[0], g1))
+    (g0,) = grads(state, (0,), 0, 2, None, (f32,))
+    g3, g4, g0 = lax.optimization_barrier((g3, g4, g0))
     r3 = send(g3, BACK[3])
     r4 = send(g4, BACK[4])
     s1 = (g1 + jnp.where(turn, 0.0, r7.astype(f32)) + r5.astype(f32)).astype(bf16)
@@ -173,8 +181,6 @@
     r1 = send(s1, BACK[1])
     s2 = (g2 + jnp.where(turn, r7.astype(f32), 0.0) + r6.astype(f32)).astype(bf16)
     r2 = send(s2, BACK[2])
-    rows[0], s2 = lax.optimization_barrier((rows[0], s2))
-    (g0,) = grads(state, (0,), 4, 1, (h0,), (f32,))
     near = lax.optimization_barrier(g0 + r3.astype(f32) + r4.astype(f32))
     out = near + r1.astype(f32) + r2.astype(f32)
     return out.reshape(1, n, width)

time: 77.8 us -> 80.7 us (1.037)
  the two profiles are of different devices: /device:TPU:28 before, /device:TPU:1 now
where the time goes in v3:
time: 80.7 us; the launch traced here: 79.3 us
  starting transfers between devices  43.2 us (54%)
  Pallas kernels  21.1 us (26%)
  waiting for transfers between devices  11.4 us (14%)
  local copies, waits for them, and re-layouts  1.67 us (2%)
  other arithmetic  1.66 us (2%)
    ppermute x14, starting transfers between devices, send(): return lax.ppermute(v, AXES, pairs)  25.1 us
    ppermute x8, starting transfers between devices, partner(): return lax.ppermute(v, AXES, [(i, i ^ 1) for i in range(NX * NYH * NZ * 4)])  18.1 us
    pallas_call x7, Pallas kernels, grads(): pl.pallas_call(functools.partial(grad_kernel, slots, first_col, groups, s...  17.1 us
    ppermute x14, waiting for transfers between devices, send(): return lax.ppermute(v, AXES, pairs)  11.3 us
    pallas_call x1, Pallas kernels, pool(): pl.pallas_call(pool_kernel, in_specs=[pl.BlockSpec(memory_space=pltpu.HBM...  4.05 us
  transfers between devices with their start and end apart: 22, of which 4 were waited for; matrix products, arithmetic and copies ran while one was open for 3% of the time, Pallas kernels for 19%

profile of v3, /device:TPU:1, one launch (start us, length us, event | category | flops | bytes accessed | tf_op | source)
XLA Modules:
  0.0 79.3 jit_solution(13122986946459156192)
XLA Ops:
  0.0 4.1 %pool.1.refs_0_ = bf16[192,1024]{1,0:T(8,128)(2,1)} custom-call(bf16[192,16,1024]{2,1,0:T(8,128)(2,1)} %bitcast.3), custom_call_target="tpu_custom_call" | custom-call | flops 6291456 | bytes 6291456 | tf_op jit(solution)/shard_map/pool/pallas_call | solution.py:61
  4.1 3.6 %collective-permute-start.2 = (bf16[192,1024]{1,0:T(8,128)(2,1)}, bf16[192,1024]{1,0:T(8,128)(2,1)S(1)}, u32[]{:S(2)}, u32[]{:S(2)}) collective-permute-start(bf16[192,1024]{1,0:T(8,128)(2,1)} %pool.1.refs_0_), channel_id=1, source_target_pairs={{0,24},{1,129},{2,26},{3,131},{4,28},{5,133},{6,30},{7,135},{8,0},... | collective-permute-start | bytes 1179656 | tf_op jit(solution)/shard_map/ppermute | solution.py:28
  7.7 2.9 %collective-permute-start = (bf16[192,1024]{1,0:T(8,128)(2,1)}, bf16[192,1024]{1,0:T(8,128)(2,1)S(1)}, u32[]{:S(2)}, u32[]{:S(2)}) collective-permute-start(bf16[192,1024]{1,0:T(8,128)(2,1)} %pool.1.refs_0_), channel_id=1, source_target_pairs={{0,8},{1,33},{2,10},{3,35},{4,12},{5,37},{6,14},{7,39},{8,16},{9,4... | collective-permute-start | bytes 1179656 | tf_op jit(solution)/shard_map/ppermute | solution.py:28
  10.6 1.2 %fusion = (s32[192]{0:T(256)S(1)}, s32[192]{0:T(256)S(1)}, s32[192]{0:T(256)S(1)}, s32[192]{0:T(256)S(1)}, s32[192]{0:T(256)S(1)}, /*index=5*/s32[192]{0:T(256)S...) fusion(s32[12288]{0:T(1024)} %param.5, ...), kind=kLoop, calls=%fused_computation.6 | loop fusion | bytes 24640 | tf_op jit(solution)/shard_map/dynamic_slice | solution.py:139
  12.1 0.3 broadcast_in_dim.22.row_ref
  12.4 0.4 collective-permute-start.4
  12.8 2.1 %collective-permute-start.6 = (bf16[192,1024]{1,0:T(8,128)(2,1)}, bf16[192,1024]{1,0:T(8,128)(2,1)S(1)}, u32[]{:S(2)}, u32[]{:S(2)}) collective-permute-start(bf16[192,1024]{1,0:T(8,128)(2,1)} %pool.1.refs_0_), channel_id=1, source_target_pairs={{0,1},{1,0},{2,3},{3,2},{4,5},{5,4},{6,7},{7,6},{8,9},{9,8},{10,11... | collective-permute-start | bytes 1179656 | tf_op jit(solution)/shard_map/ppermute | solution.py:32
  14.8 2.5 %collective-permute-start.5 = (bf16[192,1024]{1,0:T(8,128)(2,1)}, bf16[192,1024]{1,0:T(8,128)(2,1)}, u32[]{:S(2)}, u32[]{:S(2)}) collective-permute-start(bf16[192,1024]{1,0:T(8,128)(2,1)} %pool.1.refs_0_), channel_id=1, source_target_pairs={{0,28},{1,193},{2,30},{3,195},{4,0},{5,197},{6,2},{7,199},{8,4},{9... | collective-permute-start | bytes 1179656 | tf_op jit(solution)/shard_map/ppermute | solution.py:28
  17.3 3.2 %collective-permute-start.8 = (bf16[192,1024]{1,0:T(8,128)(2,1)S(1)}, bf16[192,1024]{1,0:T(8,128)(2,1)S(1)}, u32[]{:S(2)}, u32[]{:S(2)}) collective-permute-start(bf16[192,1024]{1,0:T(8,128)(2,1)S(1)} %collective-permute-done.2.refs_1_), channel_id=1, source_target_pairs={{0,1},{1,0},{2,3},{3,2},{4,5},{5,4},{6,7},{7,6},{8,9},{9,8},{10,11... | collective-permute-start | bytes 1179656 | tf_op jit(solution)/shard_map/ppermute | solution.py:32
  20.5 5.4 %collective-permute-start.7 = (bf16[192,1024]{1,0:T(8,128)(2,1)S(1)}, bf16[192,1024]{1,0:T(8,128)(2,1)S(1)}, u32[]{:S(2)}, u32[]{:S(2)}) collective-permute-start(bf16[192,1024]{1,0:T(8,128)(2,1)S(1)} %collective-permute-done.refs_0_), channel_id=1, source_target_pairs={{0,1},{1,0},{2,3},{3,2},{4,5},{5,4},{6,7},{7,6},{8,9},{9,8},{10,11... | collective-permute-start | bytes 1179656 | tf_op jit(solution)/shard_map/ppermute | solution.py:32
  25.8 4.3 %collective-permute-start.9 = (bf16[192,1024]{1,0:T(8,128)(2,1)}, bf16[192,1024]{1,0:T(8,128)(2,1)S(1)}, u32[]{:S(2)}, u32[]{:S(2)}) collective-permute-start(bf16[192,1024]{1,0:T(8,128)(2,1)} %collective-permute-done.4.refs_2_), channel_id=1, source_target_pairs={{0,1},{1,0},{2,3},{3,2},{4,5},{5,4},{6,7},{7,6},{8,9},{9,8},{10,11... | collective-permute-start | bytes 1179656 | tf_op jit(solution)/shard_map/ppermute | solution.py:32
  30.1 2.9 %collective-permute-start.3 = (bf16[192,1024]{1,0:T(8,128)(2,1)S(1)}, bf16[192,1024]{1,0:T(8,128)(2,1)S(1)}, u32[]{:S(2)}, u32[]{:S(2)}) collective-permute-start(bf16[192,1024]{1,0:T(8,128)(2,1)S(1)} %collective-permute-done.2.refs_1_), channel_id=1, source_target_pairs={{0,28},{1,33},{2,30},{3,35},{4,0},{5,37},{6,2},{7,39},{8,4},{9,41}... | collective-permute-start | bytes 1179656 | tf_op jit(solution)/shard_map/ppermute | solution.py:28
  33.0 1.2 %collective-permute-start.1 = (bf16[192,1024]{1,0:T(8,128)(2,1)S(1)}, bf16[192,1024]{1,0:T(8,128)(2,1)S(1)}, u32[]{:S(2)}, u32[]{:S(2)}) collective-permute-start(bf16[192,1024]{1,0:T(8,128)(2,1)S(1)} %collective-permute-done.refs_0_), channel_id=1, source_target_pairs={{0,4},{1,65},{2,6},{3,67},{4,8},{5,69},{6,10},{7,71},{8,12},{9,73}... | collective-permute-start | bytes 1179656 | tf_op jit(solution)/shard_map/ppermute | solution.py:28
  34.3 1.5 %collective-permute-start.10 = (bf16[192,1024]{1,0:T(8,128)(2,1)S(1)}, bf16[192,1024]{1,0:T(8,128)(2,1)S(1)}, u32[]{:S(2)}, u32[]{:S(2)}) collective-permute-start(bf16[192,1024]{1,0:T(8,128)(2,1)S(1)} %broadcast_select_fusion), channel_id=1, source_target_pairs={{0,8},{1,193},{2,10},{3,195},{4,28},{5,197},{6,30},{7,199},{8,16},... | collective-permute-start | bytes 1179656 | tf_op jit(solution)/shard_map/ppermute | solution.py:28
  35.9 4.5 %shard_map.46 = (f32[192,1024]{1,0:T(8,128)S(1)}, f32[192,1024]{1,0:T(8,128)S(1)}, f32[192,1024]{1,0:T(8,128)S(1)}, f32[192,1024]{1,0:T(8,128)S(1)}) custom-call(f32[4,768]{1,0:T(4,128)S(1)} %broadcast_in_dim.11.par_ref, s32[1536,128]{1,0:T(8,128)S(1)} %broadcast_in_dim.22.row_ref, s32[1,1536]{1,0:T(1,128)S(1)} %broadcast_in_dim.23.col_ref, ...), custom_call_target="tpu_custom_call" | custom-call | flops 2415919104 | bytes 1572864 | tf_op jit(solution)/shard_map/pallas_call | solution.py:102
  40.4 0.8 collective-permute-done.1.refs_0_.refs_1_
  41.2 2.7 %collective-permute-start.13 = (bf16[192,1024]{1,0:T(8,128)(2,1)S(1)}, bf16[192,1024]{1,0:T(8,128)(2,1)S(1)}, u32[]{:S(2)}, u32[]{:S(2)}) collective-permute-start(bf16[192,1024]{1,0:T(8,128)(2,1)S(1)} %collective-permute-done.3.refs_1_.refs_0_), channel_id=1, source_target_pairs={{0,1},{1,0},{2,3},{3,2},{4,5},{5,4},{6,7},{7,6},{8,9},{9,8},{10,11... | collective-permute-start | bytes 1179656 | tf_op jit(solution)/shard_map/ppermute | solution.py:32
  43.8 1.9 %shard_map.47 = (f32[192,1024]{1,0:T(8,128)S(1)}, f32[192,1024]{1,0:T(8,128)S(1)}) custom-call(f32[4,768]{1,0:T(4,128)S(1)} %broadcast_in_dim.11.par_ref, s32[1536,128]{1,0:T(8,128)S(1)} %broadcast_in_dim.22.row_ref, s32[1,1536]{1,0:T(1,128)S(1)} %broadcast_in_dim.23.col_ref, bf16[192,1024]{1,0:T(8,128)(2,1)S(1)} %collective-permute-done.1.refs_0_.refs_1_, ...), custom_call_target="tpu_custom_call" | custom-call | flops 1207959552 | bytes 1572864 | tf_op jit(solution)/shard_map/pallas_call | solution.py:102
  45.7 0.6 collective-permute-start.14
  46.3 1.2 %shard_map.48.refs_6_ = f32[192,1024]{1,0:T(8,128)S(1)} custom-call(f32[4,768]{1,0:T(4,128)S(1)} %broadcast_in_dim.11.par_ref, s32[1536,128]{1,0:T(8,128)S(1)} %broadcast_in_dim.22.row_ref, s32[1,1536]{1,0:T(1,128)S(1)} %broadcast_in_dim.23.col_ref, bf16[192,1024]{1,0:T(8,128)(2,1)S(1)} %collective-permute-done.10.refs_0_, ...), custom_call_target="tpu_custom_call" | custom-call | flops 603979776 | bytes 1572864 | tf_op jit(solution)/shard_map/pallas_call | solution.py:102
  47.7 1.9 %shard_map.49 = (bf16[192,1024]{1,0:T(8,128)(2,1)S(1)}, bf16[192,1024]{1,0:T(8,128)(2,1)S(1)}) custom-call(f32[4,768]{1,0:T(4,128)S(1)} %broadcast_in_dim.11.par_ref, s32[1536,128]{1,0:T(8,128)S(1)} %broadcast_in_dim.22.row_ref, s32[1,1536]{1,0:T(1,128)S(1)} %broadcast_in_dim.23.col_ref, bf16[192,1024]{1,0:T(8,128)(2,1)S(1)} %collective-permute-done.10.refs_0_, ...), custom_call_target="tpu_custom_call" | custom-call | flops 1207959552 | bytes 1572864 | tf_op jit(solution)/shard_map/pallas_call | solution.py:102
  49.5 2.6 %collective-permute-start.18 = (bf16[192,1024]{1,0:T(8,128)(2,1)S(1)}, bf16[192,1024]{1,0:T(8,128)(2,1)S(1)}, u32[]{:S(2)}, u32[]{:S(2)}) collective-permute-start(bf16[192,1024]{1,0:T(8,128)(2,1)S(1)} %get-tuple-element.72), channel_id=1, source_target_pairs={{0,28},{1,193},{2,30},{3,195},{4,0},{5,197},{6,2},{7,199},{8,4},{9... | collective-permute-start | bytes 1179656 | tf_op jit(solution)/shard_map/ppermute | solution.py:28
  52.1 1.2 %shard_map.50 = bf16[192,1024]{1,0:T(8,128)(2,1)S(1)} custom-call(f32[4,768]{1,0:T(4,128)S(1)} %broadcast_in_dim.11.par_ref, s32[1536,128]{1,0:T(8,128)S(1)} %broadcast_in_dim.22.row_ref, s32[1,1536]{1,0:T(1,128)S(1)} %broadcast_in_dim.23.col_ref, bf16[192,1024]{1,0:T(8,128)(2,1)S(1)} %collective-permute-done.3.refs_1_.refs_0_, ...), custom_call_target="tpu_custom_call" | custom-call | flops 603979776 | bytes 1572864 | tf_op jit(solution)/shard_map/pallas_call | solution.py:102
  53.3 3.2 %collective-permute-start.20 = (bf16[192,1024]{1,0:T(8,128)(2,1)S(1)}, bf16[192,1024]{1,0:T(8,128)(2,1)S(1)}, u32[]{:S(2)}, u32[]{:S(2)}) collective-permute-start(bf16[192,1024]{1,0:T(8,128)(2,1)S(1)} %shard_map.50), channel_id=1, source_target_pairs={{0,4},{1,33},{2,6},{3,35},{4,8},{5,37},{6,10},{7,39},{8,12},{9,41}... | collective-permute-start | bytes 1179656 | tf_op jit(solution)/shard_map/ppermute | solution.py:28
  56.5 4.5 %shard_map.51 = (f32[192,1024]{1,0:T(8,128)S(1)}, f32[192,1024]{1,0:T(8,128)S(1)}, bf16[192,1024]{1,0:T(8,128)(2,1)S(1)}, bf16[192,1024]{1,0:T(8,128)(2,1)S(1)}) custom-call(f32[4,768]{1,0:T(4,128)S(1)} %broadcast_in_dim.11.par_ref, s32[1536,128]{1,0:T(8,128)S(1)} %broadcast_in_dim.22.row_ref, s32[1,1536]{1,0:T(1,128)S(1)} %broadcast_in_dim.23.col_ref, ...), custom_call_target="tpu_custom_call" | custom-call | flops 2415919104 | bytes 1572864 | tf_op jit(solution)/shard_map/pallas_call | solution.py:102
  61.1 1.9 %shard_map.52 = f32[192,1024]{1,0:T(8,128)S(1)} custom-call(f32[4,768]{1,0:T(4,128)S(1)} %broadcast_in_dim.11.par_ref, s32[1536,128]{1,0:T(8,128)S(1)} %broadcast_in_dim.22.row_ref, s32[1,1536]{1,0:T(1,128)S(1)} %broadcast_in_dim.23.col_ref, bf16[192,1024]{1,0:T(8,128)(2,1)S(1)} %copy-done, ...), custom_call_target="tpu_custom_call" | custom-call | flops 1207959552 | bytes 1572864 | tf_op jit(solution)/shard_map/pallas_call | solution.py:102
  63.0 2.8 %collective-permute-start.15 = (bf16[192,1024]{1,0:T(8,128)(2,1)S(1)}, bf16[192,1024]{1,0:T(8,128)(2,1)S(1)}, u32[]{:S(2)}, u32[]{:S(2)}) collective-permute-start(bf16[192,1024]{1,0:T(8,128)(2,1)S(1)} %get-tuple-element.68), channel_id=1, source_target_pairs={{0,28},{1,193},{2,30},{3,195},{4,0},{5,197},{6,2},{7,199},{8,4},{9... | collective-permute-start | bytes 1179656 | tf_op jit(solution)/shard_map/ppermute | solution.py:28
  65.7 0.2 add_convert_fusion.1
  66.2 1.3 %collective-permute-start.21 = (bf16[192,1024]{1,0:T(8,128)(2,1)S(1)}, bf16[192,1024]{1,0:T(8,128)(2,1)S(1)}, u32[]{:S(2)}, u32[]{:S(2)}) collective-permute-start(bf16[192,1024]{1,0:T(8,128)(2,1)S(1)} %add_convert_fusion), channel_id=1, source_target_pairs={{0,8},{1,129},{2,10},{3,131},{4,12},{5,133},{6,14},{7,135},{8,16},... | collective-permute-start | bytes 1179656 | tf_op jit(solution)/shard_map/ppermute | solution.py:28
  67.6 7.1 %collective-permute-done.15 = bf16[192,1024]{1,0:T(8,128)(2,1)S(1)} collective-permute-done((bf16[192,1024]{1,0:T(8,128)(2,1)S(1)}, bf16[192,1024]{1,0:T(8,128)(2,1)S(1)}, u32[]{:S(2)}, u32[]{:S(2)}) %collective-permute-start.15) | collective-permute-done | bytes 393248 | tf_op jit(solution)/shard_map/ppermute | solution.py:28
  74.7 3.4 %collective-permute-done.16 = bf16[192,1024]{1,0:T(8,128)(2,1)S(1)} collective-permute-done((bf16[192,1024]{1,0:T(8,128)(2,1)S(1)}, bf16[192,1024]{1,0:T(8,128)(2,1)S(1)}, u32[]{:S(2)}, u32[]{:S(2)}) %collective-permute-start.16) | collective-permute-done | bytes 393248 | tf_op jit(solution)/shard_map/ppermute | solution.py:28
  78.3 1.0 %add_bitcast_fusion = f32[1,192,1024]{2,1,0:T(8,128)} fusion(bf16[192,1024]{1,0:T(8,128)(2,1)S(1)} %collective-permute-done.21, f32[192,1024]{1,0:T(8,128)S(1)} %convert_add_fusion, bf16[192,1024]{1,0:T(8,128)(2,1)S(1)} %collective-permute-done.19), kind=kLoop, calls=%fused_computation | loop fusion | flops 786432 | bytes 2359296 | tf_op jit(solution)/shard_map/reshape | solution.py:186
  (38 shorter events, 1.0 us)
Async XLA Ops:
  0.0 11.8 %copy-start.1 = (f32[2]{0:T(128)S(1)}, f32[2]{0:T(128)}, u32[]{:S(2)}) copy-start(f32[2]{0:T(128)} %param.7) | copy-start | bytes 28
  0.0 11.8 %copy-start.2 = (f32[2]{0:T(128)S(1)}, f32[2]{0:T(128)}, u32[]{:S(2)}) copy-start(f32[2]{0:T(128)} %param.6) | copy-start | bytes 28
  4.1 13.2 %collective-permute-start.2 = (bf16[192,1024]{1,0:T(8,128)(2,1)}, bf16[192,1024]{1,0:T(8,128)(2,1)S(1)}, u32[]{:S(2)}, u32[]{:S(2)}) collective-permute-start(bf16[192,1024]{1,0:T(8,128)(2,1)} %pool.1.refs_0_), channel_id=1, source_target_pairs={{0,24},{1,129},{2,26},{3,131},{4,28},{5,133},{6,30},{7,135},{8,0},... | collective-permute-start | bytes 1179656 | tf_op jit(solution)/shard_map/ppermute | solution.py:28
  7.7 12.8 %collective-permute-start = (bf16[192,1024]{1,0:T(8,128)(2,1)}, bf16[192,1024]{1,0:T(8,128)(2,1)S(1)}, u32[]{:S(2)}, u32[]{:S(2)}) collective-permute-start(bf16[192,1024]{1,0:T(8,128)(2,1)} %pool.1.refs_0_), channel_id=1, source_target_pairs={{0,8},{1,33},{2,10},{3,35},{4,12},{5,37},{6,14},{7,39},{8,16},{9,4... | collective-permute-start | bytes 1179656 | tf_op jit(solution)/shard_map/ppermute | solution.py:28
  12.4 13.5 %collective-permute-start.4 = (bf16[192,1024]{1,0:T(8,128)(2,1)}, bf16[192,1024]{1,0:T(8,128)(2,1)}, u32[]{:S(2)}, u32[]{:S(2)}) collective-permute-start(bf16[192,1024]{1,0:T(8,128)(2,1)} %pool.1.refs_0_), channel_id=1, source_target_pairs={{0,4},{1,65},{2,6},{3,67},{4,8},{5,69},{6,10},{7,71},{8,12},{9,73}... | collective-permute-start | bytes 1179656 | tf_op jit(solution)/shard_map/ppermute | solution.py:28
  12.8 17.4 %collective-permute-start.6 = (bf16[192,1024]{1,0:T(8,128)(2,1)}, bf16[192,1024]{1,0:T(8,128)(2,1)S(1)}, u32[]{:S(2)}, u32[]{:S(2)}) collective-permute-start(bf16[192,1024]{1,0:T(8,128)(2,1)} %pool.1.refs_0_), channel_id=1, source_target_pairs={{0,1},{1,0},{2,3},{3,2},{4,5},{5,4},{6,7},{7,6},{8,9},{9,8},{10,11... | collective-permute-start | bytes 1179656 | tf_op jit(solution)/shard_map/ppermute | solution.py:32
  14.8 18.2 %collective-permute-start.5 = (bf16[192,1024]{1,0:T(8,128)(2,1)}, bf16[192,1024]{1,0:T(8,128)(2,1)}, u32[]{:S(2)}, u32[]{:S(2)}) collective-permute-start(bf16[192,1024]{1,0:T(8,128)(2,1)} %pool.1.refs_0_), channel_id=1, source_target_pairs={{0,28},{1,193},{2,30},{3,195},{4,0},{5,197},{6,2},{7,199},{8,4},{9... | collective-permute-start | bytes 1179656 | tf_op jit(solution)/shard_map/ppermute | solution.py:28
  17.3 17.0 %collective-permute-start.8 = (bf16[192,1024]{1,0:T(8,128)(2,1)S(1)}, bf16[192,1024]{1,0:T(8,128)(2,1)S(1)}, u32[]{:S(2)}, u32[]{:S(2)}) collective-permute-start(bf16[192,1024]{1,0:T(8,128)(2,1)S(1)} %collective-permute-done.2.refs_1_), channel_id=1, source_target_pairs={{0,1},{1,0},{2,3},{3,2},{4,5},{5,4},{6,7},{7,6},{8,9},{9,8},{10,11... | collective-permute-start | bytes 1179656 | tf_op jit(solution)/shard_map/ppermute | solution.py:32
  20.5 15.4 %collective-permute-start.7 = (bf16[192,1024]{1,0:T(8,128)(2,1)S(1)}, bf16[192,1024]{1,0:T(8,128)(2,1)S(1)}, u32[]{:S(2)}, u32[]{:S(2)}) collective-permute-start(bf16[192,1024]{1,0:T(8,128)(2,1)S(1)} %collective-permute-done.refs_0_), channel_id=1, source_target_pairs={{0,1},{1,0},{2,3},{3,2},{4,5},{5,4},{6,7},{7,6},{8,9},{9,8},{10,11... | collective-permute-start | bytes 1179656 | tf_op jit(solution)/shard_map/ppermute | solution.py:32
  25.8 10.0 %collective-permute-start.9 = (bf16[192,1024]{1,0:T(8,128)(2,1)}, bf16[192,1024]{1,0:T(8,128)(2,1)S(1)}, u32[]{:S(2)}, u32[]{:S(2)}) collective-permute-start(bf16[192,1024]{1,0:T(8,128)(2,1)} %collective-permute-done.4.refs_2_), channel_id=1, source_target_pairs={{0,1},{1,0},{2,3},{3,2},{4,5},{5,4},{6,7},{7,6},{8,9},{9,8},{10,11... | collective-permute-start | bytes 1179656 | tf_op jit(solution)/shard_map/ppermute | solution.py:32
  30.1 10.3 %collective-permute-start.3 = (bf16[192,1024]{1,0:T(8,128)(2,1)S(1)}, bf16[192,1024]{1,0:T(8,128)(2,1)S(1)}, u32[]{:S(2)}, u32[]{:S(2)}) collective-permute-start(bf16[192,1024]{1,0:T(8,128)(2,1)S(1)} %collective-permute-done.2.refs_1_), channel_id=1, source_target_pairs={{0,28},{1,33},{2,30},{3,35},{4,0},{5,37},{6,2},{7,39},{8,4},{9,41}... | collective-permute-start | bytes 1179656 | tf_op jit(solution)/shard_map/ppermute | solution.py:28
  33.0 8.1 %collective-permute-start.1 = (bf16[192,1024]{1,0:T(8,128)(2,1)S(1)}, bf16[192,1024]{1,0:T(8,128)(2,1)S(1)}, u32[]{:S(2)}, u32[]{:S(2)}) collective-permute-start(bf16[192,1024]{1,0:T(8,128)(2,1)S(1)} %collective-permute-done.refs_0_), channel_id=1, source_target_pairs={{0,4},{1,65},{2,6},{3,67},{4,8},{5,69},{6,10},{7,71},{8,12},{9,73}... | collective-permute-start | bytes 1179656 | tf_op jit(solution)/shard_map/ppermute | solution.py:28
  34.3 11.4 %collective-permute-start.10 = (bf16[192,1024]{1,0:T(8,128)(2,1)S(1)}, bf16[192,1024]{1,0:T(8,128)(2,1)S(1)}, u32[]{:S(2)}, u32[]{:S(2)}) collective-permute-start(bf16[192,1024]{1,0:T(8,128)(2,1)S(1)} %broadcast_select_fusion), channel_id=1, source_target_pairs={{0,8},{1,193},{2,10},{3,195},{4,28},{5,197},{6,30},{7,199},{8,16},... | collective-permute-start | bytes 1179656 | tf_op jit(solution)/shard_map/ppermute | solution.py:28
  35.9 11.7 %collective-permute-start.11 = (bf16[192,1024]{1,0:T(8,128)(2,1)}, bf16[192,1024]{1,0:T(8,128)(2,1)S(1)}, u32[]{:S(2)}, u32[]{:S(2)}) collective-permute-start(bf16[192,1024]{1,0:T(8,128)(2,1)} %collective-permute-done.5.refs_3_), channel_id=1, source_target_pairs={{0,1},{1,0},{2,3},{3,2},{4,5},{5,4},{6,7},{7,6},{8,9},{9,8},{10,11... | collective-permute-start | bytes 1179656 | tf_op jit(solution)/shard_map/ppermute | solution.py:32
  41.2 6.4 %collective-permute-start.13 = (bf16[192,1024]{1,0:T(8,128)(2,1)S(1)}, bf16[192,1024]{1,0:T(8,128)(2,1)S(1)}, u32[]{:S(2)}, u32[]{:S(2)}) collective-permute-start(bf16[192,1024]{1,0:T(8,128)(2,1)S(1)} %collective-permute-done.3.refs_1_.refs_0_), channel_id=1, source_target_pairs={{0,1},{1,0},{2,3},{3,2},{4,5},{5,4},{6,7},{7,6},{8,9},{9,8},{10,11... | collective-permute-start | bytes 1179656 | tf_op jit(solution)/shard_map/ppermute | solution.py:32
  43.8 3.7 %collective-permute-start.12 = (bf16[192,1024]{1,0:T(8,128)(2,1)S(1)}, bf16[192,1024]{1,0:T(8,128)(2,1)S(1)}, u32[]{:S(2)}, u32[]{:S(2)}) collective-permute-start(bf16[192,1024]{1,0:T(8,128)(2,1)S(1)} %collective-permute-done.1.refs_0_.refs_1_), channel_id=1, source_target_pairs={{0,1},{1,0},{2,3},{3,2},{4,5},{5,4},{6,7},{7,6},{8,9},{9,8},{10,11... | collective-permute-start | bytes 1179656 | tf_op jit(solution)/shard_map/ppermute | solution.py:32
  45.7 1.9 %collective-permute-start.14 = (bf16[192,1024]{1,0:T(8,128)(2,1)S(1)}, bf16[192,1024]{1,0:T(8,128)(2,1)S(1)}, u32[]{:S(2)}, u32[]{:S(2)}) collective-permute-start(bf16[192,1024]{1,0:T(8,128)(2,1)S(1)} %collective-permute-done.10.refs_0_), channel_id=1, source_target_pairs={{0,1},{1,0},{2,3},{3,2},{4,5},{5,4},{6,7},{7,6},{8,9},{9,8},{10,11... | collective-permute-start | bytes 1179656 | tf_op jit(solution)/shard_map/ppermute | solution.py:32
  49.5 16.2 %collective-permute-start.18 = (bf16[192,1024]{1,0:T(8,128)(2,1)S(1)}, bf16[192,1024]{1,0:T(8,128)(2,1)S(1)}, u32[]{:S(2)}, u32[]{:S(2)}) collective-permute-start(bf16[192,1024]{1,0:T(8,128)(2,1)S(1)} %get-tuple-element.72), channel_id=1, source_target_pairs={{0,28},{1,193},{2,30},{3,195},{4,0},{5,197},{6,2},{7,199},{8,4},{9... | collective-permute-start | bytes 1179656 | tf_op jit(solution)/shard_map/ppermute | solution.py:28
  52.1 9.0 %copy-start = (bf16[192,1024]{1,0:T(8,128)(2,1)S(1)}, bf16[192,1024]{1,0:T(8,128)(2,1)}, u32[]{:S(2)}) copy-start(bf16[192,1024]{1,0:T(8,128)(2,1)} %pool.1.refs_0_) | copy-start | bytes 1179652
  52.1 13.6 %collective-permute-start.17 = (bf16[192,1024]{1,0:T(8,128)(2,1)S(1)}, bf16[192,1024]{1,0:T(8,128)(2,1)S(1)}, u32[]{:S(2)}, u32[]{:S(2)}) collective-permute-start(bf16[192,1024]{1,0:T(8,128)(2,1)S(1)} %get-tuple-element.71), channel_id=1, source_target_pairs={{0,24},{1,65},{2,26},{3,67},{4,12},{5,69},{6,14},{7,71},{8,0},{9,7... | collective-permute-start | bytes 1179656 | tf_op jit(solution)/shard_map/ppermute | solution.py:28
  53.3 12.7 %collective-permute-start.20 = (bf16[192,1024]{1,0:T(8,128)(2,1)S(1)}, bf16[192,1024]{1,0:T(8,128)(2,1)S(1)}, u32[]{:S(2)}, u32[]{:S(2)}) collective-permute-start(bf16[192,1024]{1,0:T(8,128)(2,1)S(1)} %shard_map.50), channel_id=1, source_target_pairs={{0,4},{1,33},{2,6},{3,35},{4,8},{5,37},{6,10},{7,39},{8,12},{9,41}... | collective-permute-start | bytes 1179656 | tf_op jit(solution)/shard_map/ppermute | solution.py:28
  63.0 11.7 %collective-permute-start.15 = (bf16[192,1024]{1,0:T(8,128)(2,1)S(1)}, bf16[192,1024]{1,0:T(8,128)(2,1)S(1)}, u32[]{:S(2)}, u32[]{:S(2)}) collective-permute-start(bf16[192,1024]{1,0:T(8,128)(2,1)S(1)} %get-tuple-element.68), channel_id=1, source_target_pairs={{0,28},{1,193},{2,30},{3,195},{4,0},{5,197},{6,2},{7,199},{8,4},{9... | collective-permute-start | bytes 1179656 | tf_op jit(solution)/shard_map/ppermute | solution.py:28
  65.7 12.3 %collective-permute-start.16 = (bf16[192,1024]{1,0:T(8,128)(2,1)S(1)}, bf16[192,1024]{1,0:T(8,128)(2,1)S(1)}, u32[]{:S(2)}, u32[]{:S(2)}) collective-permute-start(bf16[192,1024]{1,0:T(8,128)(2,1)S(1)} %get-tuple-element.69), channel_id=1, source_target_pairs={{0,4},{1,65},{2,6},{3,67},{4,8},{5,69},{6,10},{7,71},{8,12},{9,73}... | collective-permute-start | bytes 1179656 | tf_op jit(solution)/shard_map/ppermute | solution.py:28
  65.9 12.3 %collective-permute-start.19 = (bf16[192,1024]{1,0:T(8,128)(2,1)S(1)}, bf16[192,1024]{1,0:T(8,128)(2,1)S(1)}, u32[]{:S(2)}, u32[]{:S(2)}) collective-permute-start(bf16[192,1024]{1,0:T(8,128)(2,1)S(1)} %add_convert_fusion.1), channel_id=1, source_target_pairs={{0,24},{1,33},{2,26},{3,35},{4,28},{5,37},{6,30},{7,39},{8,0},{9,4... | collective-permute-start | bytes 1179656 | tf_op jit(solution)/shard_map/ppermute | solution.py:28
  66.2 12.0 %collective-permute-start.21 = (bf16[192,1024]{1,0:T(8,128)(2,1)S(1)}, bf16[192,1024]{1,0:T(8,128)(2,1)S(1)}, u32[]{:S(2)}, u32[]{:S(2)}) collective-permute-start(bf16[192,1024]{1,0:T(8,128)(2,1)S(1)} %add_convert_fusion), channel_id=1, source_target_pairs={{0,8},{1,129},{2,10},{3,131},{4,12},{5,133},{6,14},{7,135},{8,16},... | collective-permute-start | bytes 1179656 | tf_op jit(solution)/shard_map/ppermute | solution.py:28

commit v4 on v2

--- a/solution.py
+++ b/solution.py
@@ -16,15 +16,15 @@
     return (((x % NX) * NYH + yh % NYH) * NZ + z % NZ) * 4 + yl * 2 + c
 
 
-def send(v, ways):
+def send(v, ways, back=False):
     pairs = []
     for x in range(NX):
         for yh in range(NYH):
             for z in range(NZ):
                 for yl in range(NYL):
-                    for c, way in enumerate(ways):
-                        dx, dy, dz = way(z) if callable(way) else way
-                        pairs.append((flat(x, yh, z, yl, c), flat(x + dx, yh + dy, z + dz, yl, c)))
+                    for c, (dx, dy, dz) in enumerate((ways[0](z), ways[1])):
+                        pair = flat(x, yh, z, yl, c), flat(x + dx, yh + dy, z + dz, yl, c)
+                        pairs.append(pair[::-1] if back else pair)
     return lax.ppermute(v, AXES, pairs)
 
 
@@ -109,15 +109,16 @@
     )(par, row_ids, col_ids, *operands)
 
 
+def along_z(even, odd):
+    return lambda z: (0, 0, odd if z % 2 else even)
+
+
 MOVES = {
-    1: ((0, 0, 2), (0, 1, 0)), 2: ((0, 0, -2), (2, 0, 0)), 3: ((0, 0, 1), (1, 0, 0)), 4: ((0, 0, -1), (-1, 0, 0)),
-    5: ((0, 0, 1), (1, 0, 0)), 6: ((0, 0, -1), (0, 1, 0)), 7: (lambda z: (0, 0, -2 if z % 2 else 2), (-1, 0, 0)),
+    1: (along_z(2, -2), (0, 1, 0)), 2: (along_z(-2, 2), (2, 0, 0)), 3: (along_z(1, 1), (1, 0, 0)), 4: (along_z(-1, -1), (-1, 0, 0)),
+    5: (along_z(1, -1), (1, 0, 0)), 6: (along_z(-1, 1), (0, 1, 0)), 7: (along_z(2, -2), (-1, 0, 0)),
 }
-BACK = {
-    k: tuple(((lambda z, way=way: tuple(-d for d in way(z))) if callable(way) else tuple(-d for d in way)) for way in ways)
-    for k, ways in MOVES.items()
-}
-Z_OFF = (0, -2, 2, -1, 1, -3, 3, -4)
+Z_EVEN = (0, -2, 2, -1, 1, 3, -3, 4)
+Z_ODD = (0, 2, -2, -1, 1, -3, 3, 4)
 X_OFF = (0, 0, 2, -1, 1, -1, 2, 1)
 Y_OFF = (0, 1, 0, 0, 0, 1, 1, 1)
 
@@ -133,8 +134,8 @@
 
     def ids(on_first):
         parts = []
-        for zo, xo, yo in zip(Z_OFF, X_OFF, Y_OFF):
-            on_z = (x * NYH + yh) * NZ + (z + zo) % NZ
+        for even, odd, xo, yo in zip(Z_EVEN, Z_ODD, X_OFF, Y_OFF):
+            on_z = (x * NYH + yh) * NZ + (z + jnp.where(z % 2 == 0, even, odd)) % NZ
             on_xy = (((x + xo) % NX) * NYH + (yh + yo) % NYH) * NZ + z
             parts.append(lax.dynamic_slice_in_dim(subject_ids, jnp.where(on_first, on_z, on_xy) * n, n, 0))
         return jnp.concatenate(parts)
@@ -150,8 +151,7 @@
     rows[3] = send(later, MOVES[3])
     rows[4] = send(later, MOVES[4])
     rows[5] = send(rows[1], MOVES[5])
-    turn = jnp.logical_and(first, z % 2 == 1)
-    rows[7] = send(jnp.where(turn, rows[2], rows[1]), MOVES[7])
+    rows[7] = send(rows[1], MOVES[7])
     rows[6] = send(rows[2], MOVES[6])
     cols = [partner(v) for v in rows[:5]]
     state = (par, row_ids, col_ids, rows, cols)
@@ -161,18 +161,17 @@
     cols += [partner(rows[k]) for k in (5, 6, 7)]
     h7, h5, h6 = grads(state, (7, 5, 6), 0, 1, None, (f32,) * 3)
     g7, g5, g6 = grads(state, (7, 5, 6), 4, 1, (h7, h5, h6), (bf16,) * 3)
-    r7 = send(g7, BACK[7])
-    r5 = send(g5, BACK[5])
-    r6 = send(g6, BACK[6])
+    r7 = send(g7, MOVES[7], True)
+    r5 = send(g5, MOVES[5], True)
+    r6 = send(g6, MOVES[6], True)
     rows[1], g6 = lax.optimization_barrier((rows[1], g6))
     g1, g2, g3, g4 = grads(state, (1, 2, 3, 4), 4, 1, (h1, h2, h3, h4), (f32, f32, bf16, bf16))
-    r3 = send(g3, BACK[3])
-    r4 = send(g4, BACK[4])
-    s1 = (g1 + jnp.where(turn, 0.0, r7.astype(f32)) + r5.astype(f32)).astype(bf16)
-    s1, r7 = lax.optimization_barrier((s1, r7))
-    r1 = send(s1, BACK[1])
-    s2 = (g2 + jnp.where(turn, r7.astype(f32), 0.0) + r6.astype(f32)).astype(bf16)
-    r2 = send(s2, BACK[2])
+    r3 = send(g3, MOVES[3], True)
+    r4 = send(g4, MOVES[4], True)
+    s1 = (g1 + r7.astype(f32) + r5.astype(f32)).astype(bf16)
+    r1 = send(s1, MOVES[1], True)
+    s2 = (g2 + r6.astype(f32)).astype(bf16)
+    r2 = send(s2, MOVES[2], True)
     rows[0], s2 = lax.optimization_barrier((rows[0], s2))
     (g0,) = grads(state, (0,), 4, 1, (h0,), (f32,))
     near = lax.optimization_barrier(g0 + r3.astype(f32) + r4.astype(f32))

time: 77.8 us -> 78.1 us (level)
  Pallas kernels: 22.2 us -> 18.5 us
  waiting for transfers between devices: 24.3 us -> 26.5 us
  local copies, waits for them, and re-layouts: 1.85 us -> 2.84 us
  starting transfers between devices: 27.4 us -> 28.3 us
    pallas_call x6, Pallas kernels: 18.1 us -> 14.5 us  [grads(): pl.pallas_call(functools.partial(grad_kernel, slots, first_col, groups, s...]
    ppermute x14, waiting for transfers between devices: 24.2 us -> 26.5 us  [send(): return lax.ppermute(v, AXES, pairs)]
    unnamed x6 -> x8, local copies, waits for them, and re-layouts: 0.01 us -> 1 us
    ppermute x14, starting transfers between devices: 26.3 us -> 27.3 us  [send(): return lax.ppermute(v, AXES, pairs)]
  transfers between devices with their start and end apart: 22 -> 22, of which waited for: 8 -> 9; matrix products, arithmetic and copies ran while one was open for 1% -> 1% of each run, Pallas kernels for 20% -> 15%
where the time goes in v4:
time: 78.1 us; the launch traced here: 78 us
  starting transfers between devices  28.3 us (36%)
  waiting for transfers between devices  26.5 us (34%)
  Pallas kernels  18.5 us (24%)
  local copies, waits for them, and re-layouts  2.84 us (4%)
  other arithmetic  1.55 us (2%)
    ppermute x14, starting transfers between devices, send(): return lax.ppermute(v, AXES, pairs)  27.3 us
    ppermute x14, waiting for transfers between devices, send(): return lax.ppermute(v, AXES, pairs)  26.5 us
    pallas_call x6, Pallas kernels, grads(): pl.pallas_call(functools.partial(grad_kernel, slots, first_col, groups, s...  14.5 us
    pallas_call x1, Pallas kernels, pool(): pl.pallas_call(pool_kernel, in_specs=[pl.BlockSpec(memory_space=pltpu.HBM...  4.03 us
  transfers between devices with their start and end apart: 22, of which 9 were waited for; matrix products, arithmetic and copies ran while one was open for 1% of the time, Pallas kernels for 15%

profile of v4, /device:TPU:28, one launch (start us, length us, event | category | flops | bytes accessed | tf_op | source)
XLA Modules:
  0.0 78.0 jit_solution(16685096150545630231)
XLA Ops:
  0.0 1.3 %fusion = (s32[192]{0:T(256)S(1)}, s32[192]{0:T(256)S(1)}, s32[192]{0:T(256)S(1)}, s32[192]{0:T(256)S(1)}, s32[192]{0:T(256)S(1)}, /*index=5*/s32[192]{0:T(256)S...) fusion(s32[12288]{0:T(1024)} %param.5, ...), kind=kLoop, calls=%fused_computation.5 | loop fusion | bytes 24640 | tf_op jit(solution)/shard_map/dynamic_slice | solution.py:140
  1.4 4.0 %pool.1.refs_0_ = bf16[192,1024]{1,0:T(8,128)(2,1)} custom-call(bf16[192,16,1024]{2,1,0:T(8,128)(2,1)} %bitcast.3), custom_call_target="tpu_custom_call" | custom-call | flops 6291456 | bytes 6291456 | tf_op jit(solution)/shard_map/pool/pallas_call | solution.py:61
  6.0 1.9 %collective-permute-start.5 = (bf16[192,1024]{1,0:T(8,128)(2,1)}, bf16[192,1024]{1,0:T(8,128)(2,1)S(1)}, u32[]{:S(2)}, u32[]{:S(2)}) collective-permute-start(bf16[192,1024]{1,0:T(8,128)(2,1)} %pool.1.refs_0_), channel_id=1, source_target_pairs={{0,4},{1,65},{2,6},{3,67},{4,8},{5,69},{6,10},{7,71},{8,12},{9,73}... | collective-permute-start | bytes 1179656 | tf_op jit(solution)/shard_map/ppermute | solution.py:28
  7.9 3.2 %collective-permute-start = (bf16[192,1024]{1,0:T(8,128)(2,1)}, bf16[192,1024]{1,0:T(8,128)(2,1)S(1)}, u32[]{:S(2)}, u32[]{:S(2)}) collective-permute-start(bf16[192,1024]{1,0:T(8,128)(2,1)} %pool.1.refs_0_), channel_id=1, source_target_pairs={{0,8},{1,33},{2,10},{3,35},{4,28},{5,37},{6,30},{7,39},{8,16},{9,4... | collective-permute-start | bytes 1179656 | tf_op jit(solution)/shard_map/ppermute | solution.py:28
  11.2 2.2 %collective-permute-start.2 = (bf16[192,1024]{1,0:T(8,128)(2,1)}, bf16[192,1024]{1,0:T(8,128)(2,1)S(1)}, u32[]{:S(2)}, u32[]{:S(2)}) collective-permute-start(bf16[192,1024]{1,0:T(8,128)(2,1)} %pool.1.refs_0_), channel_id=1, source_target_pairs={{0,24},{1,129},{2,26},{3,131},{4,12},{5,133},{6,14},{7,135},{8,0},... | collective-permute-start | bytes 1179656 | tf_op jit(solution)/shard_map/ppermute | solution.py:28
  13.3 2.8 %collective-permute-start.6 = (bf16[192,1024]{1,0:T(8,128)(2,1)}, bf16[192,1024]{1,0:T(8,128)(2,1)S(1)}, u32[]{:S(2)}, u32[]{:S(2)}) collective-permute-start(bf16[192,1024]{1,0:T(8,128)(2,1)} %pool.1.refs_0_), channel_id=1, source_target_pairs={{0,28},{1,193},{2,30},{3,195},{4,0},{5,197},{6,2},{7,199},{8,4},{9... | collective-permute-start | bytes 1179656 | tf_op jit(solution)/shard_map/ppermute | solution.py:28
  16.1 1.7 %collective-permute-done.5.refs_1_.refs_2_ = bf16[192,1024]{1,0:T(8,128)(2,1)S(1)} collective-permute-done((bf16[192,1024]{1,0:T(8,128)(2,1)}, bf16[192,1024]{1,0:T(8,128)(2,1)S(1)}, u32[]{:S(2)}, u32[]{:S(2)}) %collective-permute-start.5) | collective-permute-done | bytes 393248 | tf_op jit(solution)/shard_map/ppermute | solution.py:28
  17.8 6.2 %collective-permute-done.refs_0_ = bf16[192,1024]{1,0:T(8,128)(2,1)S(1)} collective-permute-done((bf16[192,1024]{1,0:T(8,128)(2,1)}, bf16[192,1024]{1,0:T(8,128)(2,1)S(1)}, u32[]{:S(2)}, u32[]{:S(2)}) %collective-permute-start) | collective-permute-done | bytes 393248 | tf_op jit(solution)/shard_map/ppermute | solution.py:28
  24.0 0.5 collective-permute-start.9
  24.5 3.2 %collective-permute-start.1 = (bf16[192,1024]{1,0:T(8,128)(2,1)S(1)}, bf16[192,1024]{1,0:T(8,128)(2,1)S(1)}, u32[]{:S(2)}, u32[]{:S(2)}) collective-permute-start(bf16[192,1024]{1,0:T(8,128)(2,1)S(1)} %collective-permute-done.refs_0_), channel_id=1, source_target_pairs={{0,4},{1,65},{2,6},{3,67},{4,0},{5,69},{6,2},{7,71},{8,12},{9,73},... | collective-permute-start | bytes 1179656 | tf_op jit(solution)/shard_map/ppermute | solution.py:28
  27.8 1.4 %collective-permute-start.4 = (bf16[192,1024]{1,0:T(8,128)(2,1)S(1)}, bf16[192,1024]{1,0:T(8,128)(2,1)S(1)}, u32[]{:S(2)}, u32[]{:S(2)}) collective-permute-start(bf16[192,1024]{1,0:T(8,128)(2,1)S(1)} %collective-permute-done.refs_0_), channel_id=1, source_target_pairs={{0,8},{1,193},{2,10},{3,195},{4,28},{5,197},{6,30},{7,199},{8,16},... | collective-permute-start | bytes 1179656 | tf_op jit(solution)/shard_map/ppermute | solution.py:28
  29.2 2.5 %collective-permute-start.3 = (bf16[192,1024]{1,0:T(8,128)(2,1)S(1)}, bf16[192,1024]{1,0:T(8,128)(2,1)S(1)}, u32[]{:S(2)}, u32[]{:S(2)}) collective-permute-start(bf16[192,1024]{1,0:T(8,128)(2,1)S(1)} %collective-permute-done.2.refs_1_), channel_id=1, source_target_pairs={{0,28},{1,33},{2,30},{3,35},{4,8},{5,37},{6,10},{7,39},{8,4},{9,41... | collective-permute-start | bytes 1179656 | tf_op jit(solution)/shard_map/ppermute | solution.py:28
  31.7 1.9 %shard_map.47 = (f32[192,1024]{1,0:T(8,128)S(1)}, f32[192,1024]{1,0:T(8,128)S(1)}) custom-call(f32[4,768]{1,0:T(4,128)S(1)} %broadcast_in_dim.6.par_ref, s32[1536,128]{1,0:T(8,128)S(1)} %broadcast_in_dim.7.row_ref, s32[1,1536]{1,0:T(1,128)S(1)} %broadcast_in_dim.8.col_ref, bf16[192,1024]{1,0:T(8,128)(2,1)S(1)} %collective-permute-done.refs_0_, ...), custom_call_target="tpu_custom_call" | custom-call | flops 1207959552 | bytes 1572864 | tf_op jit(solution)/shard_map/pallas_call | solution.py:102
  33.6 1.0 %copy-done = bf16[192,1024]{1,0:T(8,128)(2,1)S(1)} copy-done((bf16[192,1024]{1,0:T(8,128)(2,1)S(1)}, bf16[192,1024]{1,0:T(8,128)(2,1)}, u32[]{:S(2)}) %copy-start) | copy-done | bytes 393240
  34.6 2.6 %shard_map.46 = (f32[192,1024]{1,0:T(8,128)S(1)}, f32[192,1024]{1,0:T(8,128)S(1)}, f32[192,1024]{1,0:T(8,128)S(1)}) custom-call(f32[4,768]{1,0:T(4,128)S(1)} %broadcast_in_dim.6.par_ref, s32[1536,128]{1,0:T(8,128)S(1)} %broadcast_in_dim.7.row_ref, s32[1,1536]{1,0:T(1,128)S(1)} %broadcast_in_dim.8.col_ref, bf16[192,1024]{1,0:T(8,128)(2,1)S(1)} %copy-done, ...), custom_call_target="tpu_custom_call" | custom-call | flops 1811939328 | bytes 1572864 | tf_op jit(solution)/shard_map/pallas_call | solution.py:102
  37.3 3.0 %collective-permute-done.4.refs_0_ = bf16[192,1024]{1,0:T(8,128)(2,1)S(1)} collective-permute-done((bf16[192,1024]{1,0:T(8,128)(2,1)S(1)}, bf16[192,1024]{1,0:T(8,128)(2,1)S(1)}, u32[]{:S(2)}, u32[]{:S(2)}) %collective-permute-start.4) | collective-permute-done | bytes 393248 | tf_op jit(solution)/shard_map/ppermute | solution.py:28
  40.3 2.2 %collective-permute-done.3.refs_2_ = bf16[192,1024]{1,0:T(8,128)(2,1)S(1)} collective-permute-done((bf16[192,1024]{1,0:T(8,128)(2,1)S(1)}, bf16[192,1024]{1,0:T(8,128)(2,1)S(1)}, u32[]{:S(2)}, u32[]{:S(2)}) %collective-permute-start.3) | collective-permute-done | bytes 393248 | tf_op jit(solution)/shard_map/ppermute | solution.py:28
  42.4 0.5 collective-permute-start.13
  43.0 2.6 %shard_map.48 = (f32[192,1024]{1,0:T(8,128)S(1)}, f32[192,1024]{1,0:T(8,128)S(1)}, f32[192,1024]{1,0:T(8,128)S(1)}) custom-call(f32[4,768]{1,0:T(4,128)S(1)} %broadcast_in_dim.6.par_ref, s32[1536,128]{1,0:T(8,128)S(1)} %broadcast_in_dim.7.row_ref, s32[1,1536]{1,0:T(1,128)S(1)} %broadcast_in_dim.8.col_ref, ...), custom_call_target="tpu_custom_call" | custom-call | flops 1811939328 | bytes 1572864 | tf_op jit(solution)/shard_map/pallas_call | solution.py:102
  45.6 2.7 %shard_map.49 = (bf16[192,1024]{1,0:T(8,128)(2,1)S(1)}, bf16[192,1024]{1,0:T(8,128)(2,1)S(1)}, bf16[192,1024]{1,0:T(8,128)(2,1)S(1)}) custom-call(f32[4,768]{1,0:T(4,128)S(1)} %broadcast_in_dim.6.par_ref, s32[1536,128]{1,0:T(8,128)S(1)} %broadcast_in_dim.7.row_ref, s32[1,1536]{1,0:T(1,128)S(1)} %broadcast_in_dim.8.col_ref, ...), custom_call_target="tpu_custom_call" | custom-call | flops 1811939328 | bytes 1572864 | tf_op jit(solution)/shard_map/pallas_call | solution.py:102
  48.3 3.2 %collective-permute-start.18 = (bf16[192,1024]{1,0:T(8,128)(2,1)S(1)}, bf16[192,1024]{1,0:T(8,128)(2,1)S(1)}, u32[]{:S(2)}, u32[]{:S(2)}) collective-permute-start(bf16[192,1024]{1,0:T(8,128)(2,1)S(1)} %get-tuple-element.61), channel_id=1, source_target_pairs={{8,0},{193,1},{10,2},{195,3},{28,4},{197,5},{30,6},{199,7},{16,8},... | collective-permute-start | bytes 1179656 | tf_op jit(solution)/shard_map/ppermute | solution.py:28
  51.5 0.6 collective-permute-start.19
  52.1 0.8 %collective-permute-start.15 = (bf16[192,1024]{1,0:T(8,128)(2,1)S(1)}, bf16[192,1024]{1,0:T(8,128)(2,1)S(1)}, u32[]{:S(2)}, u32[]{:S(2)}) collective-permute-start(bf16[192,1024]{1,0:T(8,128)(2,1)S(1)} %get-tuple-element.49), channel_id=1, source_target_pairs={{28,0},{33,1},{30,2},{35,3},{8,4},{37,5},{10,6},{39,7},{4,8},{41,9... | collective-permute-start | bytes 1179656 | tf_op jit(solution)/shard_map/ppermute | solution.py:28
  52.9 3.4 %shard_map.50 = (f32[192,1024]{1,0:T(8,128)S(1)}, f32[192,1024]{1,0:T(8,128)S(1)}, bf16[192,1024]{1,0:T(8,128)(2,1)S(1)}, bf16[192,1024]{1,0:T(8,128)(2,1)S(1)}) custom-call(f32[4,768]{1,0:T(4,128)S(1)} %broadcast_in_dim.6.par_ref, s32[1536,128]{1,0:T(8,128)S(1)} %broadcast_in_dim.7.row_ref, s32[1,1536]{1,0:T(1,128)S(1)} %broadcast_in_dim.8.col_ref, ...), custom_call_target="tpu_custom_call" | custom-call | flops 2415919104 | bytes 1572864 | tf_op jit(solution)/shard_map/pallas_call | solution.py:102
  56.3 2.5 %collective-permute-start.16 = (bf16[192,1024]{1,0:T(8,128)(2,1)S(1)}, bf16[192,1024]{1,0:T(8,128)(2,1)S(1)}, u32[]{:S(2)}, u32[]{:S(2)}) collective-permute-start(bf16[192,1024]{1,0:T(8,128)(2,1)S(1)} %get-tuple-element.58), channel_id=1, source_target_pairs={{4,0},{65,1},{6,2},{67,3},{8,4},{69,5},{10,6},{71,7},{12,8},{73,9}... | collective-permute-start | bytes 1179656 | tf_op jit(solution)/shard_map/ppermute | solution.py:28
  58.8 2.7 %collective-permute-done.19 = bf16[192,1024]{1,0:T(8,128)(2,1)S(1)} collective-permute-done((bf16[192,1024]{1,0:T(8,128)(2,1)S(1)}, bf16[192,1024]{1,0:T(8,128)(2,1)S(1)}, u32[]{:S(2)}, u32[]{:S(2)}) %collective-permute-start.19) | collective-permute-done | bytes 393248 | tf_op jit(solution)/shard_map/ppermute | solution.py:28
  61.8 2.8 %collective-permute-start.20 = (bf16[192,1024]{1,0:T(8,128)(2,1)S(1)}, bf16[192,1024]{1,0:T(8,128)(2,1)S(1)}, u32[]{:S(2)}, u32[]{:S(2)}) collective-permute-start(bf16[192,1024]{1,0:T(8,128)(2,1)S(1)} %add_convert_fusion), channel_id=1, source_target_pairs={{8,0},{33,1},{10,2},{35,3},{28,4},{37,5},{30,6},{39,7},{16,8},{41,... | collective-permute-start | bytes 1179656 | tf_op jit(solution)/shard_map/ppermute | solution.py:28
  65.0 1.2 %shard_map.51 = f32[192,1024]{1,0:T(8,128)S(1)} custom-call(f32[4,768]{1,0:T(4,128)S(1)} %broadcast_in_dim.6.par_ref, s32[1536,128]{1,0:T(8,128)S(1)} %broadcast_in_dim.7.row_ref, s32[1,1536]{1,0:T(1,128)S(1)} %broadcast_in_dim.8.col_ref, bf16[192,1024]{1,0:T(8,128)(2,1)S(1)} %copy-done.1, ...), custom_call_target="tpu_custom_call" | custom-call | flops 603979776 | bytes 1572864 | tf_op jit(solution)/shard_map/pallas_call | solution.py:102
  66.2 1.6 %collective-permute-done.17 = bf16[192,1024]{1,0:T(8,128)(2,1)S(1)} collective-permute-done((bf16[192,1024]{1,0:T(8,128)(2,1)S(1)}, bf16[192,1024]{1,0:T(8,128)(2,1)S(1)}, u32[]{:S(2)}, u32[]{:S(2)}) %collective-permute-start.17) | collective-permute-done | bytes 393248 | tf_op jit(solution)/shard_map/ppermute | solution.py:28
  68.0 6.2 %collective-permute-done.20 = bf16[192,1024]{1,0:T(8,128)(2,1)S(1)} collective-permute-done((bf16[192,1024]{1,0:T(8,128)(2,1)S(1)}, bf16[192,1024]{1,0:T(8,128)(2,1)S(1)}, u32[]{:S(2)}, u32[]{:S(2)}) %collective-permute-start.20) | collective-permute-done | bytes 393248 | tf_op jit(solution)/shard_map/ppermute | solution.py:28
  74.1 2.8 %collective-permute-done.21 = bf16[192,1024]{1,0:T(8,128)(2,1)S(1)} collective-permute-done((bf16[192,1024]{1,0:T(8,128)(2,1)S(1)}, bf16[192,1024]{1,0:T(8,128)(2,1)S(1)}, u32[]{:S(2)}, u32[]{:S(2)}) %collective-permute-start.21) | collective-permute-done | bytes 393248 | tf_op jit(solution)/shard_map/ppermute | solution.py:28
  76.9 1.1 %add_bitcast_fusion = f32[1,192,1024]{2,1,0:T(8,128)} fusion(bf16[192,1024]{1,0:T(8,128)(2,1)S(1)} %collective-permute-done.21, f32[192,1024]{1,0:T(8,128)S(1)} %convert_add_fusion, bf16[192,1024]{1,0:T(8,128)(2,1)S(1)} %collective-permute-done.20), kind=kLoop, calls=%fused_computation | loop fusion | flops 786432 | bytes 2359296 | tf_op jit(solution)/shard_map/reshape | solution.py:179
  (38 shorter events, 1.4 us)
Async XLA Ops:
  0.0 5.5 %copy-start.3 = (f32[2]{0:T(128)S(1)}, f32[2]{0:T(128)}, u32[]{:S(2)}) copy-start(f32[2]{0:T(128)} %param.6) | copy-start | bytes 28
  0.0 5.5 %copy-start.2 = (f32[2]{0:T(128)S(1)}, f32[2]{0:T(128)}, u32[]{:S(2)}) copy-start(f32[2]{0:T(128)} %param.7) | copy-start | bytes 28
  6.0 11.8 %collective-permute-start.5 = (bf16[192,1024]{1,0:T(8,128)(2,1)}, bf16[192,1024]{1,0:T(8,128)(2,1)S(1)}, u32[]{:S(2)}, u32[]{:S(2)}) collective-permute-start(bf16[192,1024]{1,0:T(8,128)(2,1)} %pool.1.refs_0_), channel_id=1, source_target_pairs={{0,4},{1,65},{2,6},{3,67},{4,8},{5,69},{6,10},{7,71},{8,12},{9,73}... | collective-permute-start | bytes 1179656 | tf_op jit(solution)/shard_map/ppermute | solution.py:28
  7.9 16.1 %collective-permute-start = (bf16[192,1024]{1,0:T(8,128)(2,1)}, bf16[192,1024]{1,0:T(8,128)(2,1)S(1)}, u32[]{:S(2)}, u32[]{:S(2)}) collective-permute-start(bf16[192,1024]{1,0:T(8,128)(2,1)} %pool.1.refs_0_), channel_id=1, source_target_pairs={{0,8},{1,33},{2,10},{3,35},{4,28},{5,37},{6,30},{7,39},{8,16},{9,4... | collective-permute-start | bytes 1179656 | tf_op jit(solution)/shard_map/ppermute | solution.py:28
  11.2 12.9 %collective-permute-start.2 = (bf16[192,1024]{1,0:T(8,128)(2,1)}, bf16[192,1024]{1,0:T(8,128)(2,1)S(1)}, u32[]{:S(2)}, u32[]{:S(2)}) collective-permute-start(bf16[192,1024]{1,0:T(8,128)(2,1)} %pool.1.refs_0_), channel_id=1, source_target_pairs={{0,24},{1,129},{2,26},{3,131},{4,12},{5,133},{6,14},{7,135},{8,0},... | collective-permute-start | bytes 1179656 | tf_op jit(solution)/shard_map/ppermute | solution.py:28
  13.3 11.2 %collective-permute-start.7 = (bf16[192,1024]{1,0:T(8,128)(2,1)}, bf16[192,1024]{1,0:T(8,128)(2,1)S(1)}, u32[]{:S(2)}, u32[]{:S(2)}) collective-permute-start(bf16[192,1024]{1,0:T(8,128)(2,1)} %pool.1.refs_0_), channel_id=1, source_target_pairs={{0,1},{1,0},{2,3},{3,2},{4,5},{5,4},{6,7},{7,6},{8,9},{9,8},{10,11... | collective-permute-start | bytes 1179656 | tf_op jit(solution)/shard_map/ppermute | solution.py:32
  13.3 14.5 %collective-permute-start.6 = (bf16[192,1024]{1,0:T(8,128)(2,1)}, bf16[192,1024]{1,0:T(8,128)(2,1)S(1)}, u32[]{:S(2)}, u32[]{:S(2)}) collective-permute-start(bf16[192,1024]{1,0:T(8,128)(2,1)} %pool.1.refs_0_), channel_id=1, source_target_pairs={{0,28},{1,193},{2,30},{3,195},{4,0},{5,197},{6,2},{7,199},{8,4},{9... | collective-permute-start | bytes 1179656 | tf_op jit(solution)/shard_map/ppermute | solution.py:28
  17.8 11.4 %collective-permute-start.10 = (bf16[192,1024]{1,0:T(8,128)(2,1)S(1)}, bf16[192,1024]{1,0:T(8,128)(2,1)S(1)}, u32[]{:S(2)}, u32[]{:S(2)}) collective-permute-start(bf16[192,1024]{1,0:T(8,128)(2,1)S(1)} %collective-permute-done.5.refs_1_.refs_2_), channel_id=1, source_target_pairs={{0,1},{1,0},{2,3},{3,2},{4,5},{5,4},{6,7},{7,6},{8,9},{9,8},{10,11... | collective-permute-start | bytes 1179656 | tf_op jit(solution)/shard_map/ppermute | solution.py:32
  24.0 7.7 %collective-permute-start.8 = (bf16[192,1024]{1,0:T(8,128)(2,1)S(1)}, bf16[192,1024]{1,0:T(8,128)(2,1)S(1)}, u32[]{:S(2)}, u32[]{:S(2)}) collective-permute-start(bf16[192,1024]{1,0:T(8,128)(2,1)S(1)} %collective-permute-done.refs_0_), channel_id=1, source_target_pairs={{0,1},{1,0},{2,3},{3,2},{4,5},{5,4},{6,7},{7,6},{8,9},{9,8},{10,11... | collective-permute-start | bytes 1179656 | tf_op jit(solution)/shard_map/ppermute | solution.py:32
  24.0 7.7 %collective-permute-start.9 = (bf16[192,1024]{1,0:T(8,128)(2,1)S(1)}, bf16[192,1024]{1,0:T(8,128)(2,1)S(1)}, u32[]{:S(2)}, u32[]{:S(2)}) collective-permute-start(bf16[192,1024]{1,0:T(8,128)(2,1)S(1)} %collective-permute-done.2.refs_1_), channel_id=1, source_target_pairs={{0,1},{1,0},{2,3},{3,2},{4,5},{5,4},{6,7},{7,6},{8,9},{9,8},{10,11... | collective-permute-start | bytes 1179656 | tf_op jit(solution)/shard_map/ppermute | solution.py:32
  24.5 12.7 %collective-permute-start.1 = (bf16[192,1024]{1,0:T(8,128)(2,1)S(1)}, bf16[192,1024]{1,0:T(8,128)(2,1)S(1)}, u32[]{:S(2)}, u32[]{:S(2)}) collective-permute-start(bf16[192,1024]{1,0:T(8,128)(2,1)S(1)} %collective-permute-done.refs_0_), channel_id=1, source_target_pairs={{0,4},{1,65},{2,6},{3,67},{4,0},{5,69},{6,2},{7,71},{8,12},{9,73},... | collective-permute-start | bytes 1179656 | tf_op jit(solution)/shard_map/ppermute | solution.py:28
  27.8 12.5 %collective-permute-start.4 = (bf16[192,1024]{1,0:T(8,128)(2,1)S(1)}, bf16[192,1024]{1,0:T(8,128)(2,1)S(1)}, u32[]{:S(2)}, u32[]{:S(2)}) collective-permute-start(bf16[192,1024]{1,0:T(8,128)(2,1)S(1)} %collective-permute-done.refs_0_), channel_id=1, source_target_pairs={{0,8},{1,193},{2,10},{3,195},{4,28},{5,197},{6,30},{7,199},{8,16},... | collective-permute-start | bytes 1179656 | tf_op jit(solution)/shard_map/ppermute | solution.py:28
  29.2 13.2 %collective-permute-start.3 = (bf16[192,1024]{1,0:T(8,128)(2,1)S(1)}, bf16[192,1024]{1,0:T(8,128)(2,1)S(1)}, u32[]{:S(2)}, u32[]{:S(2)}) collective-permute-start(bf16[192,1024]{1,0:T(8,128)(2,1)S(1)} %collective-permute-done.2.refs_1_), channel_id=1, source_target_pairs={{0,28},{1,33},{2,30},{3,35},{4,8},{5,37},{6,10},{7,39},{8,4},{9,41... | collective-permute-start | bytes 1179656 | tf_op jit(solution)/shard_map/ppermute | solution.py:28
  31.7 13.9 %collective-permute-start.11 = (bf16[192,1024]{1,0:T(8,128)(2,1)S(1)}, bf16[192,1024]{1,0:T(8,128)(2,1)S(1)}, u32[]{:S(2)}, u32[]{:S(2)}) collective-permute-start(bf16[192,1024]{1,0:T(8,128)(2,1)S(1)} %collective-permute-done.6.refs_2_.refs_3_), channel_id=1, source_target_pairs={{0,1},{1,0},{2,3},{3,2},{4,5},{5,4},{6,7},{7,6},{8,9},{9,8},{10,11... | collective-permute-start | bytes 1179656 | tf_op jit(solution)/shard_map/ppermute | solution.py:32
  33.6 1.0 %copy-start = (bf16[192,1024]{1,0:T(8,128)(2,1)S(1)}, bf16[192,1024]{1,0:T(8,128)(2,1)}, u32[]{:S(2)}) copy-start(bf16[192,1024]{1,0:T(8,128)(2,1)} %pool.1.refs_0_) | copy-start | bytes 1179652
  42.4 3.2 %collective-permute-start.12 = (bf16[192,1024]{1,0:T(8,128)(2,1)S(1)}, bf16[192,1024]{1,0:T(8,128)(2,1)S(1)}, u32[]{:S(2)}, u32[]{:S(2)}) collective-permute-start(bf16[192,1024]{1,0:T(8,128)(2,1)S(1)} %collective-permute-done.1.refs_1_), channel_id=1, source_target_pairs={{0,1},{1,0},{2,3},{3,2},{4,5},{5,4},{6,7},{7,6},{8,9},{9,8},{10,11... | collective-permute-start | bytes 1179656 | tf_op jit(solution)/shard_map/ppermute | solution.py:32
  42.4 3.2 %collective-permute-start.13 = (bf16[192,1024]{1,0:T(8,128)(2,1)S(1)}, bf16[192,1024]{1,0:T(8,128)(2,1)S(1)}, u32[]{:S(2)}, u32[]{:S(2)}) collective-permute-start(bf16[192,1024]{1,0:T(8,128)(2,1)S(1)} %collective-permute-done.3.refs_2_), channel_id=1, source_target_pairs={{0,1},{1,0},{2,3},{3,2},{4,5},{5,4},{6,7},{7,6},{8,9},{9,8},{10,11... | collective-permute-start | bytes 1179656 | tf_op jit(solution)/shard_map/ppermute | solution.py:32
  43.0 2.7 %collective-permute-start.14 = (bf16[192,1024]{1,0:T(8,128)(2,1)S(1)}, bf16[192,1024]{1,0:T(8,128)(2,1)S(1)}, u32[]{:S(2)}, u32[]{:S(2)}) collective-permute-start(bf16[192,1024]{1,0:T(8,128)(2,1)S(1)} %collective-permute-done.4.refs_0_), channel_id=1, source_target_pairs={{0,1},{1,0},{2,3},{3,2},{4,5},{5,4},{6,7},{7,6},{8,9},{9,8},{10,11... | collective-permute-start | bytes 1179656 | tf_op jit(solution)/shard_map/ppermute | solution.py:32
  48.3 16.6 %copy-start.1 = (bf16[192,1024]{1,0:T(8,128)(2,1)S(1)}, bf16[192,1024]{1,0:T(8,128)(2,1)}, u32[]{:S(2)}) copy-start(bf16[192,1024]{1,0:T(8,128)(2,1)} %pool.1.refs_0_) | copy-start | bytes 1179652
  48.3 10.5 %collective-permute-start.18 = (bf16[192,1024]{1,0:T(8,128)(2,1)S(1)}, bf16[192,1024]{1,0:T(8,128)(2,1)S(1)}, u32[]{:S(2)}, u32[]{:S(2)}) collective-permute-start(bf16[192,1024]{1,0:T(8,128)(2,1)S(1)} %get-tuple-element.61), channel_id=1, source_target_pairs={{8,0},{193,1},{10,2},{195,3},{28,4},{197,5},{30,6},{199,7},{16,8},... | collective-permute-start | bytes 1179656 | tf_op jit(solution)/shard_map/ppermute | solution.py:28
  51.5 10.1 %collective-permute-start.19 = (bf16[192,1024]{1,0:T(8,128)(2,1)S(1)}, bf16[192,1024]{1,0:T(8,128)(2,1)S(1)}, u32[]{:S(2)}, u32[]{:S(2)}) collective-permute-start(bf16[192,1024]{1,0:T(8,128)(2,1)S(1)} %get-tuple-element.62), channel_id=1, source_target_pairs={{4,0},{65,1},{6,2},{67,3},{0,4},{69,5},{2,6},{71,7},{12,8},{73,9},... | collective-permute-start | bytes 1179656 | tf_op jit(solution)/shard_map/ppermute | solution.py:28
  52.1 12.5 %collective-permute-start.15 = (bf16[192,1024]{1,0:T(8,128)(2,1)S(1)}, bf16[192,1024]{1,0:T(8,128)(2,1)S(1)}, u32[]{:S(2)}, u32[]{:S(2)}) collective-permute-start(bf16[192,1024]{1,0:T(8,128)(2,1)S(1)} %get-tuple-element.49), channel_id=1, source_target_pairs={{28,0},{33,1},{30,2},{35,3},{8,4},{37,5},{10,6},{39,7},{4,8},{41,9... | collective-permute-start | bytes 1179656 | tf_op jit(solution)/shard_map/ppermute | solution.py:28
  56.3 9.9 %collective-permute-start.16 = (bf16[192,1024]{1,0:T(8,128)(2,1)S(1)}, bf16[192,1024]{1,0:T(8,128)(2,1)S(1)}, u32[]{:S(2)}, u32[]{:S(2)}) collective-permute-start(bf16[192,1024]{1,0:T(8,128)(2,1)S(1)} %get-tuple-element.58), channel_id=1, source_target_pairs={{4,0},{65,1},{6,2},{67,3},{8,4},{69,5},{10,6},{71,7},{12,8},{73,9}... | collective-permute-start | bytes 1179656 | tf_op jit(solution)/shard_map/ppermute | solution.py:28
  58.8 9.0 %collective-permute-start.17 = (bf16[192,1024]{1,0:T(8,128)(2,1)S(1)}, bf16[192,1024]{1,0:T(8,128)(2,1)S(1)}, u32[]{:S(2)}, u32[]{:S(2)}) collective-permute-start(bf16[192,1024]{1,0:T(8,128)(2,1)S(1)} %get-tuple-element.59), channel_id=1, source_target_pairs={{28,0},{193,1},{30,2},{195,3},{0,4},{197,5},{2,6},{199,7},{4,8},{2... | collective-permute-start | bytes 1179656 | tf_op jit(solution)/shard_map/ppermute | solution.py:28
  61.8 12.4 %collective-permute-start.20 = (bf16[192,1024]{1,0:T(8,128)(2,1)S(1)}, bf16[192,1024]{1,0:T(8,128)(2,1)S(1)}, u32[]{:S(2)}, u32[]{:S(2)}) collective-permute-start(bf16[192,1024]{1,0:T(8,128)(2,1)S(1)} %add_convert_fusion), channel_id=1, source_target_pairs={{8,0},{33,1},{10,2},{35,3},{28,4},{37,5},{30,6},{39,7},{16,8},{41,... | collective-permute-start | bytes 1179656 | tf_op jit(solution)/shard_map/ppermute | solution.py:28
  64.7 12.3 %collective-permute-start.21 = (bf16[192,1024]{1,0:T(8,128)(2,1)S(1)}, bf16[192,1024]{1,0:T(8,128)(2,1)S(1)}, u32[]{:S(2)}, u32[]{:S(2)}) collective-permute-start(bf16[192,1024]{1,0:T(8,128)(2,1)S(1)} %add_convert_fusion.1), channel_id=1, source_target_pairs={{24,0},{129,1},{26,2},{131,3},{12,4},{133,5},{14,6},{135,7},{0,8},... | collective-permute-start | bytes 1179656 | tf_op jit(solution)/shard_map/ppermute | solution.py:28

commit v5 on v4

--- a/solution.py
+++ b/solution.py
@@ -146,8 +146,8 @@
 
     rows = [own] + [None] * 7
     rows[1] = send(own, MOVES[1])
-    rows[2] = send(own, MOVES[2])
     later, par, row_ids, col_ids = lax.optimization_barrier((own, par, row_ids, col_ids))
+    rows[2] = send(later, MOVES[2])
     rows[3] = send(later, MOVES[3])
     rows[4] = send(later, MOVES[4])
     rows[5] = send(rows[1], MOVES[5])
@@ -160,14 +160,18 @@
     rows[5], rows[6], rows[7], h0, h1, h2, h3, h4 = lax.optimization_barrier((rows[5], rows[6], rows[7], h0, h1, h2, h3, h4))
     cols += [partner(rows[k]) for k in (5, 6, 7)]
     h7, h5, h6 = grads(state, (7, 5, 6), 0, 1, None, (f32,) * 3)
-    g7, g5, g6 = grads(state, (7, 5, 6), 4, 1, (h7, h5, h6), (bf16,) * 3)
+    (g7,) = grads(state, (7,), 4, 1, (h7,), (bf16,))
+    rows[5], g7 = lax.optimization_barrier((rows[5], g7))
     r7 = send(g7, MOVES[7], True)
+    g5, g6 = grads(state, (5, 6), 4, 1, (h5, h6), (bf16,) * 2)
+    rows[3], g5, g6 = lax.optimization_barrier((rows[3], g5, g6))
     r5 = send(g5, MOVES[5], True)
     r6 = send(g6, MOVES[6], True)
-    rows[1], g6 = lax.optimization_barrier((rows[1], g6))
-    g1, g2, g3, g4 = grads(state, (1, 2, 3, 4), 4, 1, (h1, h2, h3, h4), (f32, f32, bf16, bf16))
+    g3, g4 = grads(state, (3, 4), 4, 1, (h3, h4), (bf16,) * 2)
+    rows[1], g3, g4 = lax.optimization_barrier((rows[1], g3, g4))
     r3 = send(g3, MOVES[3], True)
     r4 = send(g4, MOVES[4], True)
+    g1, g2 = grads(state, (1, 2), 4, 1, (h1, h2), (f32,) * 2)
     s1 = (g1 + r7.astype(f32) + r5.astype(f32)).astype(bf16)
     r1 = send(s1, MOVES[1], True)
     s2 = (g2 + r6.astype(f32)).astype(bf16)

time: 78.1 us -> 78.3 us (level)
  the two profiles are of different devices: /device:TPU:28 before, /device:TPU:20 now
where the time goes in v5:
time: 78.3 us; the launch traced here: 78.2 us
  waiting for transfers between devices  29.9 us (38%)
  starting transfers between devices  24.3 us (31%)
  Pallas kernels  19.3 us (25%)
  local copies, waits for them, and re-layouts  2.84 us (4%)
  other arithmetic  1.53 us (2%)
    ppermute x14, waiting for transfers between devices, send(): return lax.ppermute(v, AXES, pairs)  29.9 us
    ppermute x14, starting transfers between devices, send(): return lax.ppermute(v, AXES, pairs)  23.8 us
    pallas_call x8, Pallas kernels, grads(): pl.pallas_call(functools.partial(grad_kernel, slots, first_col, groups, s...  15.3 us
    pallas_call x1, Pallas kernels, pool(): pl.pallas_call(pool_kernel, in_specs=[pl.BlockSpec(memory_space=pltpu.HBM...  4.03 us
  transfers between devices with their start and end apart: 22, of which 11 were waited for; matrix products, arithmetic and copies ran while one was open for 1% of the time, Pallas kernels for 16%

profile of v5, /device:TPU:20, one launch (start us, length us, event | category | flops | bytes accessed | tf_op | source)
XLA Modules:
  0.0 78.2 jit_solution(1005007191981615592)
XLA Ops:
  0.0 1.3 %fusion = (s32[192]{0:T(256)S(1)}, s32[192]{0:T(256)S(1)}, s32[192]{0:T(256)S(1)}, s32[192]{0:T(256)S(1)}, s32[192]{0:T(256)S(1)}, /*index=5*/s32[192]{0:T(256)S...) fusion(s32[12288]{0:T(1024)} %param.5, ...), kind=kLoop, calls=%fused_computation.5 | loop fusion | bytes 24640 | tf_op jit(solution)/shard_map/dynamic_slice | solution.py:140
  1.4 4.0 %pool.1.refs_0_ = bf16[192,1024]{1,0:T(8,128)(2,1)} custom-call(bf16[192,16,1024]{2,1,0:T(8,128)(2,1)} %bitcast.3), custom_call_target="tpu_custom_call" | custom-call | flops 6291456 | bytes 6291456 | tf_op jit(solution)/shard_map/pool/pallas_call | solution.py:61
  6.0 1.9 %collective-permute-start.1 = (bf16[192,1024]{1,0:T(8,128)(2,1)}, bf16[192,1024]{1,0:T(8,128)(2,1)S(1)}, u32[]{:S(2)}, u32[]{:S(2)}) collective-permute-start(bf16[192,1024]{1,0:T(8,128)(2,1)} %pool.1.refs_0_), channel_id=1, source_target_pairs={{0,4},{1,65},{2,6},{3,67},{4,8},{5,69},{6,10},{7,71},{8,12},{9,73}... | collective-permute-start | bytes 1179656 | tf_op jit(solution)/shard_map/ppermute | solution.py:28
  7.9 5.4 %collective-permute-start.3 = (bf16[192,1024]{1,0:T(8,128)(2,1)}, bf16[192,1024]{1,0:T(8,128)(2,1)S(1)}, u32[]{:S(2)}, u32[]{:S(2)}) collective-permute-start(bf16[192,1024]{1,0:T(8,128)(2,1)} %pool.1.refs_0_), channel_id=1, source_target_pairs={{0,24},{1,129},{2,26},{3,131},{4,12},{5,133},{6,14},{7,135},{8,0},... | collective-permute-start | bytes 1179656 | tf_op jit(solution)/shard_map/ppermute | solution.py:28
  13.3 1.5 %collective-permute-start.6 = (bf16[192,1024]{1,0:T(8,128)(2,1)}, bf16[192,1024]{1,0:T(8,128)(2,1)S(1)}, u32[]{:S(2)}, u32[]{:S(2)}) collective-permute-start(bf16[192,1024]{1,0:T(8,128)(2,1)} %pool.1.refs_0_), channel_id=1, source_target_pairs={{0,28},{1,193},{2,30},{3,195},{4,0},{5,197},{6,2},{7,199},{8,4},{9... | collective-permute-start | bytes 1179656 | tf_op jit(solution)/shard_map/ppermute | solution.py:28
  14.9 2.9 %collective-permute-done.1.refs_1_.refs_0_ = bf16[192,1024]{1,0:T(8,128)(2,1)S(1)} collective-permute-done((bf16[192,1024]{1,0:T(8,128)(2,1)}, bf16[192,1024]{1,0:T(8,128)(2,1)S(1)}, u32[]{:S(2)}, u32[]{:S(2)}) %collective-permute-start.1) | collective-permute-done | bytes 393248 | tf_op jit(solution)/shard_map/ppermute | solution.py:28
  17.8 5.4 %collective-permute-done.3.refs_1_ = bf16[192,1024]{1,0:T(8,128)(2,1)S(1)} collective-permute-done((bf16[192,1024]{1,0:T(8,128)(2,1)}, bf16[192,1024]{1,0:T(8,128)(2,1)S(1)}, u32[]{:S(2)}, u32[]{:S(2)}) %collective-permute-start.3) | collective-permute-done | bytes 393248 | tf_op jit(solution)/shard_map/ppermute | solution.py:28
  23.2 0.8 %collective-permute-done.refs_0_ = bf16[192,1024]{1,0:T(8,128)(2,1)S(1)} collective-permute-done((bf16[192,1024]{1,0:T(8,128)(2,1)}, bf16[192,1024]{1,0:T(8,128)(2,1)S(1)}, u32[]{:S(2)}, u32[]{:S(2)}) %collective-permute-start) | collective-permute-done | bytes 393248 | tf_op jit(solution)/shard_map/ppermute | solution.py:28
  24.0 5.2 %collective-permute-start.4 = (bf16[192,1024]{1,0:T(8,128)(2,1)S(1)}, bf16[192,1024]{1,0:T(8,128)(2,1)S(1)}, u32[]{:S(2)}, u32[]{:S(2)}) collective-permute-start(bf16[192,1024]{1,0:T(8,128)(2,1)S(1)} %collective-permute-done.3.refs_1_), channel_id=1, source_target_pairs={{0,28},{1,33},{2,30},{3,35},{4,8},{5,37},{6,10},{7,39},{8,4},{9,41... | collective-permute-start | bytes 1179656 | tf_op jit(solution)/shard_map/ppermute | solution.py:28
  29.3 1.2 %collective-permute-start.5 = (bf16[192,1024]{1,0:T(8,128)(2,1)S(1)}, bf16[192,1024]{1,0:T(8,128)(2,1)S(1)}, u32[]{:S(2)}, u32[]{:S(2)}) collective-permute-start(bf16[192,1024]{1,0:T(8,128)(2,1)S(1)} %collective-permute-done.refs_0_), channel_id=1, source_target_pairs={{0,8},{1,193},{2,10},{3,195},{4,28},{5,197},{6,30},{7,199},{8,16},... | collective-permute-start | bytes 1179656 | tf_op jit(solution)/shard_map/ppermute | solution.py:28
  30.5 1.9 %shard_map.47 = (f32[192,1024]{1,0:T(8,128)S(1)}, f32[192,1024]{1,0:T(8,128)S(1)}) custom-call(f32[4,768]{1,0:T(4,128)S(1)} %broadcast_in_dim.6.par_ref, s32[1536,128]{1,0:T(8,128)S(1)} %broadcast_in_dim.7.row_ref, s32[1,1536]{1,0:T(1,128)S(1)} %broadcast_in_dim.8.col_ref, bf16[192,1024]{1,0:T(8,128)(2,1)S(1)} %collective-permute-done.refs_0_, ...), custom_call_target="tpu_custom_call" | custom-call | flops 1207959552 | bytes 1572864 | tf_op jit(solution)/shard_map/pallas_call | solution.py:102
  32.4 1.0 %copy-done = bf16[192,1024]{1,0:T(8,128)(2,1)S(1)} copy-done((bf16[192,1024]{1,0:T(8,128)(2,1)S(1)}, bf16[192,1024]{1,0:T(8,128)(2,1)}, u32[]{:S(2)}) %copy-start) | copy-done | bytes 393240
  33.4 2.6 %shard_map.46 = (f32[192,1024]{1,0:T(8,128)S(1)}, f32[192,1024]{1,0:T(8,128)S(1)}, f32[192,1024]{1,0:T(8,128)S(1)}) custom-call(f32[4,768]{1,0:T(4,128)S(1)} %broadcast_in_dim.6.par_ref, s32[1536,128]{1,0:T(8,128)S(1)} %broadcast_in_dim.7.row_ref, s32[1,1536]{1,0:T(1,128)S(1)} %broadcast_in_dim.8.col_ref, bf16[192,1024]{1,0:T(8,128)(2,1)S(1)} %copy-done, ...), custom_call_target="tpu_custom_call" | custom-call | flops 1811939328 | bytes 1572864 | tf_op jit(solution)/shard_map/pallas_call | solution.py:102
  36.0 1.0 %collective-permute-done.2.refs_1_.refs_0_ = bf16[192,1024]{1,0:T(8,128)(2,1)S(1)} collective-permute-done((bf16[192,1024]{1,0:T(8,128)(2,1)S(1)}, bf16[192,1024]{1,0:T(8,128)(2,1)S(1)}, u32[]{:S(2)}, u32[]{:S(2)}) %collective-permute-start.2) | collective-permute-done | bytes 393248 | tf_op jit(solution)/shard_map/ppermute | solution.py:28
  37.0 5.4 %collective-permute-done.5.refs_0_ = bf16[192,1024]{1,0:T(8,128)(2,1)S(1)} collective-permute-done((bf16[192,1024]{1,0:T(8,128)(2,1)S(1)}, bf16[192,1024]{1,0:T(8,128)(2,1)S(1)}, u32[]{:S(2)}, u32[]{:S(2)}) %collective-permute-start.5) | collective-permute-done | bytes 393248 | tf_op jit(solution)/shard_map/ppermute | solution.py:28
  43.0 2.6 %shard_map.48 = (f32[192,1024]{1,0:T(8,128)S(1)}, f32[192,1024]{1,0:T(8,128)S(1)}, f32[192,1024]{1,0:T(8,128)S(1)}) custom-call(f32[4,768]{1,0:T(4,128)S(1)} %broadcast_in_dim.6.par_ref, s32[1536,128]{1,0:T(8,128)S(1)} %broadcast_in_dim.7.row_ref, s32[1,1536]{1,0:T(1,128)S(1)} %broadcast_in_dim.8.col_ref, ...), custom_call_target="tpu_custom_call" | custom-call | flops 1811939328 | bytes 1572864 | tf_op jit(solution)/shard_map/pallas_call | solution.py:102
  45.6 1.2 %shard_map.49 = bf16[192,1024]{1,0:T(8,128)(2,1)S(1)} custom-call(f32[4,768]{1,0:T(4,128)S(1)} %broadcast_in_dim.6.par_ref, s32[1536,128]{1,0:T(8,128)S(1)} %broadcast_in_dim.7.row_ref, s32[1,1536]{1,0:T(1,128)S(1)} %broadcast_in_dim.8.col_ref, bf16[192,1024]{1,0:T(8,128)(2,1)S(1)} %collective-permute-done.5.refs_0_, ...), custom_call_target="tpu_custom_call" | custom-call | flops 603979776 | bytes 1572864 | tf_op jit(solution)/shard_map/pallas_call | solution.py:102
  46.9 1.9 %shard_map.50 = (bf16[192,1024]{1,0:T(8,128)(2,1)S(1)}, bf16[192,1024]{1,0:T(8,128)(2,1)S(1)}) custom-call(f32[4,768]{1,0:T(4,128)S(1)} %broadcast_in_dim.6.par_ref, s32[1536,128]{1,0:T(8,128)S(1)} %broadcast_in_dim.7.row_ref, s32[1,1536]{1,0:T(1,128)S(1)} %broadcast_in_dim.8.col_ref, bf16[192,1024]{1,0:T(8,128)(2,1)S(1)} %collective-permute-done.2.refs_1_.refs_0_, ...), custom_call_target="tpu_custom_call" | custom-call | flops 1207959552 | bytes 1572864 | tf_op jit(solution)/shard_map/pallas_call | solution.py:102
  48.9 2.9 %collective-permute-start.18 = (bf16[192,1024]{1,0:T(8,128)(2,1)S(1)}, bf16[192,1024]{1,0:T(8,128)(2,1)S(1)}, u32[]{:S(2)}, u32[]{:S(2)}) collective-permute-start(bf16[192,1024]{1,0:T(8,128)(2,1)S(1)} %shard_map.49), channel_id=1, source_target_pairs={{8,0},{193,1},{10,2},{195,3},{28,4},{197,5},{30,6},{199,7},{16,8},... | collective-permute-start | bytes 1179656 | tf_op jit(solution)/shard_map/ppermute | solution.py:28
  51.8 1.8 %collective-permute-start.15 = (bf16[192,1024]{1,0:T(8,128)(2,1)S(1)}, bf16[192,1024]{1,0:T(8,128)(2,1)S(1)}, u32[]{:S(2)}, u32[]{:S(2)}) collective-permute-start(bf16[192,1024]{1,0:T(8,128)(2,1)S(1)} %get-tuple-element.67), channel_id=1, source_target_pairs={{28,0},{33,1},{30,2},{35,3},{8,4},{37,5},{10,6},{39,7},{4,8},{41,9... | collective-permute-start | bytes 1179656 | tf_op jit(solution)/shard_map/ppermute | solution.py:28
  53.6 1.9 %shard_map.51 = (bf16[192,1024]{1,0:T(8,128)(2,1)S(1)}, bf16[192,1024]{1,0:T(8,128)(2,1)S(1)}) custom-call(f32[4,768]{1,0:T(4,128)S(1)} %broadcast_in_dim.6.par_ref, s32[1536,128]{1,0:T(8,128)S(1)} %broadcast_in_dim.7.row_ref, s32[1,1536]{1,0:T(1,128)S(1)} %broadcast_in_dim.8.col_ref, bf16[192,1024]{1,0:T(8,128)(2,1)S(1)} %collective-permute-done.1.refs_1_.refs_0_, ...), custom_call_target="tpu_custom_call" | custom-call | flops 1207959552 | bytes 1572864 | tf_op jit(solution)/shard_map/pallas_call | solution.py:102
  55.5 1.6 %collective-permute-start.16 = (bf16[192,1024]{1,0:T(8,128)(2,1)S(1)}, bf16[192,1024]{1,0:T(8,128)(2,1)S(1)}, u32[]{:S(2)}, u32[]{:S(2)}) collective-permute-start(bf16[192,1024]{1,0:T(8,128)(2,1)S(1)} %get-tuple-element.70), channel_id=1, source_target_pairs={{4,0},{65,1},{6,2},{67,3},{8,4},{69,5},{10,6},{71,7},{12,8},{73,9}... | collective-permute-start | bytes 1179656 | tf_op jit(solution)/shard_map/ppermute | solution.py:28
  57.6 1.9 %shard_map.52 = (f32[192,1024]{1,0:T(8,128)S(1)}, f32[192,1024]{1,0:T(8,128)S(1)}) custom-call(f32[4,768]{1,0:T(4,128)S(1)} %broadcast_in_dim.6.par_ref, s32[1536,128]{1,0:T(8,128)S(1)} %broadcast_in_dim.7.row_ref, s32[1,1536]{1,0:T(1,128)S(1)} %broadcast_in_dim.8.col_ref, bf16[192,1024]{1,0:T(8,128)(2,1)S(1)} %collective-permute-done.refs_0_, ...), custom_call_target="tpu_custom_call" | custom-call | flops 1207959552 | bytes 1572864 | tf_op jit(solution)/shard_map/pallas_call | solution.py:102
  59.5 1.4 %collective-permute-done.19 = bf16[192,1024]{1,0:T(8,128)(2,1)S(1)} collective-permute-done((bf16[192,1024]{1,0:T(8,128)(2,1)S(1)}, bf16[192,1024]{1,0:T(8,128)(2,1)S(1)}, u32[]{:S(2)}, u32[]{:S(2)}) %collective-permute-start.19) | collective-permute-done | bytes 393248 | tf_op jit(solution)/shard_map/ppermute | solution.py:28
  61.0 1.0 %collective-permute-start.20 = (bf16[192,1024]{1,0:T(8,128)(2,1)S(1)}, bf16[192,1024]{1,0:T(8,128)(2,1)S(1)}, u32[]{:S(2)}, u32[]{:S(2)}) collective-permute-start(bf16[192,1024]{1,0:T(8,128)(2,1)S(1)} %add_convert_fusion), channel_id=1, source_target_pairs={{8,0},{33,1},{10,2},{35,3},{28,4},{37,5},{30,6},{39,7},{16,8},{41,... | collective-permute-start | bytes 1179656 | tf_op jit(solution)/shard_map/ppermute | solution.py:28
  62.1 1.5 %collective-permute-done.15 = bf16[192,1024]{1,0:T(8,128)(2,1)S(1)} collective-permute-done((bf16[192,1024]{1,0:T(8,128)(2,1)S(1)}, bf16[192,1024]{1,0:T(8,128)(2,1)S(1)}, u32[]{:S(2)}, u32[]{:S(2)}) %collective-permute-start.15) | collective-permute-done | bytes 393248 | tf_op jit(solution)/shard_map/ppermute | solution.py:28
  63.6 0.6 collective-permute-start.21
  64.2 1.2 %shard_map.53 = f32[192,1024]{1,0:T(8,128)S(1)} custom-call(f32[4,768]{1,0:T(4,128)S(1)} %broadcast_in_dim.6.par_ref, s32[1536,128]{1,0:T(8,128)S(1)} %broadcast_in_dim.7.row_ref, s32[1,1536]{1,0:T(1,128)S(1)} %broadcast_in_dim.8.col_ref, bf16[192,1024]{1,0:T(8,128)(2,1)S(1)} %copy-done.1, bf16[192,1024]{1,0:T(8,128)(2,1)S(1)} %collective-permute-done.11.refs_1_.refs_2_, ...), custom_call_target="tpu_custom_call" | custom-call | flops 603979776 | bytes 1572864 | tf_op jit(solution)/shard_map/pallas_call | solution.py:102
  65.6 2.2 %collective-permute-done.17 = bf16[192,1024]{1,0:T(8,128)(2,1)S(1)} collective-permute-done((bf16[192,1024]{1,0:T(8,128)(2,1)S(1)}, bf16[192,1024]{1,0:T(8,128)(2,1)S(1)}, u32[]{:S(2)}, u32[]{:S(2)}) %collective-permute-start.17) | collective-permute-done | bytes 393248 | tf_op jit(solution)/shard_map/ppermute | solution.py:28
  67.9 6.1 %collective-permute-done.20 = bf16[192,1024]{1,0:T(8,128)(2,1)S(1)} collective-permute-done((bf16[192,1024]{1,0:T(8,128)(2,1)S(1)}, bf16[192,1024]{1,0:T(8,128)(2,1)S(1)}, u32[]{:S(2)}, u32[]{:S(2)}) %collective-permute-start.20) | collective-permute-done | bytes 393248 | tf_op jit(solution)/shard_map/ppermute | solution.py:28
  74.0 3.1 %collective-permute-done.21 = bf16[192,1024]{1,0:T(8,128)(2,1)S(1)} collective-permute-done((bf16[192,1024]{1,0:T(8,128)(2,1)S(1)}, bf16[192,1024]{1,0:T(8,128)(2,1)S(1)}, u32[]{:S(2)}, u32[]{:S(2)}) %collective-permute-start.21) | collective-permute-done | bytes 393248 | tf_op jit(solution)/shard_map/ppermute | solution.py:28
  77.1 1.1 %add_bitcast_fusion = f32[1,192,1024]{2,1,0:T(8,128)} fusion(bf16[192,1024]{1,0:T(8,128)(2,1)S(1)} %collective-permute-done.21, f32[192,1024]{1,0:T(8,128)S(1)} %convert_add_fusion, bf16[192,1024]{1,0:T(8,128)(2,1)S(1)} %collective-permute-done.20), kind=kLoop, calls=%fused_computation | loop fusion | flops 786432 | bytes 2359296 | tf_op jit(solution)/shard_map/reshape | solution.py:183
  (40 shorter events, 2.3 us)
Async XLA Ops:
  0.0 5.5 %copy-start.3 = (f32[2]{0:T(128)S(1)}, f32[2]{0:T(128)}, u32[]{:S(2)}) copy-start(f32[2]{0:T(128)} %param.6) | copy-start | bytes 28
  0.0 5.5 %copy-start.2 = (f32[2]{0:T(128)S(1)}, f32[2]{0:T(128)}, u32[]{:S(2)}) copy-start(f32[2]{0:T(128)} %param.7) | copy-start | bytes 28
  6.0 11.8 %collective-permute-start.1 = (bf16[192,1024]{1,0:T(8,128)(2,1)}, bf16[192,1024]{1,0:T(8,128)(2,1)S(1)}, u32[]{:S(2)}, u32[]{:S(2)}) collective-permute-start(bf16[192,1024]{1,0:T(8,128)(2,1)} %pool.1.refs_0_), channel_id=1, source_target_pairs={{0,4},{1,65},{2,6},{3,67},{4,8},{5,69},{6,10},{7,71},{8,12},{9,73}... | collective-permute-start | bytes 1179656 | tf_op jit(solution)/shard_map/ppermute | solution.py:28
  7.9 15.3 %collective-permute-start.3 = (bf16[192,1024]{1,0:T(8,128)(2,1)}, bf16[192,1024]{1,0:T(8,128)(2,1)S(1)}, u32[]{:S(2)}, u32[]{:S(2)}) collective-permute-start(bf16[192,1024]{1,0:T(8,128)(2,1)} %pool.1.refs_0_), channel_id=1, source_target_pairs={{0,24},{1,129},{2,26},{3,131},{4,12},{5,133},{6,14},{7,135},{8,0},... | collective-permute-start | bytes 1179656 | tf_op jit(solution)/shard_map/ppermute | solution.py:28
  13.3 10.7 %collective-permute-start = (bf16[192,1024]{1,0:T(8,128)(2,1)}, bf16[192,1024]{1,0:T(8,128)(2,1)S(1)}, u32[]{:S(2)}, u32[]{:S(2)}) collective-permute-start(bf16[192,1024]{1,0:T(8,128)(2,1)} %pool.1.refs_0_), channel_id=1, source_target_pairs={{0,8},{1,33},{2,10},{3,35},{4,28},{5,37},{6,30},{7,39},{8,16},{9,4... | collective-permute-start | bytes 1179656 | tf_op jit(solution)/shard_map/ppermute | solution.py:28
  13.3 10.7 %collective-permute-start.7 = (bf16[192,1024]{1,0:T(8,128)(2,1)}, bf16[192,1024]{1,0:T(8,128)(2,1)S(1)}, u32[]{:S(2)}, u32[]{:S(2)}) collective-permute-start(bf16[192,1024]{1,0:T(8,128)(2,1)} %pool.1.refs_0_), channel_id=1, source_target_pairs={{0,1},{1,0},{2,3},{3,2},{4,5},{5,4},{6,7},{7,6},{8,9},{9,8},{10,11... | collective-permute-start | bytes 1179656 | tf_op jit(solution)/shard_map/ppermute | solution.py:32
  13.3 15.9 %collective-permute-start.6 = (bf16[192,1024]{1,0:T(8,128)(2,1)}, bf16[192,1024]{1,0:T(8,128)(2,1)S(1)}, u32[]{:S(2)}, u32[]{:S(2)}) collective-permute-start(bf16[192,1024]{1,0:T(8,128)(2,1)} %pool.1.refs_0_), channel_id=1, source_target_pairs={{0,28},{1,193},{2,30},{3,195},{4,0},{5,197},{6,2},{7,199},{8,4},{9... | collective-permute-start | bytes 1179656 | tf_op jit(solution)/shard_map/ppermute | solution.py:28
  17.8 11.4 %collective-permute-start.10 = (bf16[192,1024]{1,0:T(8,128)(2,1)S(1)}, bf16[192,1024]{1,0:T(8,128)(2,1)S(1)}, u32[]{:S(2)}, u32[]{:S(2)}) collective-permute-start(bf16[192,1024]{1,0:T(8,128)(2,1)S(1)} %collective-permute-done.1.refs_1_.refs_0_), channel_id=1, source_target_pairs={{0,1},{1,0},{2,3},{3,2},{4,5},{5,4},{6,7},{7,6},{8,9},{9,8},{10,11... | collective-permute-start | bytes 1179656 | tf_op jit(solution)/shard_map/ppermute | solution.py:32
  23.2 7.3 %collective-permute-start.9 = (bf16[192,1024]{1,0:T(8,128)(2,1)S(1)}, bf16[192,1024]{1,0:T(8,128)(2,1)S(1)}, u32[]{:S(2)}, u32[]{:S(2)}) collective-permute-start(bf16[192,1024]{1,0:T(8,128)(2,1)S(1)} %collective-permute-done.3.refs_1_), channel_id=1, source_target_pairs={{0,1},{1,0},{2,3},{3,2},{4,5},{5,4},{6,7},{7,6},{8,9},{9,8},{10,11... | collective-permute-start | bytes 1179656 | tf_op jit(solution)/shard_map/ppermute | solution.py:32
  24.0 6.5 %collective-permute-start.8 = (bf16[192,1024]{1,0:T(8,128)(2,1)S(1)}, bf16[192,1024]{1,0:T(8,128)(2,1)S(1)}, u32[]{:S(2)}, u32[]{:S(2)}) collective-permute-start(bf16[192,1024]{1,0:T(8,128)(2,1)S(1)} %collective-permute-done.refs_0_), channel_id=1, source_target_pairs={{0,1},{1,0},{2,3},{3,2},{4,5},{5,4},{6,7},{7,6},{8,9},{9,8},{10,11... | collective-permute-start | bytes 1179656 | tf_op jit(solution)/shard_map/ppermute | solution.py:32
  24.0 12.0 %collective-permute-start.4 = (bf16[192,1024]{1,0:T(8,128)(2,1)S(1)}, bf16[192,1024]{1,0:T(8,128)(2,1)S(1)}, u32[]{:S(2)}, u32[]{:S(2)}) collective-permute-start(bf16[192,1024]{1,0:T(8,128)(2,1)S(1)} %collective-permute-done.3.refs_1_), channel_id=1, source_target_pairs={{0,28},{1,33},{2,30},{3,35},{4,8},{5,37},{6,10},{7,39},{8,4},{9,41... | collective-permute-start | bytes 1179656 | tf_op jit(solution)/shard_map/ppermute | solution.py:28
  29.3 7.8 %collective-permute-start.2 = (bf16[192,1024]{1,0:T(8,128)(2,1)S(1)}, bf16[192,1024]{1,0:T(8,128)(2,1)S(1)}, u32[]{:S(2)}, u32[]{:S(2)}) collective-permute-start(bf16[192,1024]{1,0:T(8,128)(2,1)S(1)} %collective-permute-done.refs_0_), channel_id=1, source_target_pairs={{0,4},{1,65},{2,6},{3,67},{4,0},{5,69},{6,2},{7,71},{8,12},{9,73},... | collective-permute-start | bytes 1179656 | tf_op jit(solution)/shard_map/ppermute | solution.py:28
  29.3 13.2 %collective-permute-start.5 = (bf16[192,1024]{1,0:T(8,128)(2,1)S(1)}, bf16[192,1024]{1,0:T(8,128)(2,1)S(1)}, u32[]{:S(2)}, u32[]{:S(2)}) collective-permute-start(bf16[192,1024]{1,0:T(8,128)(2,1)S(1)} %collective-permute-done.refs_0_), channel_id=1, source_target_pairs={{0,8},{1,193},{2,10},{3,195},{4,28},{5,197},{6,30},{7,199},{8,16},... | collective-permute-start | bytes 1179656 | tf_op jit(solution)/shard_map/ppermute | solution.py:28
  30.5 15.1 %collective-permute-start.11 = (bf16[192,1024]{1,0:T(8,128)(2,1)S(1)}, bf16[192,1024]{1,0:T(8,128)(2,1)S(1)}, u32[]{:S(2)}, u32[]{:S(2)}) collective-permute-start(bf16[192,1024]{1,0:T(8,128)(2,1)S(1)} %collective-permute-done.6.refs_2_.refs_1_), channel_id=1, source_target_pairs={{0,1},{1,0},{2,3},{3,2},{4,5},{5,4},{6,7},{7,6},{8,9},{9,8},{10,11... | collective-permute-start | bytes 1179656 | tf_op jit(solution)/shard_map/ppermute | solution.py:32
  32.4 1.0 %copy-start = (bf16[192,1024]{1,0:T(8,128)(2,1)S(1)}, bf16[192,1024]{1,0:T(8,128)(2,1)}, u32[]{:S(2)}) copy-start(bf16[192,1024]{1,0:T(8,128)(2,1)} %pool.1.refs_0_) | copy-start | bytes 1179652
  42.4 3.2 %collective-permute-start.12 = (bf16[192,1024]{1,0:T(8,128)(2,1)S(1)}, bf16[192,1024]{1,0:T(8,128)(2,1)S(1)}, u32[]{:S(2)}, u32[]{:S(2)}) collective-permute-start(bf16[192,1024]{1,0:T(8,128)(2,1)S(1)} %collective-permute-done.2.refs_1_.refs_0_), channel_id=1, source_target_pairs={{0,1},{1,0},{2,3},{3,2},{4,5},{5,4},{6,7},{7,6},{8,9},{9,8},{10,11... | collective-permute-start | bytes 1179656 | tf_op jit(solution)/shard_map/ppermute | solution.py:32
  42.4 3.2 %collective-permute-start.13 = (bf16[192,1024]{1,0:T(8,128)(2,1)S(1)}, bf16[192,1024]{1,0:T(8,128)(2,1)S(1)}, u32[]{:S(2)}, u32[]{:S(2)}) collective-permute-start(bf16[192,1024]{1,0:T(8,128)(2,1)S(1)} %collective-permute-done.4.refs_2_.refs_1_), channel_id=1, source_target_pairs={{0,1},{1,0},{2,3},{3,2},{4,5},{5,4},{6,7},{7,6},{8,9},{9,8},{10,11... | collective-permute-start | bytes 1179656 | tf_op jit(solution)/shard_map/ppermute | solution.py:32
  42.9 2.7 %collective-permute-start.14 = (bf16[192,1024]{1,0:T(8,128)(2,1)S(1)}, bf16[192,1024]{1,0:T(8,128)(2,1)S(1)}, u32[]{:S(2)}, u32[]{:S(2)}) collective-permute-start(bf16[192,1024]{1,0:T(8,128)(2,1)S(1)} %collective-permute-done.5.refs_0_), channel_id=1, source_target_pairs={{0,1},{1,0},{2,3},{3,2},{4,5},{5,4},{6,7},{7,6},{8,9},{9,8},{10,11... | collective-permute-start | bytes 1179656 | tf_op jit(solution)/shard_map/ppermute | solution.py:32
  48.8 15.4 %copy-start.1 = (bf16[192,1024]{1,0:T(8,128)(2,1)S(1)}, bf16[192,1024]{1,0:T(8,128)(2,1)}, u32[]{:S(2)}) copy-start(bf16[192,1024]{1,0:T(8,128)(2,1)} %pool.1.refs_0_) | copy-start | bytes 1179652
  48.8 12.1 %collective-permute-start.19 = (bf16[192,1024]{1,0:T(8,128)(2,1)S(1)}, bf16[192,1024]{1,0:T(8,128)(2,1)S(1)}, u32[]{:S(2)}, u32[]{:S(2)}) collective-permute-start(bf16[192,1024]{1,0:T(8,128)(2,1)S(1)} %get-tuple-element.74), channel_id=1, source_target_pairs={{4,0},{65,1},{6,2},{67,3},{0,4},{69,5},{2,6},{71,7},{12,8},{73,9},... | collective-permute-start | bytes 1179656 | tf_op jit(solution)/shard_map/ppermute | solution.py:28
  48.9 12.0 %collective-permute-start.18 = (bf16[192,1024]{1,0:T(8,128)(2,1)S(1)}, bf16[192,1024]{1,0:T(8,128)(2,1)S(1)}, u32[]{:S(2)}, u32[]{:S(2)}) collective-permute-start(bf16[192,1024]{1,0:T(8,128)(2,1)S(1)} %shard_map.49), channel_id=1, source_target_pairs={{8,0},{193,1},{10,2},{195,3},{28,4},{197,5},{30,6},{199,7},{16,8},... | collective-permute-start | bytes 1179656 | tf_op jit(solution)/shard_map/ppermute | solution.py:28
  51.8 11.7 %collective-permute-start.15 = (bf16[192,1024]{1,0:T(8,128)(2,1)S(1)}, bf16[192,1024]{1,0:T(8,128)(2,1)S(1)}, u32[]{:S(2)}, u32[]{:S(2)}) collective-permute-start(bf16[192,1024]{1,0:T(8,128)(2,1)S(1)} %get-tuple-element.67), channel_id=1, source_target_pairs={{28,0},{33,1},{30,2},{35,3},{8,4},{37,5},{10,6},{39,7},{4,8},{41,9... | collective-permute-start | bytes 1179656 | tf_op jit(solution)/shard_map/ppermute | solution.py:28
  55.5 10.1 %collective-permute-start.16 = (bf16[192,1024]{1,0:T(8,128)(2,1)S(1)}, bf16[192,1024]{1,0:T(8,128)(2,1)S(1)}, u32[]{:S(2)}, u32[]{:S(2)}) collective-permute-start(bf16[192,1024]{1,0:T(8,128)(2,1)S(1)} %get-tuple-element.70), channel_id=1, source_target_pairs={{4,0},{65,1},{6,2},{67,3},{8,4},{69,5},{10,6},{71,7},{12,8},{73,9}... | collective-permute-start | bytes 1179656 | tf_op jit(solution)/shard_map/ppermute | solution.py:28
  57.0 10.8 %collective-permute-start.17 = (bf16[192,1024]{1,0:T(8,128)(2,1)S(1)}, bf16[192,1024]{1,0:T(8,128)(2,1)S(1)}, u32[]{:S(2)}, u32[]{:S(2)}) collective-permute-start(bf16[192,1024]{1,0:T(8,128)(2,1)S(1)} %get-tuple-element.71), channel_id=1, source_target_pairs={{28,0},{193,1},{30,2},{195,3},{0,4},{197,5},{2,6},{199,7},{4,8},{2... | collective-permute-start | bytes 1179656 | tf_op jit(solution)/shard_map/ppermute | solution.py:28
  61.0 13.0 %collective-permute-start.20 = (bf16[192,1024]{1,0:T(8,128)(2,1)S(1)}, bf16[192,1024]{1,0:T(8,128)(2,1)S(1)}, u32[]{:S(2)}, u32[]{:S(2)}) collective-permute-start(bf16[192,1024]{1,0:T(8,128)(2,1)S(1)} %add_convert_fusion), channel_id=1, source_target_pairs={{8,0},{33,1},{10,2},{35,3},{28,4},{37,5},{30,6},{39,7},{16,8},{41,... | collective-permute-start | bytes 1179656 | tf_op jit(solution)/shard_map/ppermute | solution.py:28
  63.6 13.5 %collective-permute-start.21 = (bf16[192,1024]{1,0:T(8,128)(2,1)S(1)}, bf16[192,1024]{1,0:T(8,128)(2,1)S(1)}, u32[]{:S(2)}, u32[]{:S(2)}) collective-permute-start(bf16[192,1024]{1,0:T(8,128)(2,1)S(1)} %add_convert_fusion.1), channel_id=1, source_target_pairs={{24,0},{129,1},{26,2},{131,3},{12,4},{133,5},{14,6},{135,7},{0,8},... | collective-permute-start | bytes 1179656 | tf_op jit(solution)/shard_map/ppermute | solution.py:28

commit v6 on v5

--- a/solution.py
+++ b/solution.py
@@ -123,6 +123,9 @@
 Y_OFF = (0, 1, 0, 0, 0, 1, 1, 1)
 
 
+COLS = (0, 1, 2, 5, 7, 6, 3, 4)
+
+
 def on_device(patch_rows, subject_ids, logit_scale, logit_bias):
     n, _, width = patch_rows.shape[1:]
     f32, bf16 = jnp.float32, jnp.bfloat16
@@ -132,17 +135,17 @@
     first = lax.axis_index("con") % 2 == 0
     x, yh, z = blk // 16, (blk // 8) % 2, blk % 8
 
-    def ids(on_first):
+    def ids(on_first, slots):
         parts = []
-        for even, odd, xo, yo in zip(Z_EVEN, Z_ODD, X_OFF, Y_OFF):
+        for even, odd, xo, yo in [(Z_EVEN[k], Z_ODD[k], X_OFF[k], Y_OFF[k]) for k in slots]:
             on_z = (x * NYH + yh) * NZ + (z + jnp.where(z % 2 == 0, even, odd)) % NZ
             on_xy = (((x + xo) % NX) * NYH + (yh + yo) % NYH) * NZ + z
             parts.append(lax.dynamic_slice_in_dim(subject_ids, jnp.where(on_first, on_z, on_xy) * n, n, 0))
         return jnp.concatenate(parts)
 
     par = jnp.broadcast_to(jnp.concatenate([logit_scale, logit_bias])[:, None] * 0.5, (4, 4 * n))
-    row_ids = jnp.broadcast_to(ids(first)[:, None], (8 * n, 128))
-    col_ids = ids(jnp.logical_not(first))[None, :]
+    row_ids = jnp.broadcast_to(ids(first, range(8))[:, None], (8 * n, 128))
+    col_ids = ids(jnp.logical_not(first), COLS)[None, :]
 
     rows = [own] + [None] * 7
     rows[1] = send(own, MOVES[1])
@@ -153,13 +156,16 @@
     rows[5] = send(rows[1], MOVES[5])
     rows[7] = send(rows[1], MOVES[7])
     rows[6] = send(rows[2], MOVES[6])
-    cols = [partner(v) for v in rows[:5]]
+    cols = [partner(rows[k]) for k in (0, 1, 2, 5)]
     state = (par, row_ids, col_ids, rows, cols)
-    h0, h3, h4 = grads(state, (0, 3, 4), 0, 1, None, (f32,) * 3)
-    h1, h2 = grads(state, (1, 2), 0, 1, None, (f32,) * 2)
-    rows[5], rows[6], rows[7], h0, h1, h2, h3, h4 = lax.optimization_barrier((rows[5], rows[6], rows[7], h0, h1, h2, h3, h4))
-    cols += [partner(rows[k]) for k in (5, 6, 7)]
+    h0, h1, h2 = grads(state, (0, 1, 2), 0, 1, None, (f32,) * 3)
+    rows[7], rows[6], h0, h1, h2 = lax.optimization_barrier((rows[7], rows[6], h0, h1, h2))
+    cols += [partner(rows[k]) for k in (7, 6)]
     h7, h5, h6 = grads(state, (7, 5, 6), 0, 1, None, (f32,) * 3)
+    rows[3], rows[4], h7, h5, h6 = lax.optimization_barrier((rows[3], rows[4], h7, h5, h6))
+    cols += [partner(rows[k]) for k in (3, 4)]
+    h3, h4 = grads(state, (3, 4), 0, 1, None, (f32,) * 2)
+    h7, h3, h4 = lax.optimization_barrier((h7, h3, h4))
     (g7,) = grads(state, (7,), 4, 1, (h7,), (bf16,))
     rows[5], g7 = lax.optimization_barrier((rows[5], g7))
     r7 = send(g7, MOVES[7], True)

time: 78.3 us -> 82.5 us (1.054)
  the two profiles are of different devices: /device:TPU:20 before, /device:TPU:10 now
where the time goes in v6:
time: 82.5 us; the launch traced here: 82.3 us
  starting transfers between devices  32.8 us (40%)
  waiting for transfers between devices  25.8 us (31%)
  Pallas kernels  19.2 us (23%)
  local copies, waits for them, and re-layouts  2.72 us (3%)
  other arithmetic  1.55 us (2%)
    ppermute x14, starting transfers between devices, send(): return lax.ppermute(v, AXES, pairs)  31.3 us
    ppermute x14, waiting for transfers between devices, send(): return lax.ppermute(v, AXES, pairs)  25.3 us
    pallas_call x8, Pallas kernels, grads(): pl.pallas_call(functools.partial(grad_kernel, slots, first_col, groups, s...  15.2 us
    pallas_call x1, Pallas kernels, pool(): pl.pallas_call(pool_kernel, in_specs=[pl.BlockSpec(memory_space=pltpu.HBM...  4.05 us
  transfers between devices with their start and end apart: 22, of which 11 were waited for; matrix products, arithmetic and copies ran while one was open for 3% of the time, Pallas kernels for 15%

profile of v6, /device:TPU:10, one launch (start us, length us, event | category | flops | bytes accessed | tf_op | source)
XLA Modules:
  0.0 82.3 jit_solution(9406574927131512608)
XLA Ops:
  0.0 4.1 %pool.1.refs_0_ = bf16[192,1024]{1,0:T(8,128)(2,1)} custom-call(bf16[192,16,1024]{2,1,0:T(8,128)(2,1)} %bitcast.3), custom_call_target="tpu_custom_call" | custom-call | flops 6291456 | bytes 6291456 | tf_op jit(solution)/shard_map/pool/pallas_call | solution.py:61
  4.1 3.3 %collective-permute-start = (bf16[192,1024]{1,0:T(8,128)(2,1)}, bf16[192,1024]{1,0:T(8,128)(2,1)S(1)}, u32[]{:S(2)}, u32[]{:S(2)}) collective-permute-start(bf16[192,1024]{1,0:T(8,128)(2,1)} %pool.1.refs_0_), channel_id=1, source_target_pairs={{0,8},{1,33},{2,10},{3,35},{4,28},{5,37},{6,30},{7,39},{8,16},{9,4... | collective-permute-start | bytes 1179656 | tf_op jit(solution)/shard_map/ppermute | solution.py:28
  7.4 1.2 %fusion = (s32[192]{0:T(256)S(1)}, s32[192]{0:T(256)S(1)}, s32[192]{0:T(256)S(1)}, s32[192]{0:T(256)S(1)}, s32[192]{0:T(256)S(1)}, /*index=5*/s32[192]{0:T(256)S...) fusion(s32[12288]{0:T(1024)} %param.5, ...), kind=kLoop, calls=%fused_computation.5 | loop fusion | bytes 24640 | tf_op jit(solution)/shard_map/dynamic_slice | solution.py:143
  9.2 3.5 %collective-permute-start.4 = (bf16[192,1024]{1,0:T(8,128)(2,1)}, bf16[192,1024]{1,0:T(8,128)(2,1)S(1)}, u32[]{:S(2)}, u32[]{:S(2)}) collective-permute-start(bf16[192,1024]{1,0:T(8,128)(2,1)} %pool.1.refs_0_), channel_id=1, source_target_pairs={{0,24},{1,129},{2,26},{3,131},{4,12},{5,133},{6,14},{7,135},{8,0},... | collective-permute-start | bytes 1179656 | tf_op jit(solution)/shard_map/ppermute | solution.py:28
  12.7 3.7 %collective-permute-done.refs_1_.refs_0_ = bf16[192,1024]{1,0:T(8,128)(2,1)S(1)} collective-permute-done((bf16[192,1024]{1,0:T(8,128)(2,1)}, bf16[192,1024]{1,0:T(8,128)(2,1)S(1)}, u32[]{:S(2)}, u32[]{:S(2)}) %collective-permute-start) | collective-permute-done | bytes 393248 | tf_op jit(solution)/shard_map/ppermute | solution.py:28
  16.4 4.9 %collective-permute-start.9 = (bf16[192,1024]{1,0:T(8,128)(2,1)S(1)}, bf16[192,1024]{1,0:T(8,128)(2,1)S(1)}, u32[]{:S(2)}, u32[]{:S(2)}) collective-permute-start(bf16[192,1024]{1,0:T(8,128)(2,1)S(1)} %collective-permute-done.refs_1_.refs_0_), channel_id=1, source_target_pairs={{0,4},{1,65},{2,6},{3,67},{4,0},{5,69},{6,2},{7,71},{8,12},{9,73},... | collective-permute-start | bytes 1179656 | tf_op jit(solution)/shard_map/ppermute | solution.py:28
  21.3 0.5 collective-permute-start.8
  21.8 5.2 %collective-permute-done.9.refs_1_.refs_0_ = bf16[192,1024]{1,0:T(8,128)(2,1)S(1)} collective-permute-done((bf16[192,1024]{1,0:T(8,128)(2,1)S(1)}, bf16[192,1024]{1,0:T(8,128)(2,1)S(1)}, u32[]{:S(2)}, u32[]{:S(2)}) %collective-permute-start.9) | collective-permute-done | bytes 393248 | tf_op jit(solution)/shard_map/ppermute | solution.py:28
  27.0 5.0 %collective-permute-start.5 = (bf16[192,1024]{1,0:T(8,128)(2,1)S(1)}, bf16[192,1024]{1,0:T(8,128)(2,1)S(1)}, u32[]{:S(2)}, u32[]{:S(2)}) collective-permute-start(bf16[192,1024]{1,0:T(8,128)(2,1)S(1)} %collective-permute-done.4.refs_2_.refs_1_), channel_id=1, source_target_pairs={{0,28},{1,33},{2,30},{3,35},{4,8},{5,37},{6,10},{7,39},{8,4},{9,41... | collective-permute-start | bytes 1179656 | tf_op jit(solution)/shard_map/ppermute | solution.py:28
  32.1 1.5 %collective-permute-start.1 = (bf16[192,1024]{1,0:T(8,128)(2,1)}, bf16[192,1024]{1,0:T(8,128)(2,1)S(1)}, u32[]{:S(2)}, u32[]{:S(2)}) collective-permute-start(bf16[192,1024]{1,0:T(8,128)(2,1)} %pool.1.refs_0_), channel_id=1, source_target_pairs={{0,4},{1,65},{2,6},{3,67},{4,8},{5,69},{6,10},{7,71},{8,12},{9,73}... | collective-permute-start | bytes 1179656 | tf_op jit(solution)/shard_map/ppermute | solution.py:28
  33.6 1.8 %collective-permute-start.2 = (bf16[192,1024]{1,0:T(8,128)(2,1)}, bf16[192,1024]{1,0:T(8,128)(2,1)S(1)}, u32[]{:S(2)}, u32[]{:S(2)}) collective-permute-start(bf16[192,1024]{1,0:T(8,128)(2,1)} %pool.1.refs_0_), channel_id=1, source_target_pairs={{0,28},{1,193},{2,30},{3,195},{4,0},{5,197},{6,2},{7,199},{8,4},{9... | collective-permute-start | bytes 1179656 | tf_op jit(solution)/shard_map/ppermute | solution.py:28
  35.4 1.0 %copy-done = bf16[192,1024]{1,0:T(8,128)(2,1)S(1)} copy-done((bf16[192,1024]{1,0:T(8,128)(2,1)S(1)}, bf16[192,1024]{1,0:T(8,128)(2,1)}, u32[]{:S(2)}) %copy-start) | copy-done | bytes 393240
  36.5 2.6 %shard_map.46 = (f32[192,1024]{1,0:T(8,128)S(1)}, f32[192,1024]{1,0:T(8,128)S(1)}, f32[192,1024]{1,0:T(8,128)S(1)}) custom-call(f32[4,768]{1,0:T(4,128)S(1)} %broadcast_in_dim.6.par_ref, s32[1536,128]{1,0:T(8,128)S(1)} %broadcast_in_dim.7.row_ref, s32[1,1536]{1,0:T(1,128)S(1)} %broadcast_in_dim.8.col_ref, bf16[192,1024]{1,0:T(8,128)(2,1)S(1)} %copy-done, ...), custom_call_target="tpu_custom_call" | custom-call | flops 1811939328 | bytes 1572864 | tf_op jit(solution)/shard_map/pallas_call | solution.py:102
  39.1 2.5 %collective-permute-done.5.refs_2_.refs_1_ = bf16[192,1024]{1,0:T(8,128)(2,1)S(1)} collective-permute-done((bf16[192,1024]{1,0:T(8,128)(2,1)S(1)}, bf16[192,1024]{1,0:T(8,128)(2,1)S(1)}, u32[]{:S(2)}, u32[]{:S(2)}) %collective-permute-start.5) | collective-permute-done | bytes 393248 | tf_op jit(solution)/shard_map/ppermute | solution.py:28
  42.1 2.6 %shard_map.47 = (f32[192,1024]{1,0:T(8,128)S(1)}, f32[192,1024]{1,0:T(8,128)S(1)}, f32[192,1024]{1,0:T(8,128)S(1)}) custom-call(f32[4,768]{1,0:T(4,128)S(1)} %broadcast_in_dim.6.par_ref, s32[1536,128]{1,0:T(8,128)S(1)} %broadcast_in_dim.7.row_ref, s32[1,1536]{1,0:T(1,128)S(1)} %broadcast_in_dim.8.col_ref, ...), custom_call_target="tpu_custom_call" | custom-call | flops 1811939328 | bytes 1572864 | tf_op jit(solution)/shard_map/pallas_call | solution.py:102
  44.7 1.6 %collective-permute-done.1.refs_0_ = bf16[192,1024]{1,0:T(8,128)(2,1)S(1)} collective-permute-done((bf16[192,1024]{1,0:T(8,128)(2,1)}, bf16[192,1024]{1,0:T(8,128)(2,1)S(1)}, u32[]{:S(2)}, u32[]{:S(2)}) %collective-permute-start.1) | collective-permute-done | bytes 393248 | tf_op jit(solution)/shard_map/ppermute | solution.py:28
  46.3 0.5 collective-permute-start.14
  46.8 0.5 collective-permute-start.12
  47.3 1.9 %shard_map.48 = (f32[192,1024]{1,0:T(8,128)S(1)}, f32[192,1024]{1,0:T(8,128)S(1)}) custom-call(f32[4,768]{1,0:T(4,128)S(1)} %broadcast_in_dim.6.par_ref, s32[1536,128]{1,0:T(8,128)S(1)} %broadcast_in_dim.7.row_ref, s32[1,1536]{1,0:T(1,128)S(1)} %broadcast_in_dim.8.col_ref, bf16[192,1024]{1,0:T(8,128)(2,1)S(1)} %collective-permute-done.1.refs_0_, ...), custom_call_target="tpu_custom_call" | custom-call | flops 1207959552 | bytes 1572864 | tf_op jit(solution)/shard_map/pallas_call | solution.py:102
  49.2 0.5 collective-permute-done.12.refs_2_.refs_3_
  49.7 1.2 %shard_map.49 = bf16[192,1024]{1,0:T(8,128)(2,1)S(1)} custom-call(f32[4,768]{1,0:T(4,128)S(1)} %broadcast_in_dim.6.par_ref, s32[1536,128]{1,0:T(8,128)S(1)} %broadcast_in_dim.7.row_ref, s32[1,1536]{1,0:T(1,128)S(1)} %broadcast_in_dim.8.col_ref, bf16[192,1024]{1,0:T(8,128)(2,1)S(1)} %collective-permute-done.3.refs_0_, ...), custom_call_target="tpu_custom_call" | custom-call | flops 603979776 | bytes 1572864 | tf_op jit(solution)/shard_map/pallas_call | solution.py:102
  50.9 1.9 %shard_map.50 = (bf16[192,1024]{1,0:T(8,128)(2,1)S(1)}, bf16[192,1024]{1,0:T(8,128)(2,1)S(1)}) custom-call(f32[4,768]{1,0:T(4,128)S(1)} %broadcast_in_dim.6.par_ref, s32[1536,128]{1,0:T(8,128)S(1)} %broadcast_in_dim.7.row_ref, s32[1,1536]{1,0:T(1,128)S(1)} %broadcast_in_dim.8.col_ref, bf16[192,1024]{1,0:T(8,128)(2,1)S(1)} %collective-permute-done.9.refs_1_.refs_0_, ...), custom_call_target="tpu_custom_call" | custom-call | flops 1207959552 | bytes 1572864 | tf_op jit(solution)/shard_map/pallas_call | solution.py:102
  52.9 4.7 %collective-permute-start.18 = (bf16[192,1024]{1,0:T(8,128)(2,1)S(1)}, bf16[192,1024]{1,0:T(8,128)(2,1)S(1)}, u32[]{:S(2)}, u32[]{:S(2)}) collective-permute-start(bf16[192,1024]{1,0:T(8,128)(2,1)S(1)} %shard_map.49), channel_id=1, source_target_pairs={{8,0},{193,1},{10,2},{195,3},{28,4},{197,5},{30,6},{199,7},{16,8},... | collective-permute-start | bytes 1179656 | tf_op jit(solution)/shard_map/ppermute | solution.py:28
  57.6 1.9 %shard_map.51 = (bf16[192,1024]{1,0:T(8,128)(2,1)S(1)}, bf16[192,1024]{1,0:T(8,128)(2,1)S(1)}) custom-call(f32[4,768]{1,0:T(4,128)S(1)} %broadcast_in_dim.6.par_ref, s32[1536,128]{1,0:T(8,128)S(1)} %broadcast_in_dim.7.row_ref, s32[1,1536]{1,0:T(1,128)S(1)} %broadcast_in_dim.8.col_ref, bf16[192,1024]{1,0:T(8,128)(2,1)S(1)} %collective-permute-done.1.refs_0_, ...), custom_call_target="tpu_custom_call" | custom-call | flops 1207959552 | bytes 1572864 | tf_op jit(solution)/shard_map/pallas_call | solution.py:102
  59.4 3.3 %collective-permute-start.16 = (bf16[192,1024]{1,0:T(8,128)(2,1)S(1)}, bf16[192,1024]{1,0:T(8,128)(2,1)S(1)}, u32[]{:S(2)}, u32[]{:S(2)}) collective-permute-start(bf16[192,1024]{1,0:T(8,128)(2,1)S(1)} %get-tuple-element.80), channel_id=1, source_target_pairs={{4,0},{65,1},{6,2},{67,3},{8,4},{69,5},{10,6},{71,7},{12,8},{73,9}... | collective-permute-start | bytes 1179656 | tf_op jit(solution)/shard_map/ppermute | solution.py:28
  62.8 1.9 %shard_map.52 = (f32[192,1024]{1,0:T(8,128)S(1)}, f32[192,1024]{1,0:T(8,128)S(1)}) custom-call(f32[4,768]{1,0:T(4,128)S(1)} %broadcast_in_dim.6.par_ref, s32[1536,128]{1,0:T(8,128)S(1)} %broadcast_in_dim.7.row_ref, s32[1,1536]{1,0:T(1,128)S(1)} %broadcast_in_dim.8.col_ref, bf16[192,1024]{1,0:T(8,128)(2,1)S(1)} %collective-permute-done.refs_1_.refs_0_, ...), custom_call_target="tpu_custom_call" | custom-call | flops 1207959552 | bytes 1572864 | tf_op jit(solution)/shard_map/pallas_call | solution.py:102
  65.0 2.8 %collective-permute-start.20 = (bf16[192,1024]{1,0:T(8,128)(2,1)S(1)}, bf16[192,1024]{1,0:T(8,128)(2,1)S(1)}, u32[]{:S(2)}, u32[]{:S(2)}) collective-permute-start(bf16[192,1024]{1,0:T(8,128)(2,1)S(1)} %add_convert_fusion), channel_id=1, source_target_pairs={{8,0},{33,1},{10,2},{35,3},{28,4},{37,5},{30,6},{39,7},{16,8},{41,... | collective-permute-start | bytes 1179656 | tf_op jit(solution)/shard_map/ppermute | solution.py:28
  68.2 1.2 %shard_map.53 = f32[192,1024]{1,0:T(8,128)S(1)} custom-call(f32[4,768]{1,0:T(4,128)S(1)} %broadcast_in_dim.6.par_ref, s32[1536,128]{1,0:T(8,128)S(1)} %broadcast_in_dim.7.row_ref, s32[1,1536]{1,0:T(1,128)S(1)} %broadcast_in_dim.8.col_ref, bf16[192,1024]{1,0:T(8,128)(2,1)S(1)} %copy-done.1, bf16[192,1024]{1,0:T(8,128)(2,1)S(1)} %collective-permute-done.11.refs_1_.refs_2_, ...), custom_call_target="tpu_custom_call" | custom-call | flops 603979776 | bytes 1572864 | tf_op jit(solution)/shard_map/pallas_call | solution.py:102
  69.5 1.9 %collective-permute-done.16 = bf16[192,1024]{1,0:T(8,128)(2,1)S(1)} collective-permute-done((bf16[192,1024]{1,0:T(8,128)(2,1)S(1)}, bf16[192,1024]{1,0:T(8,128)(2,1)S(1)}, u32[]{:S(2)}, u32[]{:S(2)}) %collective-permute-start.16) | collective-permute-done | bytes 393248 | tf_op jit(solution)/shard_map/ppermute | solution.py:28
  72.0 7.8 %collective-permute-done.20 = bf16[192,1024]{1,0:T(8,128)(2,1)S(1)} collective-permute-done((bf16[192,1024]{1,0:T(8,128)(2,1)S(1)}, bf16[192,1024]{1,0:T(8,128)(2,1)S(1)}, u32[]{:S(2)}, u32[]{:S(2)}) %collective-permute-start.20) | collective-permute-done | bytes 393248 | tf_op jit(solution)/shard_map/ppermute | solution.py:28
  79.8 1.4 %collective-permute-done.21 = bf16[192,1024]{1,0:T(8,128)(2,1)S(1)} collective-permute-done((bf16[192,1024]{1,0:T(8,128)(2,1)S(1)}, bf16[192,1024]{1,0:T(8,128)(2,1)S(1)}, u32[]{:S(2)}, u32[]{:S(2)}) %collective-permute-start.21) | collective-permute-done | bytes 393248 | tf_op jit(solution)/shard_map/ppermute | solution.py:28
  81.2 1.0 %add_bitcast_fusion = f32[1,192,1024]{2,1,0:T(8,128)} fusion(bf16[192,1024]{1,0:T(8,128)(2,1)S(1)} %collective-permute-done.21, f32[192,1024]{1,0:T(8,128)S(1)} %convert_add_fusion, bf16[192,1024]{1,0:T(8,128)(2,1)S(1)} %collective-permute-done.20), kind=kLoop, calls=%fused_computation | loop fusion | flops 786432 | bytes 2359296 | tf_op jit(solution)/shard_map/reshape | solution.py:189
  (40 shorter events, 2.6 us)
Async XLA Ops:
  0.0 8.8 %copy-start.3 = (f32[2]{0:T(128)S(1)}, f32[2]{0:T(128)}, u32[]{:S(2)}) copy-start(f32[2]{0:T(128)} %param.6) | copy-start | bytes 28
  0.0 8.8 %copy-start.2 = (f32[2]{0:T(128)S(1)}, f32[2]{0:T(128)}, u32[]{:S(2)}) copy-start(f32[2]{0:T(128)} %param.7) | copy-start | bytes 28
  4.1 12.3 %collective-permute-start = (bf16[192,1024]{1,0:T(8,128)(2,1)}, bf16[192,1024]{1,0:T(8,128)(2,1)S(1)}, u32[]{:S(2)}, u32[]{:S(2)}) collective-permute-start(bf16[192,1024]{1,0:T(8,128)(2,1)} %pool.1.refs_0_), channel_id=1, source_target_pairs={{0,8},{1,33},{2,10},{3,35},{4,28},{5,37},{6,30},{7,39},{8,16},{9,4... | collective-permute-start | bytes 1179656 | tf_op jit(solution)/shard_map/ppermute | solution.py:28
  9.2 12.1 %collective-permute-start.4 = (bf16[192,1024]{1,0:T(8,128)(2,1)}, bf16[192,1024]{1,0:T(8,128)(2,1)S(1)}, u32[]{:S(2)}, u32[]{:S(2)}) collective-permute-start(bf16[192,1024]{1,0:T(8,128)(2,1)} %pool.1.refs_0_), channel_id=1, source_target_pairs={{0,24},{1,129},{2,26},{3,131},{4,12},{5,133},{6,14},{7,135},{8,0},... | collective-permute-start | bytes 1179656 | tf_op jit(solution)/shard_map/ppermute | solution.py:28
  16.4 10.6 %collective-permute-start.9 = (bf16[192,1024]{1,0:T(8,128)(2,1)S(1)}, bf16[192,1024]{1,0:T(8,128)(2,1)S(1)}, u32[]{:S(2)}, u32[]{:S(2)}) collective-permute-start(bf16[192,1024]{1,0:T(8,128)(2,1)S(1)} %collective-permute-done.refs_1_.refs_0_), channel_id=1, source_target_pairs={{0,4},{1,65},{2,6},{3,67},{4,0},{5,69},{6,2},{7,71},{8,12},{9,73},... | collective-permute-start | bytes 1179656 | tf_op jit(solution)/shard_map/ppermute | solution.py:28
  21.3 10.8 %collective-permute-start.6 = (bf16[192,1024]{1,0:T(8,128)(2,1)}, bf16[192,1024]{1,0:T(8,128)(2,1)S(1)}, u32[]{:S(2)}, u32[]{:S(2)}) collective-permute-start(bf16[192,1024]{1,0:T(8,128)(2,1)} %pool.1.refs_0_), channel_id=1, source_target_pairs={{0,1},{1,0},{2,3},{3,2},{4,5},{5,4},{6,7},{7,6},{8,9},{9,8},{10,11... | collective-permute-start | bytes 1179656 | tf_op jit(solution)/shard_map/ppermute | solution.py:32
  21.3 10.8 %collective-permute-start.8 = (bf16[192,1024]{1,0:T(8,128)(2,1)S(1)}, bf16[192,1024]{1,0:T(8,128)(2,1)S(1)}, u32[]{:S(2)}, u32[]{:S(2)}) collective-permute-start(bf16[192,1024]{1,0:T(8,128)(2,1)S(1)} %collective-permute-done.4.refs_2_.refs_1_), channel_id=1, source_target_pairs={{0,1},{1,0},{2,3},{3,2},{4,5},{5,4},{6,7},{7,6},{8,9},{9,8},{10,11... | collective-permute-start | bytes 1179656 | tf_op jit(solution)/shard_map/ppermute | solution.py:32
  21.8 11.8 %collective-permute-start.7 = (bf16[192,1024]{1,0:T(8,128)(2,1)S(1)}, bf16[192,1024]{1,0:T(8,128)(2,1)S(1)}, u32[]{:S(2)}, u32[]{:S(2)}) collective-permute-start(bf16[192,1024]{1,0:T(8,128)(2,1)S(1)} %collective-permute-done.refs_1_.refs_0_), channel_id=1, source_target_pairs={{0,1},{1,0},{2,3},{3,2},{4,5},{5,4},{6,7},{7,6},{8,9},{9,8},{10,11... | collective-permute-start | bytes 1179656 | tf_op jit(solution)/shard_map/ppermute | solution.py:32
  27.0 8.4 %collective-permute-start.10 = (bf16[192,1024]{1,0:T(8,128)(2,1)S(1)}, bf16[192,1024]{1,0:T(8,128)(2,1)S(1)}, u32[]{:S(2)}, u32[]{:S(2)}) collective-permute-start(bf16[192,1024]{1,0:T(8,128)(2,1)S(1)} %collective-permute-done.9.refs_1_.refs_0_), channel_id=1, source_target_pairs={{0,1},{1,0},{2,3},{3,2},{4,5},{5,4},{6,7},{7,6},{8,9},{9,8},{10,11... | collective-permute-start | bytes 1179656 | tf_op jit(solution)/shard_map/ppermute | solution.py:32
  27.0 14.6 %collective-permute-start.5 = (bf16[192,1024]{1,0:T(8,128)(2,1)S(1)}, bf16[192,1024]{1,0:T(8,128)(2,1)S(1)}, u32[]{:S(2)}, u32[]{:S(2)}) collective-permute-start(bf16[192,1024]{1,0:T(8,128)(2,1)S(1)} %collective-permute-done.4.refs_2_.refs_1_), channel_id=1, source_target_pairs={{0,28},{1,33},{2,30},{3,35},{4,8},{5,37},{6,10},{7,39},{8,4},{9,41... | collective-permute-start | bytes 1179656 | tf_op jit(solution)/shard_map/ppermute | solution.py:28
  32.1 10.0 %collective-permute-start.3 = (bf16[192,1024]{1,0:T(8,128)(2,1)S(1)}, bf16[192,1024]{1,0:T(8,128)(2,1)S(1)}, u32[]{:S(2)}, u32[]{:S(2)}) collective-permute-start(bf16[192,1024]{1,0:T(8,128)(2,1)S(1)} %collective-permute-done.refs_1_.refs_0_), channel_id=1, source_target_pairs={{0,8},{1,193},{2,10},{3,195},{4,28},{5,197},{6,30},{7,199},{8,16},... | collective-permute-start | bytes 1179656 | tf_op jit(solution)/shard_map/ppermute | solution.py:28
  32.1 14.2 %collective-permute-start.1 = (bf16[192,1024]{1,0:T(8,128)(2,1)}, bf16[192,1024]{1,0:T(8,128)(2,1)S(1)}, u32[]{:S(2)}, u32[]{:S(2)}) collective-permute-start(bf16[192,1024]{1,0:T(8,128)(2,1)} %pool.1.refs_0_), channel_id=1, source_target_pairs={{0,4},{1,65},{2,6},{3,67},{4,8},{5,69},{6,10},{7,71},{8,12},{9,73}... | collective-permute-start | bytes 1179656 | tf_op jit(solution)/shard_map/ppermute | solution.py:28
  33.6 12.6 %collective-permute-start.2 = (bf16[192,1024]{1,0:T(8,128)(2,1)}, bf16[192,1024]{1,0:T(8,128)(2,1)S(1)}, u32[]{:S(2)}, u32[]{:S(2)}) collective-permute-start(bf16[192,1024]{1,0:T(8,128)(2,1)} %pool.1.refs_0_), channel_id=1, source_target_pairs={{0,28},{1,193},{2,30},{3,195},{4,0},{5,197},{6,2},{7,199},{8,4},{9... | collective-permute-start | bytes 1179656 | tf_op jit(solution)/shard_map/ppermute | solution.py:28
  35.4 1.0 %copy-start = (bf16[192,1024]{1,0:T(8,128)(2,1)S(1)}, bf16[192,1024]{1,0:T(8,128)(2,1)}, u32[]{:S(2)}) copy-start(bf16[192,1024]{1,0:T(8,128)(2,1)} %pool.1.refs_0_) | copy-start | bytes 1179652
  46.3 2.9 %collective-permute-start.13 = (bf16[192,1024]{1,0:T(8,128)(2,1)S(1)}, bf16[192,1024]{1,0:T(8,128)(2,1)S(1)}, u32[]{:S(2)}, u32[]{:S(2)}) collective-permute-start(bf16[192,1024]{1,0:T(8,128)(2,1)S(1)} %collective-permute-done.1.refs_0_), channel_id=1, source_target_pairs={{0,1},{1,0},{2,3},{3,2},{4,5},{5,4},{6,7},{7,6},{8,9},{9,8},{10,11... | collective-permute-start | bytes 1179656 | tf_op jit(solution)/shard_map/ppermute | solution.py:32
  46.3 2.9 %collective-permute-start.14 = (bf16[192,1024]{1,0:T(8,128)(2,1)S(1)}, bf16[192,1024]{1,0:T(8,128)(2,1)S(1)}, u32[]{:S(2)}, u32[]{:S(2)}) collective-permute-start(bf16[192,1024]{1,0:T(8,128)(2,1)S(1)} %collective-permute-done.2.refs_1_), channel_id=1, source_target_pairs={{0,1},{1,0},{2,3},{3,2},{4,5},{5,4},{6,7},{7,6},{8,9},{9,8},{10,11... | collective-permute-start | bytes 1179656 | tf_op jit(solution)/shard_map/ppermute | solution.py:32
  46.8 2.4 %collective-permute-start.11 = (bf16[192,1024]{1,0:T(8,128)(2,1)S(1)}, bf16[192,1024]{1,0:T(8,128)(2,1)S(1)}, u32[]{:S(2)}, u32[]{:S(2)}) collective-permute-start(bf16[192,1024]{1,0:T(8,128)(2,1)S(1)} %collective-permute-done.3.refs_0_), channel_id=1, source_target_pairs={{0,1},{1,0},{2,3},{3,2},{4,5},{5,4},{6,7},{7,6},{8,9},{9,8},{10,11... | collective-permute-start | bytes 1179656 | tf_op jit(solution)/shard_map/ppermute | solution.py:32
  46.8 2.9 %collective-permute-start.12 = (bf16[192,1024]{1,0:T(8,128)(2,1)S(1)}, bf16[192,1024]{1,0:T(8,128)(2,1)S(1)}, u32[]{:S(2)}, u32[]{:S(2)}) collective-permute-start(bf16[192,1024]{1,0:T(8,128)(2,1)S(1)} %collective-permute-done.5.refs_2_.refs_1_), channel_id=1, source_target_pairs={{0,1},{1,0},{2,3},{3,2},{4,5},{5,4},{6,7},{7,6},{8,9},{9,8},{10,11... | collective-permute-start | bytes 1179656 | tf_op jit(solution)/shard_map/ppermute | solution.py:32
  52.8 15.4 %copy-start.1 = (bf16[192,1024]{1,0:T(8,128)(2,1)S(1)}, bf16[192,1024]{1,0:T(8,128)(2,1)}, u32[]{:S(2)}) copy-start(bf16[192,1024]{1,0:T(8,128)(2,1)} %pool.1.refs_0_) | copy-start | bytes 1179652
  52.8 12.1 %collective-permute-start.19 = (bf16[192,1024]{1,0:T(8,128)(2,1)S(1)}, bf16[192,1024]{1,0:T(8,128)(2,1)S(1)}, u32[]{:S(2)}, u32[]{:S(2)}) collective-permute-start(bf16[192,1024]{1,0:T(8,128)(2,1)S(1)} %get-tuple-element.84), channel_id=1, source_target_pairs={{4,0},{65,1},{6,2},{67,3},{0,4},{69,5},{2,6},{71,7},{12,8},{73,9},... | collective-permute-start | bytes 1179656 | tf_op jit(solution)/shard_map/ppermute | solution.py:28
  52.9 12.0 %collective-permute-start.18 = (bf16[192,1024]{1,0:T(8,128)(2,1)S(1)}, bf16[192,1024]{1,0:T(8,128)(2,1)S(1)}, u32[]{:S(2)}, u32[]{:S(2)}) collective-permute-start(bf16[192,1024]{1,0:T(8,128)(2,1)S(1)} %shard_map.49), channel_id=1, source_target_pairs={{8,0},{193,1},{10,2},{195,3},{28,4},{197,5},{30,6},{199,7},{16,8},... | collective-permute-start | bytes 1179656 | tf_op jit(solution)/shard_map/ppermute | solution.py:28
  57.6 10.2 %collective-permute-start.15 = (bf16[192,1024]{1,0:T(8,128)(2,1)S(1)}, bf16[192,1024]{1,0:T(8,128)(2,1)S(1)}, u32[]{:S(2)}, u32[]{:S(2)}) collective-permute-start(bf16[192,1024]{1,0:T(8,128)(2,1)S(1)} %get-tuple-element.77), channel_id=1, source_target_pairs={{28,0},{33,1},{30,2},{35,3},{8,4},{37,5},{10,6},{39,7},{4,8},{41,9... | collective-permute-start | bytes 1179656 | tf_op jit(solution)/shard_map/ppermute | solution.py:28
  59.4 11.9 %collective-permute-start.16 = (bf16[192,1024]{1,0:T(8,128)(2,1)S(1)}, bf16[192,1024]{1,0:T(8,128)(2,1)S(1)}, u32[]{:S(2)}, u32[]{:S(2)}) collective-permute-start(bf16[192,1024]{1,0:T(8,128)(2,1)S(1)} %get-tuple-element.80), channel_id=1, source_target_pairs={{4,0},{65,1},{6,2},{67,3},{8,4},{69,5},{10,6},{71,7},{12,8},{73,9}... | collective-permute-start | bytes 1179656 | tf_op jit(solution)/shard_map/ppermute | solution.py:28
  62.8 9.0 %collective-permute-start.17 = (bf16[192,1024]{1,0:T(8,128)(2,1)S(1)}, bf16[192,1024]{1,0:T(8,128)(2,1)S(1)}, u32[]{:S(2)}, u32[]{:S(2)}) collective-permute-start(bf16[192,1024]{1,0:T(8,128)(2,1)S(1)} %get-tuple-element.81), channel_id=1, source_target_pairs={{28,0},{193,1},{30,2},{195,3},{0,4},{197,5},{2,6},{199,7},{4,8},{2... | collective-permute-start | bytes 1179656 | tf_op jit(solution)/shard_map/ppermute | solution.py:28
  65.0 14.7 %collective-permute-start.20 = (bf16[192,1024]{1,0:T(8,128)(2,1)S(1)}, bf16[192,1024]{1,0:T(8,128)(2,1)S(1)}, u32[]{:S(2)}, u32[]{:S(2)}) collective-permute-start(bf16[192,1024]{1,0:T(8,128)(2,1)S(1)} %add_convert_fusion), channel_id=1, source_target_pairs={{8,0},{33,1},{10,2},{35,3},{28,4},{37,5},{30,6},{39,7},{16,8},{41,... | collective-permute-start | bytes 1179656 | tf_op jit(solution)/shard_map/ppermute | solution.py:28
  67.9 13.3 %collective-permute-start.21 = (bf16[192,1024]{1,0:T(8,128)(2,1)S(1)}, bf16[192,1024]{1,0:T(8,128)(2,1)S(1)}, u32[]{:S(2)}, u32[]{:S(2)}) collective-permute-start(bf16[192,1024]{1,0:T(8,128)(2,1)S(1)} %add_convert_fusion.1), channel_id=1, source_target_pairs={{24,0},{129,1},{26,2},{131,3},{12,4},{133,5},{14,6},{135,7},{0,8},... | collective-permute-start | bytes 1179656 | tf_op jit(solution)/shard_map/ppermute | solution.py:28

commit v7 on v2

--- a/solution.py
+++ b/solution.py
@@ -160,14 +160,18 @@
     rows[5], rows[6], rows[7], h0, h1, h2, h3, h4 = lax.optimization_barrier((rows[5], rows[6], rows[7], h0, h1, h2, h3, h4))
     cols += [partner(rows[k]) for k in (5, 6, 7)]
     h7, h5, h6 = grads(state, (7, 5, 6), 0, 1, None, (f32,) * 3)
-    g7, g5, g6 = grads(state, (7, 5, 6), 4, 1, (h7, h5, h6), (bf16,) * 3)
+    (g7,) = grads(state, (7,), 4, 1, (h7,), (bf16,))
+    rows[5], g7 = lax.optimization_barrier((rows[5], g7))
     r7 = send(g7, BACK[7])
+    g5, g6 = grads(state, (5, 6), 4, 1, (h5, h6), (bf16,) * 2)
+    rows[3], g5, g6 = lax.optimization_barrier((rows[3], g5, g6))
     r5 = send(g5, BACK[5])
     r6 = send(g6, BACK[6])
-    rows[1], g6 = lax.optimization_barrier((rows[1], g6))
-    g1, g2, g3, g4 = grads(state, (1, 2, 3, 4), 4, 1, (h1, h2, h3, h4), (f32, f32, bf16, bf16))
+    g3, g4 = grads(state, (3, 4), 4, 1, (h3, h4), (bf16,) * 2)
+    rows[1], g3, g4 = lax.optimization_barrier((rows[1], g3, g4))
     r3 = send(g3, BACK[3])
     r4 = send(g4, BACK[4])
+    g1, g2 = grads(state, (1, 2), 4, 1, (h1, h2), (f32,) * 2)
     s1 = (g1 + jnp.where(turn, 0.0, r7.astype(f32)) + r5.astype(f32)).astype(bf16)
     s1, r7 = lax.optimization_barrier((s1, r7))
     r1 = send(s1, BACK[1])

time: 77.8 us -> 79.1 us (1.017)
  the two profiles are of different devices: /device:TPU:28 before, /device:TPU:84 now
where the time goes in v7:
time: 79.1 us; the launch traced here: 78.9 us
  waiting for transfers between devices  29.1 us (37%)
  starting transfers between devices  23.1 us (29%)
  Pallas kernels  22.9 us (29%)
  local copies, waits for them, and re-layouts  1.85 us (2%)
  other arithmetic  1.7 us (2%)
    ppermute x14, waiting for transfers between devices, send(): return lax.ppermute(v, AXES, pairs)  29.1 us
    ppermute x14, starting transfers between devices, send(): return lax.ppermute(v, AXES, pairs)  22.2 us
    pallas_call x8, Pallas kernels, grads(): pl.pallas_call(functools.partial(grad_kernel, slots, first_col, groups, s...  18.9 us
    pallas_call x1, Pallas kernels, pool(): pl.pallas_call(pool_kernel, in_specs=[pl.BlockSpec(memory_space=pltpu.HBM...  4.03 us
  transfers between devices with their start and end apart: 22, of which 8 were waited for; matrix products, arithmetic and copies ran while one was open for 1% of the time, Pallas kernels for 20%

profile of v7, /device:TPU:84, one launch (start us, length us, event | category | flops | bytes accessed | tf_op | source)
XLA Modules:
  0.0 78.9 jit_solution(16063322602821889229)
XLA Ops:
  0.0 1.3 %fusion = (s32[192]{0:T(256)S(1)}, s32[192]{0:T(256)S(1)}, s32[192]{0:T(256)S(1)}, s32[192]{0:T(256)S(1)}, s32[192]{0:T(256)S(1)}, /*index=5*/s32[192]{0:T(256)S...) fusion(s32[12288]{0:T(1024)} %param.5, ...), kind=kLoop, calls=%fused_computation.6 | loop fusion | bytes 24640 | tf_op jit(solution)/shard_map/dynamic_slice | solution.py:139
  1.4 4.0 %pool.1.refs_0_ = bf16[192,1024]{1,0:T(8,128)(2,1)} custom-call(bf16[192,16,1024]{2,1,0:T(8,128)(2,1)} %bitcast.3), custom_call_target="tpu_custom_call" | custom-call | flops 6291456 | bytes 6291456 | tf_op jit(solution)/shard_map/pool/pallas_call | solution.py:61
  6.0 1.9 %collective-permute-start.1 = (bf16[192,1024]{1,0:T(8,128)(2,1)}, bf16[192,1024]{1,0:T(8,128)(2,1)S(1)}, u32[]{:S(2)}, u32[]{:S(2)}) collective-permute-start(bf16[192,1024]{1,0:T(8,128)(2,1)} %pool.1.refs_0_), channel_id=1, source_target_pairs={{0,4},{1,65},{2,6},{3,67},{4,8},{5,69},{6,10},{7,71},{8,12},{9,73}... | collective-permute-start | bytes 1179656 | tf_op jit(solution)/shard_map/ppermute | solution.py:28
  7.9 3.6 %collective-permute-start = (bf16[192,1024]{1,0:T(8,128)(2,1)}, bf16[192,1024]{1,0:T(8,128)(2,1)S(1)}, u32[]{:S(2)}, u32[]{:S(2)}) collective-permute-start(bf16[192,1024]{1,0:T(8,128)(2,1)} %pool.1.refs_0_), channel_id=1, source_target_pairs={{0,8},{1,33},{2,10},{3,35},{4,12},{5,37},{6,14},{7,39},{8,16},{9,4... | collective-permute-start | bytes 1179656 | tf_op jit(solution)/shard_map/ppermute | solution.py:28
  11.5 1.0 %collective-permute-start.6 = (bf16[192,1024]{1,0:T(8,128)(2,1)}, bf16[192,1024]{1,0:T(8,128)(2,1)S(1)}, u32[]{:S(2)}, u32[]{:S(2)}) collective-permute-start(bf16[192,1024]{1,0:T(8,128)(2,1)} %pool.1.refs_0_), channel_id=1, source_target_pairs={{0,28},{1,193},{2,30},{3,195},{4,0},{5,197},{6,2},{7,199},{8,4},{9... | collective-permute-start | bytes 1179656 | tf_op jit(solution)/shard_map/ppermute | solution.py:28
  12.5 4.9 %collective-permute-done.1.refs_1_.refs_0_ = bf16[192,1024]{1,0:T(8,128)(2,1)S(1)} collective-permute-done((bf16[192,1024]{1,0:T(8,128)(2,1)}, bf16[192,1024]{1,0:T(8,128)(2,1)S(1)}, u32[]{:S(2)}, u32[]{:S(2)}) %collective-permute-start.1) | collective-permute-done | bytes 393248 | tf_op jit(solution)/shard_map/ppermute | solution.py:28
  17.4 4.6 %collective-permute-done.refs_0_ = bf16[192,1024]{1,0:T(8,128)(2,1)S(1)} collective-permute-done((bf16[192,1024]{1,0:T(8,128)(2,1)}, bf16[192,1024]{1,0:T(8,128)(2,1)S(1)}, u32[]{:S(2)}, u32[]{:S(2)}) %collective-permute-start) | collective-permute-done | bytes 393248 | tf_op jit(solution)/shard_map/ppermute | solution.py:28
  22.0 2.3 %collective-permute-done.3.refs_1_ = bf16[192,1024]{1,0:T(8,128)(2,1)S(1)} collective-permute-done((bf16[192,1024]{1,0:T(8,128)(2,1)}, bf16[192,1024]{1,0:T(8,128)(2,1)S(1)}, u32[]{:S(2)}, u32[]{:S(2)}) %collective-permute-start.3) | collective-permute-done | bytes 393248 | tf_op jit(solution)/shard_map/ppermute | solution.py:28
  24.4 2.9 %collective-permute-start.5 = (bf16[192,1024]{1,0:T(8,128)(2,1)S(1)}, bf16[192,1024]{1,0:T(8,128)(2,1)S(1)}, u32[]{:S(2)}, u32[]{:S(2)}) collective-permute-start(bf16[192,1024]{1,0:T(8,128)(2,1)S(1)} %broadcast_select_fusion), channel_id=1, source_target_pairs={{0,8},{1,193},{2,10},{3,195},{4,28},{5,197},{6,30},{7,199},{8,16},... | collective-permute-start | bytes 1179656 | tf_op jit(solution)/shard_map/ppermute | solution.py:28
  27.2 1.2 %collective-permute-done.6.refs_2_.refs_1_ = bf16[192,1024]{1,0:T(8,128)(2,1)S(1)} collective-permute-done((bf16[192,1024]{1,0:T(8,128)(2,1)}, bf16[192,1024]{1,0:T(8,128)(2,1)S(1)}, u32[]{:S(2)}, u32[]{:S(2)}) %collective-permute-start.6) | collective-permute-done | bytes 393248 | tf_op jit(solution)/shard_map/ppermute | solution.py:28
  28.4 2.2 %collective-permute-start.2 = (bf16[192,1024]{1,0:T(8,128)(2,1)S(1)}, bf16[192,1024]{1,0:T(8,128)(2,1)S(1)}, u32[]{:S(2)}, u32[]{:S(2)}) collective-permute-start(bf16[192,1024]{1,0:T(8,128)(2,1)S(1)} %collective-permute-done.refs_0_), channel_id=1, source_target_pairs={{0,4},{1,65},{2,6},{3,67},{4,8},{5,69},{6,10},{7,71},{8,12},{9,73}... | collective-permute-start | bytes 1179656 | tf_op jit(solution)/shard_map/ppermute | solution.py:28
  30.9 3.1 %shard_map.47 = (f32[192,1024]{1,0:T(8,128)S(1)}, f32[192,1024]{1,0:T(8,128)S(1)}) custom-call(f32[4,768]{1,0:T(4,128)S(1)} %broadcast_in_dim.11.par_ref, s32[1536,128]{1,0:T(8,128)S(1)} %broadcast_in_dim.22.row_ref, s32[1,1536]{1,0:T(1,128)S(1)} %broadcast_in_dim.23.col_ref, bf16[192,1024]{1,0:T(8,128)(2,1)S(1)} %collective-permute-done.refs_0_, ...), custom_call_target="tpu_custom_call" | custom-call | flops 1207959552 | bytes 1572864 | tf_op jit(solution)/shard_map/pallas_call | solution.py:102
  34.0 3.9 %shard_map.46 = (f32[192,1024]{1,0:T(8,128)S(1)}, f32[192,1024]{1,0:T(8,128)S(1)}, f32[192,1024]{1,0:T(8,128)S(1)}) custom-call(f32[4,768]{1,0:T(4,128)S(1)} %broadcast_in_dim.11.par_ref, s32[1536,128]{1,0:T(8,128)S(1)} %broadcast_in_dim.22.row_ref, s32[1,1536]{1,0:T(1,128)S(1)} %broadcast_in_dim.23.col_ref, bf16[192,1024]{1,0:T(8,128)(2,1)S(1)} %copy-done, ...), custom_call_target="tpu_custom_call" | custom-call | flops 1811939328 | bytes 1572864 | tf_op jit(solution)/shard_map/pallas_call | solution.py:102
  37.9 0.5 collective-permute-done.4.refs_2_.refs_1_
  38.5 0.4 collective-permute-start.13
  39.0 3.9 %shard_map.48 = (f32[192,1024]{1,0:T(8,128)S(1)}, f32[192,1024]{1,0:T(8,128)S(1)}, f32[192,1024]{1,0:T(8,128)S(1)}) custom-call(f32[4,768]{1,0:T(4,128)S(1)} %broadcast_in_dim.11.par_ref, s32[1536,128]{1,0:T(8,128)S(1)} %broadcast_in_dim.22.row_ref, s32[1,1536]{1,0:T(1,128)S(1)} %broadcast_in_dim.23.col_ref, ...), custom_call_target="tpu_custom_call" | custom-call | flops 1811939328 | bytes 1572864 | tf_op jit(solution)/shard_map/pallas_call | solution.py:102
  42.9 1.2 %shard_map.49 = bf16[192,1024]{1,0:T(8,128)(2,1)S(1)} custom-call(f32[4,768]{1,0:T(4,128)S(1)} %broadcast_in_dim.11.par_ref, s32[1536,128]{1,0:T(8,128)S(1)} %broadcast_in_dim.22.row_ref, s32[1,1536]{1,0:T(1,128)S(1)} %broadcast_in_dim.23.col_ref, bf16[192,1024]{1,0:T(8,128)(2,1)S(1)} %collective-permute-done.5.refs_0_, ...), custom_call_target="tpu_custom_call" | custom-call | flops 603979776 | bytes 1572864 | tf_op jit(solution)/shard_map/pallas_call | solution.py:102
  44.1 1.9 %shard_map.50 = (bf16[192,1024]{1,0:T(8,128)(2,1)S(1)}, bf16[192,1024]{1,0:T(8,128)(2,1)S(1)}) custom-call(f32[4,768]{1,0:T(4,128)S(1)} %broadcast_in_dim.11.par_ref, s32[1536,128]{1,0:T(8,128)S(1)} %broadcast_in_dim.22.row_ref, s32[1,1536]{1,0:T(1,128)S(1)} %broadcast_in_dim.23.col_ref, bf16[192,1024]{1,0:T(8,128)(2,1)S(1)} %collective-permute-done.2.refs_1_.refs_0_, ...), custom_call_target="tpu_custom_call" | custom-call | flops 1207959552 | bytes 1572864 | tf_op jit(solution)/shard_map/pallas_call | solution.py:102
  46.0 1.1 %collective-permute-start.16 = (bf16[192,1024]{1,0:T(8,128)(2,1)S(1)}, bf16[192,1024]{1,0:T(8,128)(2,1)S(1)}, u32[]{:S(2)}, u32[]{:S(2)}) collective-permute-start(bf16[192,1024]{1,0:T(8,128)(2,1)S(1)} %get-tuple-element.71), channel_id=1, source_target_pairs={{0,28},{1,193},{2,30},{3,195},{4,0},{5,197},{6,2},{7,199},{8,4},{9... | collective-permute-start | bytes 1179656 | tf_op jit(solution)/shard_map/ppermute | solution.py:28
  47.1 3.7 %collective-permute-start.15 = (bf16[192,1024]{1,0:T(8,128)(2,1)S(1)}, bf16[192,1024]{1,0:T(8,128)(2,1)S(1)}, u32[]{:S(2)}, u32[]{:S(2)}) collective-permute-start(bf16[192,1024]{1,0:T(8,128)(2,1)S(1)} %shard_map.49), channel_id=1, source_target_pairs={{0,24},{1,65},{2,26},{3,67},{4,12},{5,69},{6,14},{7,71},{8,0},{9,7... | collective-permute-start | bytes 1179656 | tf_op jit(solution)/shard_map/ppermute | solution.py:28
  50.8 0.8 collective-permute-start.17
  51.5 1.9 %shard_map.51 = (bf16[192,1024]{1,0:T(8,128)(2,1)S(1)}, bf16[192,1024]{1,0:T(8,128)(2,1)S(1)}) custom-call(f32[4,768]{1,0:T(4,128)S(1)} %broadcast_in_dim.11.par_ref, s32[1536,128]{1,0:T(8,128)S(1)} %broadcast_in_dim.22.row_ref, s32[1,1536]{1,0:T(1,128)S(1)} %broadcast_in_dim.23.col_ref, bf16[192,1024]{1,0:T(8,128)(2,1)S(1)} %collective-permute-done.1.refs_1_.refs_0_, ...), custom_call_target="tpu_custom_call" | custom-call | flops 1207959552 | bytes 1572864 | tf_op jit(solution)/shard_map/pallas_call | solution.py:102
  53.4 1.3 %collective-permute-start.18 = (bf16[192,1024]{1,0:T(8,128)(2,1)S(1)}, bf16[192,1024]{1,0:T(8,128)(2,1)S(1)}, u32[]{:S(2)}, u32[]{:S(2)}) collective-permute-start(bf16[192,1024]{1,0:T(8,128)(2,1)S(1)} %get-tuple-element.76), channel_id=1, source_target_pairs={{0,28},{1,193},{2,30},{3,195},{4,0},{5,197},{6,2},{7,199},{8,4},{9... | collective-permute-start | bytes 1179656 | tf_op jit(solution)/shard_map/ppermute | solution.py:28
  54.7 0.8 collective-permute-start.19
  55.5 1.9 %shard_map.52 = (f32[192,1024]{1,0:T(8,128)S(1)}, f32[192,1024]{1,0:T(8,128)S(1)}) custom-call(f32[4,768]{1,0:T(4,128)S(1)} %broadcast_in_dim.11.par_ref, s32[1536,128]{1,0:T(8,128)S(1)} %broadcast_in_dim.22.row_ref, s32[1,1536]{1,0:T(1,128)S(1)} %broadcast_in_dim.23.col_ref, bf16[192,1024]{1,0:T(8,128)(2,1)S(1)} %collective-permute-done.refs_0_, ...), custom_call_target="tpu_custom_call" | custom-call | flops 1207959552 | bytes 1572864 | tf_op jit(solution)/shard_map/pallas_call | solution.py:102
  57.4 4.0 %collective-permute-done.15 = bf16[192,1024]{1,0:T(8,128)(2,1)S(1)} collective-permute-done((bf16[192,1024]{1,0:T(8,128)(2,1)S(1)}, bf16[192,1024]{1,0:T(8,128)(2,1)S(1)}, u32[]{:S(2)}, u32[]{:S(2)}) %collective-permute-start.15) | collective-permute-done | bytes 393248 | tf_op jit(solution)/shard_map/ppermute | solution.py:28
  61.8 2.7 %collective-permute-start.21 = (bf16[192,1024]{1,0:T(8,128)(2,1)S(1)}, bf16[192,1024]{1,0:T(8,128)(2,1)S(1)}, u32[]{:S(2)}, u32[]{:S(2)}) collective-permute-start(bf16[192,1024]{1,0:T(8,128)(2,1)S(1)} %add_convert_fusion), channel_id=1, source_target_pairs={{0,8},{1,129},{2,10},{3,131},{4,12},{5,133},{6,14},{7,135},{8,16},... | collective-permute-start | bytes 1179656 | tf_op jit(solution)/shard_map/ppermute | solution.py:28
  64.5 0.3 collective-permute-start.20
  64.8 1.2 %shard_map.53 = f32[192,1024]{1,0:T(8,128)S(1)} custom-call(f32[4,768]{1,0:T(4,128)S(1)} %broadcast_in_dim.11.par_ref, s32[1536,128]{1,0:T(8,128)S(1)} %broadcast_in_dim.22.row_ref, s32[1,1536]{1,0:T(1,128)S(1)} %broadcast_in_dim.23.col_ref, bf16[192,1024]{1,0:T(8,128)(2,1)S(1)} %copy-done, bf16[192,1024]{1,0:T(8,128)(2,1)S(1)} %collective-permute-done.11.refs_1_.refs_2_, ...), custom_call_target="tpu_custom_call" | custom-call | flops 603979776 | bytes 1572864 | tf_op jit(solution)/shard_map/pallas_call | solution.py:102
  66.2 6.4 %collective-permute-done.21 = bf16[192,1024]{1,0:T(8,128)(2,1)S(1)} collective-permute-done((bf16[192,1024]{1,0:T(8,128)(2,1)S(1)}, bf16[192,1024]{1,0:T(8,128)(2,1)S(1)}, u32[]{:S(2)}, u32[]{:S(2)}) %collective-permute-start.21) | collective-permute-done | bytes 393248 | tf_op jit(solution)/shard_map/ppermute | solution.py:28
  72.6 5.2 %collective-permute-done.20 = bf16[192,1024]{1,0:T(8,128)(2,1)S(1)} collective-permute-done((bf16[192,1024]{1,0:T(8,128)(2,1)S(1)}, bf16[192,1024]{1,0:T(8,128)(2,1)S(1)}, u32[]{:S(2)}, u32[]{:S(2)}) %collective-permute-start.20) | collective-permute-done | bytes 393248 | tf_op jit(solution)/shard_map/ppermute | solution.py:28
  77.9 1.1 %add_bitcast_fusion = f32[1,192,1024]{2,1,0:T(8,128)} fusion(bf16[192,1024]{1,0:T(8,128)(2,1)S(1)} %collective-permute-done.21, f32[192,1024]{1,0:T(8,128)S(1)} %convert_add_fusion, bf16[192,1024]{1,0:T(8,128)(2,1)S(1)} %collective-permute-done.20), kind=kLoop, calls=%fused_computation | loop fusion | flops 786432 | bytes 2359296 | tf_op jit(solution)/shard_map/reshape | solution.py:184
  (39 shorter events, 1.7 us)
Async XLA Ops:
  0.0 5.5 %copy-start.2 = (f32[2]{0:T(128)S(1)}, f32[2]{0:T(128)}, u32[]{:S(2)}) copy-start(f32[2]{0:T(128)} %param.6) | copy-start | bytes 28
  0.0 5.5 %copy-start.1 = (f32[2]{0:T(128)S(1)}, f32[2]{0:T(128)}, u32[]{:S(2)}) copy-start(f32[2]{0:T(128)} %param.7) | copy-start | bytes 28
  5.5 28.5 %copy-start = (bf16[192,1024]{1,0:T(8,128)(2,1)S(1)}, bf16[192,1024]{1,0:T(8,128)(2,1)}, u32[]{:S(2)}) copy-start(bf16[192,1024]{1,0:T(8,128)(2,1)} %pool.1.refs_0_) | copy-start | bytes 1179652
  6.0 11.4 %collective-permute-start.1 = (bf16[192,1024]{1,0:T(8,128)(2,1)}, bf16[192,1024]{1,0:T(8,128)(2,1)S(1)}, u32[]{:S(2)}, u32[]{:S(2)}) collective-permute-start(bf16[192,1024]{1,0:T(8,128)(2,1)} %pool.1.refs_0_), channel_id=1, source_target_pairs={{0,4},{1,65},{2,6},{3,67},{4,8},{5,69},{6,10},{7,71},{8,12},{9,73}... | collective-permute-start | bytes 1179656 | tf_op jit(solution)/shard_map/ppermute | solution.py:28
  7.9 14.1 %collective-permute-start = (bf16[192,1024]{1,0:T(8,128)(2,1)}, bf16[192,1024]{1,0:T(8,128)(2,1)S(1)}, u32[]{:S(2)}, u32[]{:S(2)}) collective-permute-start(bf16[192,1024]{1,0:T(8,128)(2,1)} %pool.1.refs_0_), channel_id=1, source_target_pairs={{0,8},{1,33},{2,10},{3,35},{4,12},{5,37},{6,14},{7,39},{8,16},{9,4... | collective-permute-start | bytes 1179656 | tf_op jit(solution)/shard_map/ppermute | solution.py:28
  11.5 12.8 %collective-permute-start.3 = (bf16[192,1024]{1,0:T(8,128)(2,1)}, bf16[192,1024]{1,0:T(8,128)(2,1)S(1)}, u32[]{:S(2)}, u32[]{:S(2)}) collective-permute-start(bf16[192,1024]{1,0:T(8,128)(2,1)} %pool.1.refs_0_), channel_id=1, source_target_pairs={{0,24},{1,129},{2,26},{3,131},{4,28},{5,133},{6,30},{7,135},{8,0},... | collective-permute-start | bytes 1179656 | tf_op jit(solution)/shard_map/ppermute | solution.py:28
  11.5 12.9 %collective-permute-start.7 = (bf16[192,1024]{1,0:T(8,128)(2,1)}, bf16[192,1024]{1,0:T(8,128)(2,1)S(1)}, u32[]{:S(2)}, u32[]{:S(2)}) collective-permute-start(bf16[192,1024]{1,0:T(8,128)(2,1)} %pool.1.refs_0_), channel_id=1, source_target_pairs={{0,1},{1,0},{2,3},{3,2},{4,5},{5,4},{6,7},{7,6},{8,9},{9,8},{10,11... | collective-permute-start | bytes 1179656 | tf_op jit(solution)/shard_map/ppermute | solution.py:32
  11.5 16.9 %collective-permute-start.6 = (bf16[192,1024]{1,0:T(8,128)(2,1)}, bf16[192,1024]{1,0:T(8,128)(2,1)S(1)}, u32[]{:S(2)}, u32[]{:S(2)}) collective-permute-start(bf16[192,1024]{1,0:T(8,128)(2,1)} %pool.1.refs_0_), channel_id=1, source_target_pairs={{0,28},{1,193},{2,30},{3,195},{4,0},{5,197},{6,2},{7,199},{8,4},{9... | collective-permute-start | bytes 1179656 | tf_op jit(solution)/shard_map/ppermute | solution.py:28
  17.4 13.1 %collective-permute-start.10 = (bf16[192,1024]{1,0:T(8,128)(2,1)S(1)}, bf16[192,1024]{1,0:T(8,128)(2,1)}, u32[]{:S(2)}, u32[]{:S(2)}) collective-permute-start(bf16[192,1024]{1,0:T(8,128)(2,1)S(1)} %collective-permute-done.1.refs_1_.refs_0_), channel_id=1, source_target_pairs={{0,1},{1,0},{2,3},{3,2},{4,5},{5,4},{6,7},{7,6},{8,9},{9,8},{10,11... | collective-permute-start | bytes 1179656 | tf_op jit(solution)/shard_map/ppermute | solution.py:32
  22.0 8.6 %collective-permute-start.8 = (bf16[192,1024]{1,0:T(8,128)(2,1)S(1)}, bf16[192,1024]{1,0:T(8,128)(2,1)}, u32[]{:S(2)}, u32[]{:S(2)}) collective-permute-start(bf16[192,1024]{1,0:T(8,128)(2,1)S(1)} %collective-permute-done.refs_0_), channel_id=1, source_target_pairs={{0,1},{1,0},{2,3},{3,2},{4,5},{5,4},{6,7},{7,6},{8,9},{9,8},{10,11... | collective-permute-start | bytes 1179656 | tf_op jit(solution)/shard_map/ppermute | solution.py:32
  24.3 6.6 %collective-permute-start.9 = (bf16[192,1024]{1,0:T(8,128)(2,1)S(1)}, bf16[192,1024]{1,0:T(8,128)(2,1)}, u32[]{:S(2)}, u32[]{:S(2)}) collective-permute-start(bf16[192,1024]{1,0:T(8,128)(2,1)S(1)} %collective-permute-done.3.refs_1_), channel_id=1, source_target_pairs={{0,1},{1,0},{2,3},{3,2},{4,5},{5,4},{6,7},{7,6},{8,9},{9,8},{10,11... | collective-permute-start | bytes 1179656 | tf_op jit(solution)/shard_map/ppermute | solution.py:32
  24.4 13.5 %collective-permute-start.5 = (bf16[192,1024]{1,0:T(8,128)(2,1)S(1)}, bf16[192,1024]{1,0:T(8,128)(2,1)S(1)}, u32[]{:S(2)}, u32[]{:S(2)}) collective-permute-start(bf16[192,1024]{1,0:T(8,128)(2,1)S(1)} %broadcast_select_fusion), channel_id=1, source_target_pairs={{0,8},{1,193},{2,10},{3,195},{4,28},{5,197},{6,30},{7,199},{8,16},... | collective-permute-start | bytes 1179656 | tf_op jit(solution)/shard_map/ppermute | solution.py:28
  28.4 9.5 %collective-permute-start.2 = (bf16[192,1024]{1,0:T(8,128)(2,1)S(1)}, bf16[192,1024]{1,0:T(8,128)(2,1)S(1)}, u32[]{:S(2)}, u32[]{:S(2)}) collective-permute-start(bf16[192,1024]{1,0:T(8,128)(2,1)S(1)} %collective-permute-done.refs_0_), channel_id=1, source_target_pairs={{0,4},{1,65},{2,6},{3,67},{4,8},{5,69},{6,10},{7,71},{8,12},{9,73}... | collective-permute-start | bytes 1179656 | tf_op jit(solution)/shard_map/ppermute | solution.py:28
  30.6 7.8 %collective-permute-start.4 = (bf16[192,1024]{1,0:T(8,128)(2,1)S(1)}, bf16[192,1024]{1,0:T(8,128)(2,1)S(1)}, u32[]{:S(2)}, u32[]{:S(2)}) collective-permute-start(bf16[192,1024]{1,0:T(8,128)(2,1)S(1)} %collective-permute-done.3.refs_1_), channel_id=1, source_target_pairs={{0,28},{1,33},{2,30},{3,35},{4,0},{5,37},{6,2},{7,39},{8,4},{9,41}... | collective-permute-start | bytes 1179656 | tf_op jit(solution)/shard_map/ppermute | solution.py:28
  30.6 12.3 %collective-permute-start.11 = (bf16[192,1024]{1,0:T(8,128)(2,1)S(1)}, bf16[192,1024]{1,0:T(8,128)(2,1)S(1)}, u32[]{:S(2)}, u32[]{:S(2)}) collective-permute-start(bf16[192,1024]{1,0:T(8,128)(2,1)S(1)} %collective-permute-done.6.refs_2_.refs_1_), channel_id=1, source_target_pairs={{0,1},{1,0},{2,3},{3,2},{4,5},{5,4},{6,7},{7,6},{8,9},{9,8},{10,11... | collective-permute-start | bytes 1179656 | tf_op jit(solution)/shard_map/ppermute | solution.py:32
  38.4 4.5 %collective-permute-start.12 = (bf16[192,1024]{1,0:T(8,128)(2,1)S(1)}, bf16[192,1024]{1,0:T(8,128)(2,1)S(1)}, u32[]{:S(2)}, u32[]{:S(2)}) collective-permute-start(bf16[192,1024]{1,0:T(8,128)(2,1)S(1)} %collective-permute-done.2.refs_1_.refs_0_), channel_id=1, source_target_pairs={{0,1},{1,0},{2,3},{3,2},{4,5},{5,4},{6,7},{7,6},{8,9},{9,8},{10,11... | collective-permute-start | bytes 1179656 | tf_op jit(solution)/shard_map/ppermute | solution.py:32
  38.5 4.4 %collective-permute-start.13 = (bf16[192,1024]{1,0:T(8,128)(2,1)S(1)}, bf16[192,1024]{1,0:T(8,128)(2,1)S(1)}, u32[]{:S(2)}, u32[]{:S(2)}) collective-permute-start(bf16[192,1024]{1,0:T(8,128)(2,1)S(1)} %collective-permute-done.4.refs_2_.refs_1_), channel_id=1, source_target_pairs={{0,1},{1,0},{2,3},{3,2},{4,5},{5,4},{6,7},{7,6},{8,9},{9,8},{10,11... | collective-permute-start | bytes 1179656 | tf_op jit(solution)/shard_map/ppermute | solution.py:32
  38.9 4.0 %collective-permute-start.14 = (bf16[192,1024]{1,0:T(8,128)(2,1)S(1)}, bf16[192,1024]{1,0:T(8,128)(2,1)S(1)}, u32[]{:S(2)}, u32[]{:S(2)}) collective-permute-start(bf16[192,1024]{1,0:T(8,128)(2,1)S(1)} %collective-permute-done.5.refs_0_), channel_id=1, source_target_pairs={{0,1},{1,0},{2,3},{3,2},{4,5},{5,4},{6,7},{7,6},{8,9},{9,8},{10,11... | collective-permute-start | bytes 1179656 | tf_op jit(solution)/shard_map/ppermute | solution.py:32
  46.0 11.4 %collective-permute-start.16 = (bf16[192,1024]{1,0:T(8,128)(2,1)S(1)}, bf16[192,1024]{1,0:T(8,128)(2,1)S(1)}, u32[]{:S(2)}, u32[]{:S(2)}) collective-permute-start(bf16[192,1024]{1,0:T(8,128)(2,1)S(1)} %get-tuple-element.71), channel_id=1, source_target_pairs={{0,28},{1,193},{2,30},{3,195},{4,0},{5,197},{6,2},{7,199},{8,4},{9... | collective-permute-start | bytes 1179656 | tf_op jit(solution)/shard_map/ppermute | solution.py:28
  47.1 14.3 %collective-permute-start.15 = (bf16[192,1024]{1,0:T(8,128)(2,1)S(1)}, bf16[192,1024]{1,0:T(8,128)(2,1)S(1)}, u32[]{:S(2)}, u32[]{:S(2)}) collective-permute-start(bf16[192,1024]{1,0:T(8,128)(2,1)S(1)} %shard_map.49), channel_id=1, source_target_pairs={{0,24},{1,65},{2,26},{3,67},{4,12},{5,69},{6,14},{7,71},{8,0},{9,7... | collective-permute-start | bytes 1179656 | tf_op jit(solution)/shard_map/ppermute | solution.py:28
  50.8 10.9 %collective-permute-start.17 = (bf16[192,1024]{1,0:T(8,128)(2,1)S(1)}, bf16[192,1024]{1,0:T(8,128)(2,1)S(1)}, u32[]{:S(2)}, u32[]{:S(2)}) collective-permute-start(bf16[192,1024]{1,0:T(8,128)(2,1)S(1)} %get-tuple-element.73), channel_id=1, source_target_pairs={{0,4},{1,33},{2,6},{3,35},{4,8},{5,37},{6,10},{7,39},{8,12},{9,41}... | collective-permute-start | bytes 1179656 | tf_op jit(solution)/shard_map/ppermute | solution.py:28
  53.4 12.6 %collective-permute-start.18 = (bf16[192,1024]{1,0:T(8,128)(2,1)S(1)}, bf16[192,1024]{1,0:T(8,128)(2,1)S(1)}, u32[]{:S(2)}, u32[]{:S(2)}) collective-permute-start(bf16[192,1024]{1,0:T(8,128)(2,1)S(1)} %get-tuple-element.76), channel_id=1, source_target_pairs={{0,28},{1,193},{2,30},{3,195},{4,0},{5,197},{6,2},{7,199},{8,4},{9... | collective-permute-start | bytes 1179656 | tf_op jit(solution)/shard_map/ppermute | solution.py:28
  54.7 11.3 %collective-permute-start.19 = (bf16[192,1024]{1,0:T(8,128)(2,1)S(1)}, bf16[192,1024]{1,0:T(8,128)(2,1)S(1)}, u32[]{:S(2)}, u32[]{:S(2)}) collective-permute-start(bf16[192,1024]{1,0:T(8,128)(2,1)S(1)} %get-tuple-element.77), channel_id=1, source_target_pairs={{0,4},{1,65},{2,6},{3,67},{4,8},{5,69},{6,10},{7,71},{8,12},{9,73}... | collective-permute-start | bytes 1179656 | tf_op jit(solution)/shard_map/ppermute | solution.py:28
  61.8 10.8 %collective-permute-start.21 = (bf16[192,1024]{1,0:T(8,128)(2,1)S(1)}, bf16[192,1024]{1,0:T(8,128)(2,1)S(1)}, u32[]{:S(2)}, u32[]{:S(2)}) collective-permute-start(bf16[192,1024]{1,0:T(8,128)(2,1)S(1)} %add_convert_fusion), channel_id=1, source_target_pairs={{0,8},{1,129},{2,10},{3,131},{4,12},{5,133},{6,14},{7,135},{8,16},... | collective-permute-start | bytes 1179656 | tf_op jit(solution)/shard_map/ppermute | solution.py:28
  64.5 13.4 %collective-permute-start.20 = (bf16[192,1024]{1,0:T(8,128)(2,1)S(1)}, bf16[192,1024]{1,0:T(8,128)(2,1)S(1)}, u32[]{:S(2)}, u32[]{:S(2)}) collective-permute-start(bf16[192,1024]{1,0:T(8,128)(2,1)S(1)} %add_convert_fusion.1), channel_id=1, source_target_pairs={{0,24},{1,33},{2,26},{3,35},{4,28},{5,37},{6,30},{7,39},{8,0},{9,4... | collective-permute-start | bytes 1179656 | tf_op jit(solution)/shard_map/ppermute | solution.py:28
